TPU v7x, 256 devices: a whole 4x4x8 slice. The times are simulated.
256 devices in a mesh: batch: 32 (over y, x, core), seq: 8 (over z).
Axes of the slice: x: 4, y: 4, z: 8, core: 2. Of those that a mesh axis runs over, the one named last changes fastest.
Arguments:
- query_rows: bfloat16 [32, 2560, 3072], P('batch', 'seq'), may hold values from -16 to 16
- key_rows: bfloat16 [32, 2560, 3072], P('batch', 'seq'), may hold values from -16 to 16
- value_rows: bfloat16 [32, 2560, 3072], P('batch', 'seq'), may hold values from -10 to 10
- cached_rows: bfloat16 [32, 2560, 3072], P('batch', 'seq'), may hold values from -4 to 4
- plan: int32 [32, 28], replicated, may hold values from 0 to 1, as said below
- timestep: int32 [32], replicated, may hold values from 0 to 27
- assignment: int32 [32], replicated, may hold values from 0 to 31, as said below
Outputs:
- refreshed: bfloat16 [32, 2560, 3072], P('batch', 'seq')
Inputs may be any that keep to these rules, and one draw needn't show every extreme that they name: plan[r, t] is 1 for t = 0 and for the timesteps at which request r refreshes, every 3 timesteps from its own offset, else 0. `assignment`: a permutation of the requests; of the two slots g and g + 16, exactly one holds a request with active = 1.
All inputs are finite; a program needn't handle non-finite values.
Results may differ from a plain program's by a relative error of at most 0.0025.
Values may be sent and summed in bfloat16 or wider, within the bound.
No kernel may reach another device: no remote copies, remote signals or barrier semaphores. Data moves between devices by JAX's collectives and lax.ppermute only.
A program may use at most 128 MiB of HBM per device.

v0:
```python
import math

import jax
import jax.numpy as jnp
from jax import lax
from jax.sharding import PartitionSpec as P

HEAD_DIM = 128


def partner(value, axis, stride):
    mask = 2**stride
    pairs = [(source, source ^ mask) for source in range(lax.axis_size(axis))]
    return lax.ppermute(value, axis, pairs)


def block_rows(row_count):
    for candidate in range(512, row_count + 1):
        if row_count % candidate == 0:
            return candidate
    return row_count


def attend(head_queries, head_keys, head_values):
    row_count, head_count, depth = head_queries.shape
    block = block_rows(row_count)
    factor = 1.0 / math.sqrt(depth)
    stacked = head_queries.reshape(row_count // block, block, head_count, depth)

    def one_block(query_block):
        scores = (
            jnp.einsum("qnd,knd->nqk", query_block, head_keys, preferred_element_type=jnp.float32)
            * factor
        )
        peak = jnp.max(scores, axis=2, keepdims=True)
        shifted = jnp.exp(scores - peak)
        total = jnp.sum(shifted, axis=2)
        weights = shifted.astype(jnp.bfloat16)
        mixed = jnp.einsum("nqk,knd->qnd", weights, head_values, preferred_element_type=jnp.float32)
        return (mixed / jnp.transpose(total)[:, :, None]).astype(jnp.bfloat16)

    return lax.map(one_block, stacked).reshape(row_count, head_count, depth)


def body(query_rows, key_rows, value_rows, cached_rows, plan, timestep, assignment):
    pieces = lax.axis_size("seq")
    local_rows = query_rows.shape[1]
    width = query_rows.shape[2]
    group = lax.axis_index("batch")
    slot_index = jnp.arange(assignment.shape[0], dtype=jnp.int32)
    request = jnp.sum(jnp.where(slot_index == group, assignment, 0))
    moment = jnp.sum(jnp.where(slot_index == request, timestep, 0))
    step_index = jnp.arange(plan.shape[1], dtype=jnp.int32)
    chosen = (slot_index[:, None] == request) & (step_index[None, :] == moment)
    active = jnp.sum(jnp.where(chosen, plan, 0)) > 0

    def arrange(rows):
        return rows[0].reshape(local_rows, pieces, width // (pieces * HEAD_DIM), HEAD_DIM)

    head_queries = lax.all_to_all(
        arrange(query_rows), "seq", split_axis=1, concat_axis=0, tiled=True
    )[:, 0]
    head_keys = lax.all_to_all(arrange(key_rows), "seq", split_axis=1, concat_axis=0, tiled=True)[
        :, 0
    ]
    head_values = lax.all_to_all(
        arrange(value_rows), "seq", split_axis=1, concat_axis=0, tiled=True
    )[:, 0]
    halfway = head_queries.shape[0] // 2
    top_bit = lax.axis_size("batch").bit_length() - 2
    far_keys, far_values, far_queries = partner(
        (head_keys, head_values, head_queries[halfway:]), "batch", top_bit
    )
    use_keys = jnp.where(active, head_keys, far_keys)
    use_values = jnp.where(active, head_values, far_values)
    use_queries = jnp.where(active, head_queries[:halfway], far_queries)
    part_out = attend(use_queries, use_keys, use_values)
    returned = partner(part_out, "batch", top_bit)
    attended = jnp.concatenate([part_out, returned], axis=0)
    moved = lax.all_to_all(attended[:, None], "seq", split_axis=0, concat_axis=1, tiled=True)
    fresh = moved.reshape(1, local_rows, width)
    return jnp.where(active, fresh, cached_rows)


def solution(mesh):
    placed = (
        P("batch", "seq", None),
        P("batch", "seq", None),
        P("batch", "seq", None),
        P("batch", "seq", None),
        P(),
        P(),
        P(),
    )
    return jax.shard_map(
        body, mesh=mesh, in_specs=placed, out_specs=P("batch", "seq", None), check_vma=False
    )
```

profile of v0, /device:TPU:34, one launch (start us, length us, event | category | flops | bytes accessed | tf_op | source)
XLA Modules:
  0.0 395.8 jit_solution(1711716590007203280)
XLA Ops:
  0.0 2.9 copy.38
  2.9 2.4 copy.39
  5.4 8.6 %all-to-all-start.2 = ((bf16[320,8,3,128]{3,0,2,1:T(8,128)(2,1)}), bf16[320,8,3,128]{3,0,2,1:T(8,128)(2,1)}, u32[]{:S(2)}, u32[]{:S(2)}) async-start(bf16[320,8,3,128]{3,0,2,1:T(8,128)(2,1)} %copy.39), calls=%async_computation.2 | async-start | bytes 3932160 | tf_op jit(solution)/shard_map/all_to_all | solution.py:66
  13.9 2.9 copy.32
  16.8 2.4 copy.33
  19.2 41.7 %all-to-all-done.2 = bf16[320,8,3,128]{3,0,2,1:T(8,128)(2,1)} async-done(((bf16[320,8,3,128]{3,0,2,1:T(8,128)(2,1)}), bf16[320,8,3,128]{3,0,2,1:T(8,128)(2,1)}, u32[]{:S(2)}, u32[]{:S(2)}) %all-to-all-start.2) | async-done | bytes 1966112 | tf_op jit(solution)/shard_map/all_to_all | solution.py:66
  61.0 5.7 %all-to-all-start = ((bf16[320,8,3,128]{3,0,2,1:T(8,128)(2,1)}), bf16[320,8,3,128]{3,0,2,1:T(8,128)(2,1)}, u32[]{:S(2)}, u32[]{:S(2)}) async-start(bf16[320,8,3,128]{3,0,2,1:T(8,128)(2,1)} %copy.33), calls=%async_computation | async-start | bytes 3932160 | tf_op jit(solution)/shard_map/all_to_all | solution.py:60
  66.6 2.9 copy.35
  69.6 2.5 copy.36
  72.0 39.2 %all-to-all-done = bf16[320,8,3,128]{3,0,2,1:T(8,128)(2,1)} async-done(((bf16[320,8,3,128]{3,0,2,1:T(8,128)(2,1)}), bf16[320,8,3,128]{3,0,2,1:T(8,128)(2,1)}, u32[]{:S(2)}, u32[]{:S(2)}) %all-to-all-start) | async-done | bytes 1966112 | tf_op jit(solution)/shard_map/all_to_all | solution.py:60
  111.2 5.7 %all-to-all-start.1 = ((bf16[320,8,3,128]{3,0,2,1:T(8,128)(2,1)}), bf16[320,8,3,128]{3,0,2,1:T(8,128)(2,1)}, u32[]{:S(2)}, u32[]{:S(2)}) async-start(bf16[320,8,3,128]{3,0,2,1:T(8,128)(2,1)} %copy.36), calls=%async_computation.1 | async-start | bytes 3932160 | tf_op jit(solution)/shard_map/all_to_all | solution.py:63
  117.0 1.7 copy.40
  118.6 3.3 collective-permute-start.2
  121.9 1.7 copy.52
  123.6 1.4 fusion.21
  125.0 0.3 collective-permute-start
  125.3 0.0 copy-start.3
  125.3 0.0 copy-start.4
  125.3 0.0 copy-start.2
  125.3 36.3 %all-to-all-done.1 = bf16[320,8,3,128]{3,0,2,1:T(8,128)(2,1)} async-done(((bf16[320,8,3,128]{3,0,2,1:T(8,128)(2,1)}), bf16[320,8,3,128]{3,0,2,1:T(8,128)(2,1)}, u32[]{:S(2)}, u32[]{:S(2)}) %all-to-all-start.1) | async-done | bytes 1966112 | tf_op jit(solution)/shard_map/all_to_all | solution.py:63
  161.6 3.0 copy.37
  164.5 3.2 collective-permute-start.1
  167.7 0.0 copy-done.3
  167.7 0.7 fusion.20
  168.4 0.7 iota_compare_fusion.1
  169.1 0.0 copy-done.4
  169.1 1.4 select_reduce_fusion.1
  170.5 0.6 iota_compare_fusion
  171.1 0.0 copy-done.2
  171.1 0.8 select_reduce_fusion
  172.6 14.4 %collective-permute-done = bf16[1280,3,128]{2,0,1:T(8,128)(2,1)S(1)} collective-permute-done((bf16[1280,3,128]{2,0,1:T(8,128)(2,1)}, bf16[1280,3,128]{2,0,1:T(8,128)(2,1)S(1)}, u32[]{:S(2)}, u32[]{:S(2)}) %collective-permute-start) | collective-permute-done | bytes 983072 | tf_op jit(solution)/shard_map/ppermute | solution.py:14
  187.1 0.0 copy-start.1
  187.1 0.9 copy-done.1
  188.0 1.3 broadcast_select_fusion.2
  189.3 0.0 collective-permute-done.2
  189.3 1.6 broadcast_select_fusion
  191.0 34.1 %collective-permute-done.1 = bf16[2560,3,128]{2,0,1:T(8,128)(2,1)} collective-permute-done((bf16[2560,3,128]{2,0,1:T(8,128)(2,1)}, bf16[2560,3,128]{2,0,1:T(8,128)(2,1)}, u32[]{:S(2)}, u32[]{:S(2)}) %collective-permute-start.1) | collective-permute-done | bytes 1966112 | tf_op jit(solution)/shard_map/ppermute | solution.py:14
  225.1 1.8 broadcast_select_fusion.1
  226.8 55.7 %while.10 = (s32[]{:T(128)}, bf16[2,640,3,128]{3,1,0,2:T(8,128)(2,1)}, bf16[2,640,3,128]{3,1,0,2:T(8,128)(2,1)S(1)}, bf16[2560,3,128]{2,0,1:T(8,128)(2,1)S(1)}, bf16[2560,3,128]{2,0,1:T(8,128)(2,1)}, /*index=5*/s32[]{:T(128)}) while((s32[]{:T(128)}, bf16[2,640,3,128]{3,1,0,2:T(8,128)(2,1)}, bf16[2,640,3,128]{3,1,0,2:T(8,128)(2,1)S(1)}, ...), condition=%wide.region_6.7_spmd, body=%wide.region_3.6_spmd.sunk | while | flops 2556391680 | bytes 63936584 | solution.py:42
  226.9 8.2 %multiply_reduce_fusion.2 = (f32[3,640]{1,0:T(4,128)S(1)}, f32[3,640,2560]{2,1,0:T(8,128)}) fusion(bf16[2560,3,128]{2,0,1:T(8,128)(2,1)S(1)} %get-tuple-element.112, bf16[2,640,3,128]{3,1,0,2:T(8,128)(2,1)S(1)} %get-tuple-element.111, s32[]{:T(128)} %get-tuple-element.103), kind=kOutput, calls=%fused_computation.1.clone.1 | convolution fusion | flops 1268119680 | bytes 22126084 | tf_op jit(solution)/shard_map/while/body/eval_jaxpr/qnd,knd->nqk/dot_general | solution.py:32
  235.1 9.9 %fusion.32 = f32[3,640]{1,0:T(4,128)S(1)} fusion(f32[3,640,2560]{2,1,0:T(8,128)} %get-tuple-element.95, f32[3,640]{1,0:T(4,128)S(1)} %get-tuple-element.96), kind=kLoop, calls=%fused_computation.2.clone.1 | loop fusion | flops 14743680 | bytes 19676160 | tf_op jit(solution)/shard_map/while/body/eval_jaxpr/reduce_sum | solution.py:37
  245.0 9.7 %fusion.33 = bf16[2,640,3,128]{3,1,0,2:T(8,128)(2,1)} fusion(bf16[2,640,3,128]{3,1,0,2:T(8,128)(2,1)} %get-tuple-element.104, s32[]{:T(128)} %get-tuple-element.103, bf16[2560,3,128]{2,0,1:T(8,128)(2,1)} %get-tuple-element.113, f32[3,640,2560]{2,1,0:T(8,128)} %get-tuple-element.95, f32[3,640]{1,0:T(4,128)S(1)} %get-tuple-element.96, ...), kind=kOutput, calls=%fused_computation.8.clone.1 | convolution fusion | flops 1273528320 | bytes 22134272 | tf_op jit(solution)/shard_map/while/body/eval_jaxpr/nqk,knd->qnd/dot_general | solution.py:39
  254.7 8.2 %multiply_reduce_fusion.2 = (f32[3,640]{1,0:T(4,128)S(1)}, f32[3,640,2560]{2,1,0:T(8,128)}) fusion(bf16[2560,3,128]{2,0,1:T(8,128)(2,1)S(1)} %get-tuple-element.112, bf16[2,640,3,128]{3,1,0,2:T(8,128)(2,1)S(1)} %get-tuple-element.111, s32[]{:T(128)} %get-tuple-element.103), kind=kOutput, calls=%fused_computation.1.clone.1 | convolution fusion | flops 1268119680 | bytes 22126084 | tf_op jit(solution)/shard_map/while/body/eval_jaxpr/qnd,knd->nqk/dot_general | solution.py:32
  263.0 9.9 %fusion.32 = f32[3,640]{1,0:T(4,128)S(1)} fusion(f32[3,640,2560]{2,1,0:T(8,128)} %get-tuple-element.95, f32[3,640]{1,0:T(4,128)S(1)} %get-tuple-element.96), kind=kLoop, calls=%fused_computation.2.clone.1 | loop fusion | flops 14743680 | bytes 19676160 | tf_op jit(solution)/shard_map/while/body/eval_jaxpr/reduce_sum | solution.py:37
  272.9 9.7 %fusion.33 = bf16[2,640,3,128]{3,1,0,2:T(8,128)(2,1)} fusion(bf16[2,640,3,128]{3,1,0,2:T(8,128)(2,1)} %get-tuple-element.104, s32[]{:T(128)} %get-tuple-element.103, bf16[2560,3,128]{2,0,1:T(8,128)(2,1)} %get-tuple-element.113, f32[3,640,2560]{2,1,0:T(8,128)} %get-tuple-element.95, f32[3,640]{1,0:T(4,128)S(1)} %get-tuple-element.96, ...), kind=kOutput, calls=%fused_computation.8.clone.1 | convolution fusion | flops 1273528320 | bytes 22134272 | tf_op jit(solution)/shard_map/while/body/eval_jaxpr/nqk,knd->qnd/dot_general | solution.py:39
  282.6 3.8 collective-permute-start.3
  286.4 18.1 %collective-permute-done.3 = bf16[1280,3,128]{2,0,1:T(8,128)(2,1)S(1)} collective-permute-done((bf16[1280,3,128]{2,0,1:T(8,128)(2,1)}, bf16[1280,3,128]{2,0,1:T(8,128)(2,1)S(1)}, u32[]{:S(2)}, u32[]{:S(2)}) %collective-permute-start.3) | collective-permute-done | bytes 983072 | tf_op jit(solution)/shard_map/ppermute | solution.py:14
  304.4 1.3 maximum_bitcast_fusion
  305.8 13.1 %copy.43 = bf16[2560,1,3,128]{3,2,1,0:T(4,128)(2,1)} copy(bf16[2560,1,3,128]{3,0,2,1:T(8,128)(2,1)S(1)} %maximum_bitcast_fusion) | data formatting | bytes 3932160 | tf_op jit(solution)/shard_map/broadcast_in_dim | solution.py:80
  318.9 7.2 %all-to-all-start.3 = ((bf16[2560,1,3,128]{3,2,1,0:T(4,128)(2,1)}), bf16[2560,1,3,128]{3,2,1,0:T(4,128)(2,1)S(1)}, u32[]{:S(2)}, u32[]{:S(2)}) async-start(bf16[2560,1,3,128]{3,2,1,0:T(4,128)(2,1)} %copy.43), calls=%async_computation.3 | async-start | bytes 5242880 | tf_op jit(solution)/shard_map/all_to_all | solution.py:80
  326.1 4.1 %copy.46 = bf16[1,320,3072]{1,2,0:T(8,128)(2,1)} copy(bf16[1,320,3072]{2,1,0:T(8,128)(2,1)} %param.12) | data formatting | bytes 3932160 | tf_op args[3]
  330.2 52.4 %all-to-all-done.3 = bf16[2560,1,3,128]{3,2,1,0:T(4,128)(2,1)S(1)} async-done(((bf16[2560,1,3,128]{3,2,1,0:T(4,128)(2,1)}), bf16[2560,1,3,128]{3,2,1,0:T(4,128)(2,1)S(1)}, u32[]{:S(2)}, u32[]{:S(2)}) %all-to-all-start.3) | async-done | bytes 1966112 | tf_op jit(solution)/shard_map/all_to_all | solution.py:80
  382.6 1.6 copy.44
  384.1 0.0 copy-start
  384.2 4.2 %copy.45 = bf16[320,8,1,3,128]{0,4,3,1,2:T(8,128)(2,1)} copy(bf16[320,8,1,3,128]{4,0,1,3,2:T(8,128)(2,1)} %bitcast.73) | data formatting | bytes 3932160 | tf_op jit(solution)/shard_map/all_to_all | solution.py:80
  388.4 0.0 copy-done
  388.4 3.4 bitcast_select_fusion
  391.7 4.1 %copy.47 = bf16[1,320,3072]{2,1,0:T(8,128)(2,1)} copy(bf16[1,320,3072]{1,2,0:T(8,128)(2,1)} %bitcast_select_fusion) | data formatting | bytes 3932160 | tf_op jit(solution)/shard_map/jit(_where)/select_n | solution.py:82
  (1 shorter events, 0.0 us)
Async XLA Ops:
  5.4 55.6 %all-to-all-start.2 = ((bf16[320,8,3,128]{3,0,2,1:T(8,128)(2,1)}), bf16[320,8,3,128]{3,0,2,1:T(8,128)(2,1)}, u32[]{:S(2)}, u32[]{:S(2)}) async-start(bf16[320,8,3,128]{3,0,2,1:T(8,128)(2,1)} %copy.39), calls=%async_computation.2 | async-start | bytes 3932160 | tf_op jit(solution)/shard_map/all_to_all | solution.py:66
  61.0 50.3 %all-to-all-start = ((bf16[320,8,3,128]{3,0,2,1:T(8,128)(2,1)}), bf16[320,8,3,128]{3,0,2,1:T(8,128)(2,1)}, u32[]{:S(2)}, u32[]{:S(2)}) async-start(bf16[320,8,3,128]{3,0,2,1:T(8,128)(2,1)} %copy.33), calls=%async_computation | async-start | bytes 3932160 | tf_op jit(solution)/shard_map/all_to_all | solution.py:60
  111.2 50.3 %all-to-all-start.1 = ((bf16[320,8,3,128]{3,0,2,1:T(8,128)(2,1)}), bf16[320,8,3,128]{3,0,2,1:T(8,128)(2,1)}, u32[]{:S(2)}, u32[]{:S(2)}) async-start(bf16[320,8,3,128]{3,0,2,1:T(8,128)(2,1)} %copy.36), calls=%async_computation.1 | async-start | bytes 3932160 | tf_op jit(solution)/shard_map/all_to_all | solution.py:63
  118.6 70.7 %collective-permute-start.2 = (bf16[2560,3,128]{2,0,1:T(8,128)(2,1)S(1)}, bf16[2560,3,128]{2,0,1:T(8,128)(2,1)}, u32[]{:S(2)}, u32[]{:S(2)}) collective-permute-start(bf16[2560,3,128]{2,0,1:T(8,128)(2,1)S(1)} %bitcast.71), channel_id=1, source_target_pairs={{0,128},{8,136},{16,144},{24,152},{32,160},{40,168},{48,176},{56,1... | collective-permute-start | bytes 5898248 | tf_op jit(solution)/shard_map/ppermute | solution.py:14
  125.0 62.1 %collective-permute-start = (bf16[1280,3,128]{2,0,1:T(8,128)(2,1)}, bf16[1280,3,128]{2,0,1:T(8,128)(2,1)S(1)}, u32[]{:S(2)}, u32[]{:S(2)}) collective-permute-start(bf16[1280,3,128]{2,0,1:T(8,128)(2,1)} %bitcast.9), channel_id=1, source_target_pairs={{0,128},{8,136},{16,144},{24,152},{32,160},{40,168},{48,176},{56,1... | collective-permute-start | bytes 2949128 | tf_op jit(solution)/shard_map/ppermute | solution.py:14
  125.3 42.4 %copy-start.3 = (s32[32]{0:T(128)S(1)}, s32[32]{0:T(128)}, u32[]{:S(2)}) copy-start(s32[32]{0:T(128)} %param.15) | copy-start | bytes 388
  125.3 43.8 %copy-start.4 = (s32[32]{0:T(128)S(1)}, s32[32]{0:T(128)}, u32[]{:S(2)}) copy-start(s32[32]{0:T(128)} %param.14) | copy-start | bytes 388
  125.3 45.8 %copy-start.2 = (s32[32,28]{1,0:T(8,128)S(1)}, s32[32,28]{1,0:T(8,128)}, u32[]{:S(2)}) copy-start(s32[32,28]{1,0:T(8,128)} %param.13) | copy-start | bytes 10756
  164.5 60.6 %collective-permute-start.1 = (bf16[2560,3,128]{2,0,1:T(8,128)(2,1)}, bf16[2560,3,128]{2,0,1:T(8,128)(2,1)}, u32[]{:S(2)}, u32[]{:S(2)}) collective-permute-start(bf16[2560,3,128]{2,0,1:T(8,128)(2,1)} %bitcast.14), channel_id=1, source_target_pairs={{0,128},{8,136},{16,144},{24,152},{32,160},{40,168},{48,176},{56,1... | collective-permute-start | bytes 5898248 | tf_op jit(solution)/shard_map/ppermute | solution.py:14
  187.1 1.0 copy-start.1
  282.6 21.9 %collective-permute-start.3 = (bf16[1280,3,128]{2,0,1:T(8,128)(2,1)}, bf16[1280,3,128]{2,0,1:T(8,128)(2,1)S(1)}, u32[]{:S(2)}, u32[]{:S(2)}) collective-permute-start(bf16[1280,3,128]{2,0,1:T(8,128)(2,1)} %bitcast.75), channel_id=1, source_target_pairs={{0,128},{8,136},{16,144},{24,152},{32,160},{40,168},{48,176},{56,1... | collective-permute-start | bytes 2949128 | tf_op jit(solution)/shard_map/ppermute | solution.py:14
  318.9 63.7 %all-to-all-start.3 = ((bf16[2560,1,3,128]{3,2,1,0:T(4,128)(2,1)}), bf16[2560,1,3,128]{3,2,1,0:T(4,128)(2,1)S(1)}, u32[]{:S(2)}, u32[]{:S(2)}) async-start(bf16[2560,1,3,128]{3,2,1,0:T(4,128)(2,1)} %copy.43), calls=%async_computation.3 | async-start | bytes 5242880 | tf_op jit(solution)/shard_map/all_to_all | solution.py:80
  384.1 4.2 %copy-start = (bf16[1,320,3072]{1,2,0:T(8,128)(2,1)S(1)}, bf16[1,320,3072]{1,2,0:T(8,128)(2,1)}, u32[]{:S(2)}) copy-start(bf16[1,320,3072]{1,2,0:T(8,128)(2,1)} %copy.46) | copy-start | bytes 5898244
where the time goes:
time: 399 us; the launch traced here: 396 us
  waiting for transfers between devices  236 us (59%)
  local copies, waits for them, and re-layouts  51.8 us (13%)
  starting transfers between devices  37.8 us (9%)
  matrix products  35.9 us (9%)
  other arithmetic  33.3 us (8%)
    ppermute x4, waiting for transfers between devices, partner(): return lax.ppermute(value, axis, pairs)  66.7 us
    all_to_all x1, waiting for transfers between devices, body(): lax.all_to_all(attended[:, None], 'seq', split_axis=0, concat_axis=1, til...  52.4 us
    all_to_all x1, waiting for transfers between devices, body(): lax.all_to_all(arrange(value_rows), 'seq', split_axis=1, concat_axis=0, t...  41.7 us
    all_to_all x1, waiting for transfers between devices, body(): lax.all_to_all(arrange(query_rows), 'seq', split_axis=1, concat_axis=0, t...  39.2 us
    all_to_all x1, waiting for transfers between devices, body(): lax.all_to_all(arrange(key_rows), 'seq', split_axis=1, concat_axis=0, til...  36.3 us
    reduce_sum x2, other arithmetic, one_block(): total = jnp.sum(shifted, axis=2)  19.8 us
    dot_general x2, matrix products, one_block(): jnp.einsum('nqk,knd->qnd', weights, head_values, preferred_element_type=j...  19.4 us
    dot_general x2, matrix products, one_block(): jnp.einsum('qnd,knd->nqk', query_block, head_keys, preferred_element_type...  16.5 us
  transfers between devices with their start and end apart: 8, of which 7 were waited for; matrix products, arithmetic and copies ran while one was open for 7% of the time, Pallas kernels for 0%

commit v1 on v0

v1 whole, which is shorter than its diff:
```python
import functools
import math

import jax
import jax.numpy as jnp
from jax import lax
from jax.experimental import pallas as pl
from jax.experimental.pallas import tpu as pltpu
from jax.sharding import PartitionSpec as P

HEAD_DIM = 128
GROUPS = 3
VMEM_LIMIT = 48 << 20

ANY = pl.BlockSpec(memory_space=pl.ANY)
SMEM = pl.BlockSpec(memory_space=pltpu.SMEM)


def params():
    return pltpu.CompilerParams(vmem_limit_bytes=VMEM_LIMIT)


def ring(pieces):
    order = [0]
    for step in range(1, pieces // 2):
        order += [step, pieces - step]
    if pieces > 1:
        order.append(pieces // 2)
    return order


def head_columns(me, offset, group, pieces):
    head = group * pieces + lax.rem(me + offset, pieces)
    return pl.ds(pl.multiple_of(head * HEAD_DIM, HEAD_DIM), HEAD_DIM)


def run_copies(copies):
    for copy in copies:
        copy.start()
    for copy in copies:
        copy.wait()


def pack_kernel(pieces, group, *refs):
    sources, outs, sems = refs[:3], refs[3 : 3 + pieces], refs[3 + pieces]
    me = lax.axis_index("seq")
    run_copies(
        [
            pltpu.make_async_copy(
                sources[part].at[0, :, head_columns(me, offset, group, pieces)],
                outs[offset].at[part],
                sems.at[offset, part],
            )
            for offset in range(pieces)
            for part in range(3)
        ]
    )


def pack_far_kernel(pieces, group, assignment, timestep, plan, *refs):
    sources, out, flag, sems = refs[:3], refs[3], refs[4], refs[5]
    me = lax.axis_index("seq")
    slot = lax.axis_index("batch")
    request = assignment[slot]
    flag[0] = plan[request, timestep[request]]
    run_copies(
        [
            pltpu.make_async_copy(
                sources[part].at[0, :, head_columns(me, offset, group, pieces)],
                out.at[offset, part],
                sems.at[offset, part],
            )
            for offset in range(pieces)
            for part in range(3)
        ]
    )


def pack_second_kernel(pieces, group, flag, *refs):
    sources, far = refs[:3], refs[3]
    pairs, queries = refs[4 : 4 + pieces], refs[4 + pieces : 4 + 2 * pieces]
    sems = refs[4 + 2 * pieces]
    me = lax.axis_index("seq")

    def target(offset, part):
        return queries[offset] if part == 0 else pairs[offset].at[part - 1]

    @pl.when(flag[0] > 0)
    def _():
        run_copies(
            [
                pltpu.make_async_copy(
                    sources[part].at[0, :, head_columns(me, offset, group, pieces)],
                    target(offset, part),
                    sems.at[offset, part],
                )
                for offset in range(pieces)
                for part in range(3)
            ]
        )

    @pl.when(flag[0] <= 0)
    def _():
        run_copies(
            [
                pltpu.make_async_copy(far.at[offset, part], target(offset, part), sems.at[offset, part])
                for offset in range(pieces)
                for part in range(3)
            ]
        )


def attend_block(query, keys, values):
    factor = math.log2(math.e) / math.sqrt(HEAD_DIM)
    scores = lax.dot_general(
        query, keys[...], (((1,), (1,)), ((), ())), preferred_element_type=jnp.float32
    )
    peak = jnp.max(scores, axis=1, keepdims=True)
    shifted = jnp.exp2((scores - peak) * factor)
    total = jnp.sum(shifted, axis=1, keepdims=True)
    mixed = jnp.dot(
        shifted.astype(jnp.bfloat16), values[...], preferred_element_type=jnp.float32
    )
    return (mixed / total).astype(jnp.bfloat16)


def first_kernel(pieces, rows, *refs):
    ins, outs = refs[:pieces], refs[pieces : 2 * pieces]
    queries, keys, values, results, sems, out_sems = refs[2 * pieces :]
    fetch = [
        pltpu.make_async_copy(
            ins[i].at[part], (queries, keys, values)[part].at[pl.ds(i * rows, rows)], sems.at[part, i]
        )
        for part in (1, 2, 0)
        for i in range(pieces)
    ]
    run_copies(fetch)

    @pl.loop(0, pieces)
    def _(i):
        here = pl.ds(pl.multiple_of(i * rows, rows), rows)
        results[here] = attend_block(queries[here], keys, values)

    run_copies(
        [
            pltpu.make_async_copy(results.at[pl.ds(i * rows, rows)], outs[i], out_sems.at[i])
            for i in range(pieces)
        ]
    )


def second_kernel(pieces, rows, count, flag, *refs):
    pairs, refs = refs[:pieces], refs[pieces:]
    queries_in, refs = refs[:count], refs[count:]
    earlier, refs = refs[:count], refs[count:]
    outs_a, outs_b = refs[:count], refs[count : 2 * count]
    queries, keys, values, results, sems, query_sems, a_sems, b_sems = refs[2 * count :]
    fetch = [
        pltpu.make_async_copy(
            pairs[i].at[part], (keys, values)[part].at[pl.ds(i * rows, rows)], sems.at[part, i]
        )
        for part in (0, 1)
        for i in range(pieces)
    ] + [
        pltpu.make_async_copy(queries_in[i], queries.at[pl.ds(i * rows, rows)], query_sems.at[i])
        for i in range(count)
    ]
    run_copies(fetch)

    @pl.loop(0, count)
    def _(i):
        here = pl.ds(pl.multiple_of(i * rows, rows), rows)
        results[here] = attend_block(queries[here], keys, values)

    @pl.when(flag[0] > 0)
    def _():
        run_copies([pltpu.make_async_copy(earlier[i], outs_a[i], a_sems.at[i]) for i in range(count)])

    @pl.when(flag[0] <= 0)
    def _():
        run_copies(
            [
                pltpu.make_async_copy(results.at[pl.ds(i * rows, rows)], outs_a[i], a_sems.at[i])
                for i in range(count)
            ]
        )

    run_copies(
        [
            pltpu.make_async_copy(results.at[pl.ds(i * rows, rows)], outs_b[i], b_sems.at[i])
            for i in range(count)
        ]
    )


def join_kernel(count, *refs):
    ins, out, sems = refs[:count], refs[count], refs[count + 1]
    run_copies([pltpu.make_async_copy(ins[i], out.at[i], sems.at[i]) for i in range(count)])


def final_kernel(pieces, order, flag, *refs):
    cached, refs = refs[0], refs[1:]
    from_a, refs = refs[:pieces], refs[pieces:]
    from_b, refs = refs[:pieces], refs[pieces:]
    far, out, sems = refs[:2], refs[2], refs[3]
    me = lax.axis_index("seq")
    half = pieces // 2

    @pl.when(flag[0] > 0)
    def _():
        copies = []
        for position, offset in enumerate(order):
            pieces_of = (from_a[offset], from_b[offset], far[position // half].at[position % half])
            for group, piece in enumerate(pieces_of):
                copies.append(
                    pltpu.make_async_copy(
                        piece,
                        out.at[0, :, head_columns(me, offset, group, pieces)],
                        sems.at[group, offset],
                    )
                )
        run_copies(copies)

    @pl.when(flag[0] <= 0)
    def _():
        run_copies([pltpu.make_async_copy(cached, out, sems.at[0, 0])])


def body(query_rows, key_rows, value_rows, cached_rows, plan, timestep, assignment):
    pieces = lax.axis_size("seq")
    slots = lax.axis_size("batch")
    rows = query_rows.shape[1]
    order = ring(pieces)
    kind = query_rows.dtype
    dma = pltpu.SemaphoreType.DMA

    def forward(value, offset):
        if offset == 0:
            return value
        return lax.ppermute(value, "seq", [(s, (s + offset) % pieces) for s in range(pieces)])

    def backward(value, offset):
        return forward(value, (pieces - offset) % pieces)

    def across(value):
        mask = slots // 2
        return lax.ppermute(value, "batch", [(s, s ^ mask) for s in range(slots)])

    def shape(*dims):
        return jax.ShapeDtypeStruct(dims, kind)

    sources = (query_rows, key_rows, value_rows)
    far_out, flag = pl.pallas_call(
        functools.partial(pack_far_kernel, pieces, 2),
        out_shape=(shape(pieces, 3, rows, HEAD_DIM), jax.ShapeDtypeStruct((1,), jnp.int32)),
        in_specs=[SMEM] * 3 + [ANY] * 3,
        out_specs=(ANY, SMEM),
        scratch_shapes=[dma((pieces, 3))],
        compiler_params=params(),
        name="pack_far",
    )(assignment, timestep, plan, *sources)
    first_out = pl.pallas_call(
        functools.partial(pack_kernel, pieces, 0),
        out_shape=[shape(3, rows, HEAD_DIM)] * pieces,
        in_specs=[ANY] * 3,
        out_specs=[ANY] * pieces,
        scratch_shapes=[dma((pieces, 3))],
        compiler_params=params(),
        name="pack_first",
    )(*sources)
    far_in = across(far_out)
    first_in = [None] * pieces
    for offset in order:
        first_in[offset] = forward(first_out[offset], offset)

    packed = pl.pallas_call(
        functools.partial(pack_second_kernel, pieces, 1),
        out_shape=[shape(2, rows, HEAD_DIM)] * pieces + [shape(rows, HEAD_DIM)] * pieces,
        in_specs=[SMEM] + [ANY] * 4,
        out_specs=[ANY] * (2 * pieces),
        scratch_shapes=[dma((pieces, 3))],
        compiler_params=params(),
        name="pack_second",
    )(flag, *sources, far_in)
    pairs_in = [None] * pieces
    queries_in = [None] * pieces
    for offset in order:
        pairs_in[offset] = forward(packed[offset], offset)
    for offset in order:
        queries_in[offset] = forward(packed[pieces + offset], offset)

    def cost(blocks):
        flops = blocks * rows * rows * pieces * HEAD_DIM * 4
        return pl.CostEstimate(
            flops=flops, bytes_accessed=2 * pieces * rows * HEAD_DIM * 2, transcendentals=blocks * rows * rows * pieces
        )

    first_result = pl.pallas_call(
        functools.partial(first_kernel, pieces, rows),
        out_shape=[shape(rows, HEAD_DIM)] * pieces,
        in_specs=[ANY] * pieces,
        out_specs=[ANY] * pieces,
        scratch_shapes=[pltpu.VMEM((pieces * rows, HEAD_DIM), kind)] * 4
        + [dma((3, pieces)), dma((pieces,))],
        compiler_params=params(),
        cost_estimate=cost(pieces),
        name="attend_first",
    )(*first_in)

    result_a = [None] * pieces
    result_b = [None] * pieces
    count = 2
    for begin in range(0, pieces, count):
        offsets = order[begin : begin + count]
        results = pl.pallas_call(
            functools.partial(second_kernel, pieces, rows, count),
            out_shape=[shape(rows, HEAD_DIM)] * (2 * count),
            in_specs=[SMEM] + [ANY] * (pieces + 2 * count),
            out_specs=[ANY] * (2 * count),
            scratch_shapes=[
                pltpu.VMEM((count * rows, HEAD_DIM), kind),
                pltpu.VMEM((pieces * rows, HEAD_DIM), kind),
                pltpu.VMEM((pieces * rows, HEAD_DIM), kind),
                pltpu.VMEM((count * rows, HEAD_DIM), kind),
                dma((2, pieces)),
                dma((count,)),
                dma((count,)),
                dma((count,)),
            ],
            compiler_params=params(),
            cost_estimate=cost(count),
            name=f"attend_second_{begin}",
        )(
            flag,
            *pairs_in,
            *[queries_in[offset] for offset in offsets],
            *[first_result[offset] for offset in offsets],
        )
        for i, offset in enumerate(offsets):
            result_a[offset] = results[i]
            result_b[offset] = results[count + i]

    back_a = [None] * pieces
    back_b = [None] * pieces
    for offset in order:
        back_a[offset] = backward(result_a[offset], offset)
    half = pieces // 2
    far_back = []
    for begin in range(0, pieces, half):
        joined = pl.pallas_call(
            functools.partial(join_kernel, half),
            out_shape=shape(half, rows, HEAD_DIM),
            in_specs=[ANY] * half,
            out_specs=ANY,
            scratch_shapes=[dma((half,))],
            compiler_params=params(),
            name=f"join_{begin}",
        )(*[back_a[offset] for offset in order[begin : begin + half]])
        far_back.append(across(joined))
    for offset in order:
        back_b[offset] = backward(result_b[offset], offset)

    return pl.pallas_call(
        functools.partial(final_kernel, pieces, order),
        out_shape=shape(*cached_rows.shape),
        in_specs=[SMEM] + [ANY] * (1 + 2 * pieces + 2),
        out_specs=ANY,
        scratch_shapes=[dma((GROUPS, pieces))],
        compiler_params=params(),
        name="final",
    )(flag, cached_rows, *back_a, *back_b, *far_back)


def solution(mesh):
    rows = P("batch", "seq", None)
    return jax.shard_map(
        body,
        mesh=mesh,
        in_specs=(rows, rows, rows, rows, P(), P(), P()),
        out_specs=rows,
        check_vma=False,
    )
```

time: 399 us -> 226 us (0.57)
  the two profiles are of different devices: /device:TPU:34 before, /device:TPU:2 now
where the time goes in v1:
time: 226 us; the launch traced here: 221 us
  starting transfers between devices  95.9 us (42%)
  Pallas kernels  63.2 us (28%)
  waiting for transfers between devices  56.9 us (25%)
  local copies, waits for them, and re-layouts  5.13 us (2%)
    ppermute x35, starting transfers between devices, forward(): lax.ppermute(value, 'seq', [(s, (s + offset) % pieces) for s in range(pie...  86.1 us
    ppermute x35, waiting for transfers between devices, forward(): lax.ppermute(value, 'seq', [(s, (s + offset) % pieces) for s in range(pie...  43.2 us
    pallas_call x4, Pallas kernels, body(): pl.pallas_call(functools.partial(second_kernel, pieces, rows, count), out...  31.2 us
    pallas_call x1, Pallas kernels, body(): pl.pallas_call(functools.partial(first_kernel, pieces, rows), out_shape=[...  21.9 us
    ppermute x3, waiting for transfers between devices, across(): return lax.ppermute(value, 'batch', [(s, s ^ mask) for s in range(slots)])  13.7 us
    ppermute x3, starting transfers between devices, across(): return lax.ppermute(value, 'batch', [(s, s ^ mask) for s in range(slots)])  9.74 us
    unnamed x18, local copies, waits for them, and re-layouts  5.13 us
  transfers between devices with their start and end apart: 38, of which 8 were waited for; matrix products, arithmetic and copies ran while one was open for 0% of the time, Pallas kernels for 26%

profile of v1, /device:TPU:2, one launch (start us, length us, event | category | flops | bytes accessed | tf_op | source)
XLA Modules:
  0.0 221.5 jit_solution(10403499036000121498)
XLA Ops:
  0.0 1.5 copy-done
  1.5 1.5 copy-done.2
  3.1 0.7 copy-done.5
  3.8 0.7 copy-done.6
  4.5 0.7 copy-done.7
  5.1 3.1 %pack_far.1 = (bf16[8,3,320,128]{3,2,1,0:T(8,128)(2,1)S(1)}, s32[1]{0:T(128)}) custom-call(s32[32]{0:T(128)S(1)} %copy-done.6, s32[32]{0:T(128)S(1)} %copy-done.7, s32[32,28]{1,0:T(8,128)S(1)} %copy-done.5, bf16[1,320,3072]{2,1,0:T(8,128)(2,1)S(1)} %copy-done, bf16[1,320,3072]{2,1,0:T(8,128)(2,1)S(1)} %copy-done.2, bf16[1,320,3072]{2,1,0:T(8,128)(2,1)} %refs_2_.5), custom_call_target="tpu_custom_call" | custom-call | tf_op jit(solution)/shard_map/pack_far/pallas_call | solution.py:253
  8.2 3.3 %collective-permute-start = (bf16[8,3,320,128]{3,2,1,0:T(8,128)(2,1)S(1)}, bf16[8,3,320,128]{3,2,1,0:T(8,128)(2,1)S(1)}, u32[]{:S(2)}, u32[]{:S(2)}) collective-permute-start(bf16[8,3,320,128]{3,2,1,0:T(8,128)(2,1)S(1)} %get-tuple-element.56), channel_id=1, source_target_pairs={{0,128},{8,136},{16,144},{24,152},{32,160},{40,168},{48,176},{56,1... | collective-permute-start | bytes 5898248 | tf_op jit(solution)/shard_map/ppermute | solution.py:247
  11.5 1.5 pack_first.1
  13.1 2.0 collective-permute-start.9
  15.1 3.3 %collective-permute-start.10 = (bf16[3,320,128]{2,1,0:T(8,128)(2,1)S(1)}, bf16[3,320,128]{2,1,0:T(8,128)(2,1)S(1)}, u32[]{:S(2)}, u32[]{:S(2)}) collective-permute-start(bf16[3,320,128]{2,1,0:T(8,128)(2,1)S(1)} %get-tuple-element.69), channel_id=1, source_target_pairs={{0,2},{1,3},{2,4},{3,5},{4,6},{5,7},{6,0},{7,1},{8,10},{9,11},{10,... | collective-permute-start | bytes 737288 | tf_op jit(solution)/shard_map/ppermute | solution.py:240
  18.3 4.0 %collective-permute-start.11 = (bf16[3,320,128]{2,1,0:T(8,128)(2,1)S(1)}, bf16[3,320,128]{2,1,0:T(8,128)(2,1)S(1)}, u32[]{:S(2)}, u32[]{:S(2)}) collective-permute-start(bf16[3,320,128]{2,1,0:T(8,128)(2,1)S(1)} %get-tuple-element.70), channel_id=1, source_target_pairs={{0,3},{1,4},{2,5},{3,6},{4,7},{5,0},{6,1},{7,2},{8,11},{9,12},{10,... | collective-permute-start | bytes 737288 | tf_op jit(solution)/shard_map/ppermute | solution.py:240
  22.4 0.5 collective-permute-start.12
  22.9 3.8 %collective-permute-done.9.refs_1_ = bf16[3,320,128]{2,1,0:T(8,128)(2,1)S(1)} collective-permute-done((bf16[3,320,128]{2,1,0:T(8,128)(2,1)S(1)}, bf16[3,320,128]{2,1,0:T(8,128)(2,1)S(1)}, u32[]{:S(2)}, u32[]{:S(2)}) %collective-permute-start.9) | collective-permute-done | bytes 245792 | tf_op jit(solution)/shard_map/ppermute | solution.py:240
  26.7 4.7 %collective-permute-start.13 = (bf16[3,320,128]{2,1,0:T(8,128)(2,1)S(1)}, bf16[3,320,128]{2,1,0:T(8,128)(2,1)S(1)}, u32[]{:S(2)}, u32[]{:S(2)}) collective-permute-start(bf16[3,320,128]{2,1,0:T(8,128)(2,1)S(1)} %get-tuple-element.72), channel_id=1, source_target_pairs={{0,5},{1,6},{2,7},{3,0},{4,1},{5,2},{6,3},{7,4},{8,13},{9,14},{10,... | collective-permute-start | bytes 737288 | tf_op jit(solution)/shard_map/ppermute | solution.py:240
  31.4 9.3 %collective-permute-done.10.refs_2_ = bf16[3,320,128]{2,1,0:T(8,128)(2,1)S(1)} collective-permute-done((bf16[3,320,128]{2,1,0:T(8,128)(2,1)S(1)}, bf16[3,320,128]{2,1,0:T(8,128)(2,1)S(1)}, u32[]{:S(2)}, u32[]{:S(2)}) %collective-permute-start.10) | collective-permute-done | bytes 245792 | tf_op jit(solution)/shard_map/ppermute | solution.py:240
  40.7 0.0 collective-permute-start.14
  40.7 13.7 %collective-permute-done.refs_3_ = bf16[8,3,320,128]{3,2,1,0:T(8,128)(2,1)S(1)} collective-permute-done((bf16[8,3,320,128]{3,2,1,0:T(8,128)(2,1)S(1)}, bf16[8,3,320,128]{3,2,1,0:T(8,128)(2,1)S(1)}, u32[]{:S(2)}, u32[]{:S(2)}) %collective-permute-start) | collective-permute-done | bytes 1966112 | tf_op jit(solution)/shard_map/ppermute | solution.py:247
  54.4 5.9 %collective-permute-start.15 = (bf16[3,320,128]{2,1,0:T(8,128)(2,1)S(1)}, bf16[3,320,128]{2,1,0:T(8,128)(2,1)S(1)}, u32[]{:S(2)}, u32[]{:S(2)}) collective-permute-start(bf16[3,320,128]{2,1,0:T(8,128)(2,1)S(1)} %get-tuple-element.74), channel_id=1, source_target_pairs={{0,7},{1,0},{2,1},{3,2},{4,3},{5,4},{6,5},{7,6},{8,15},{9,8},{10,9... | collective-permute-start | bytes 737288 | tf_op jit(solution)/shard_map/ppermute | solution.py:240
  60.2 2.5 %pack_second.1 = (bf16[2,320,128]{2,1,0:T(8,128)(2,1)S(1)}, bf16[2,320,128]{2,1,0:T(8,128)(2,1)S(1)}, bf16[2,320,128]{2,1,0:T(8,128)(2,1)S(1)}, bf16[2,320,128]{...) custom-call(s32[1]{0:T(128)} %get-tuple-element.55.flag, ...), custom_call_target="tpu_custom_call" | custom-call | tf_op jit(solution)/shard_map/pack_second/pallas_call | solution.py:276
  62.7 0.0 collective-permute-done.11.refs_3_
  62.7 0.1 collective-permute-start.1
  62.8 0.0 collective-permute-done.12.refs_4_
  62.8 2.3 %collective-permute-start.2 = (bf16[2,320,128]{2,1,0:T(8,128)(2,1)S(1)}, bf16[2,320,128]{2,1,0:T(8,128)(2,1)S(1)}, u32[]{:S(2)}, u32[]{:S(2)}) collective-permute-start(bf16[2,320,128]{2,1,0:T(8,128)(2,1)S(1)} %get-tuple-element.59), channel_id=1, source_target_pairs={{0,2},{1,3},{2,4},{3,5},{4,6},{5,7},{6,0},{7,1},{8,10},{9,11},{10,... | collective-permute-start | bytes 491528 | tf_op jit(solution)/shard_map/ppermute | solution.py:240
  65.2 3.6 %collective-permute-start.3 = (bf16[2,320,128]{2,1,0:T(8,128)(2,1)S(1)}, bf16[2,320,128]{2,1,0:T(8,128)(2,1)S(1)}, u32[]{:S(2)}, u32[]{:S(2)}) collective-permute-start(bf16[2,320,128]{2,1,0:T(8,128)(2,1)S(1)} %get-tuple-element.60), channel_id=1, source_target_pairs={{0,3},{1,4},{2,5},{3,6},{4,7},{5,0},{6,1},{7,2},{8,11},{9,12},{10,... | collective-permute-start | bytes 491528 | tf_op jit(solution)/shard_map/ppermute | solution.py:240
  68.8 0.6 collective-permute-start.4
  69.4 2.3 %collective-permute-start.8 = (bf16[320,128]{1,0:T(8,128)(2,1)S(1)}, bf16[320,128]{1,0:T(8,128)(2,1)S(1)}, u32[]{:S(2)}, u32[]{:S(2)}) collective-permute-start(bf16[320,128]{1,0:T(8,128)(2,1)S(1)} %get-tuple-element.66), channel_id=1, source_target_pairs={{0,1},{1,2},{2,3},{3,4},{4,5},{5,6},{6,7},{7,0},{8,9},{9,10},{10,1... | collective-permute-start | bytes 245768 | tf_op jit(solution)/shard_map/ppermute | solution.py:240
  71.7 23.2 %collective-permute-done.8.refs_9_ = bf16[320,128]{1,0:T(8,128)(2,1)S(1)} collective-permute-done((bf16[320,128]{1,0:T(8,128)(2,1)S(1)}, bf16[320,128]{1,0:T(8,128)(2,1)S(1)}, u32[]{:S(2)}, u32[]{:S(2)}) %collective-permute-start.8) | collective-permute-done | bytes 81952 | tf_op jit(solution)/shard_map/ppermute | solution.py:240
  94.9 2.8 %collective-permute-start.6 = (bf16[2,320,128]{2,1,0:T(8,128)(2,1)S(1)}, bf16[2,320,128]{2,1,0:T(8,128)(2,1)S(1)}, u32[]{:S(2)}, u32[]{:S(2)}) collective-permute-start(bf16[2,320,128]{2,1,0:T(8,128)(2,1)S(1)} %get-tuple-element.63), channel_id=1, source_target_pairs={{0,6},{1,7},{2,0},{3,1},{4,2},{5,3},{6,4},{7,5},{8,14},{9,15},{10,... | collective-permute-start | bytes 491528 | tf_op jit(solution)/shard_map/ppermute | solution.py:240
  97.8 1.1 collective-permute-start.7
  98.9 0.5 collective-permute-start.17
  99.4 2.4 %collective-permute-start.18 = (bf16[320,128]{1,0:T(8,128)(2,1)S(1)}, bf16[320,128]{1,0:T(8,128)(2,1)S(1)}, u32[]{:S(2)}, u32[]{:S(2)}) collective-permute-start(bf16[320,128]{1,0:T(8,128)(2,1)S(1)} %get-tuple-element.80), channel_id=1, source_target_pairs={{0,2},{1,3},{2,4},{3,5},{4,6},{5,7},{6,0},{7,1},{8,10},{9,11},{10,... | collective-permute-start | bytes 245768 | tf_op jit(solution)/shard_map/ppermute | solution.py:240
  101.8 21.9 %attend_first.1 = (bf16[320,128]{1,0:T(8,128)(2,1)S(1)}, bf16[320,128]{1,0:T(8,128)(2,1)S(1)}, bf16[320,128]{1,0:T(8,128)(2,1)S(1)}, bf16[320,128]{1,0:T(8,128)(...) custom-call(bf16[3,320,128]{2,1,0:T(8,128)(2,1)S(1)} %get-tuple-elem, ...), custom_call_target="tpu_custom_call" | custom-call | flops 3355443200 | bytes 1310720 | tf_op jit(solution)/shard_map/attend_first/pallas_call | solution.py:298
  123.7 1.8 collective-permute-start.20
  125.4 2.6 %collective-permute-start.21 = (bf16[320,128]{1,0:T(8,128)(2,1)S(1)}, bf16[320,128]{1,0:T(8,128)(2,1)S(1)}, u32[]{:S(2)}, u32[]{:S(2)}) collective-permute-start(bf16[320,128]{1,0:T(8,128)(2,1)S(1)} %get-tuple-element.85), channel_id=1, source_target_pairs={{0,3},{1,4},{2,5},{3,6},{4,7},{5,0},{6,1},{7,2},{8,11},{9,12},{10,... | collective-permute-start | bytes 245768 | tf_op jit(solution)/shard_map/ppermute | solution.py:240
  128.1 2.4 %collective-permute-start.23 = (bf16[320,128]{1,0:T(8,128)(2,1)S(1)}, bf16[320,128]{1,0:T(8,128)(2,1)S(1)}, u32[]{:S(2)}, u32[]{:S(2)}) collective-permute-start(bf16[320,128]{1,0:T(8,128)(2,1)S(1)} %get-tuple-element.89), channel_id=1, source_target_pairs={{0,5},{1,6},{2,7},{3,0},{4,1},{5,2},{6,3},{7,4},{8,13},{9,14},{10,... | collective-permute-start | bytes 245768 | tf_op jit(solution)/shard_map/ppermute | solution.py:240
  130.5 7.8 %attend_second_0.1 = (bf16[320,128]{1,0:T(8,128)(2,1)S(1)}, bf16[320,128]{1,0:T(8,128)(2,1)S(1)}, bf16[320,128]{1,0:T(8,128)(2,1)S(1)}, bf16[320,128]{1,0:T(8,128)(2,1)S(1)}) custom-call(s32[1]{0:T(128)} %get-tuple-element.55.flag, bf16[2,320,128]{2,1,0:T(8,128)(2,1)S(1)} %get-tuple-element.57.refs_0_, ...), custom_call_target="tpu_custom_call" | custom-call | flops 838860800 | bytes 1310720 | tf_op jit(solution)/shard_map/attend_second_0/pallas_call | solution.py:315
  138.3 3.5 %collective-permute-start.24 = (bf16[320,128]{1,0:T(8,128)(2,1)S(1)}, bf16[320,128]{1,0:T(8,128)(2,1)S(1)}, u32[]{:S(2)}, u32[]{:S(2)}) collective-permute-start(bf16[320,128]{1,0:T(8,128)(2,1)S(1)} %get-tuple-element.90), channel_id=1, source_target_pairs={{0,4},{1,5},{2,6},{3,7},{4,0},{5,1},{6,2},{7,3},{8,12},{9,13},{10,... | collective-permute-start | bytes 245768 | tf_op jit(solution)/shard_map/ppermute | solution.py:240
  141.7 0.7 collective-permute-start.16
  142.4 7.8 %attend_second_2.1 = (bf16[320,128]{1,0:T(8,128)(2,1)S(1)}, bf16[320,128]{1,0:T(8,128)(2,1)S(1)}, bf16[320,128]{1,0:T(8,128)(2,1)S(1)}, bf16[320,128]{1,0:T(8,128)(2,1)S(1)}) custom-call(s32[1]{0:T(128)} %get-tuple-element.55.flag, bf16[2,320,128]{2,1,0:T(8,128)(2,1)S(1)} %get-tuple-element.57.refs_0_, ...), custom_call_target="tpu_custom_call" | custom-call | flops 838860800 | bytes 1310720 | tf_op jit(solution)/shard_map/attend_second_2/pallas_call | solution.py:315
  150.2 12.7 %collective-permute-start.19 = (bf16[320,128]{1,0:T(8,128)(2,1)S(1)}, bf16[320,128]{1,0:T(8,128)(2,1)S(1)}, u32[]{:S(2)}, u32[]{:S(2)}) collective-permute-start(bf16[320,128]{1,0:T(8,128)(2,1)S(1)} %get-tuple-element.83), channel_id=1, source_target_pairs={{0,6},{1,7},{2,0},{3,1},{4,2},{5,3},{6,4},{7,5},{8,14},{9,15},{10,... | collective-permute-start | bytes 245768 | tf_op jit(solution)/shard_map/ppermute | solution.py:240
  162.9 7.8 %attend_second_4.1 = (bf16[320,128]{1,0:T(8,128)(2,1)S(1)}, bf16[320,128]{1,0:T(8,128)(2,1)S(1)}, bf16[320,128]{1,0:T(8,128)(2,1)S(1)}, bf16[320,128]{1,0:T(8,128)(2,1)S(1)}) custom-call(s32[1]{0:T(128)} %get-tuple-element.55.flag, bf16[2,320,128]{2,1,0:T(8,128)(2,1)S(1)} %get-tuple-element.57.refs_0_, ...), custom_call_target="tpu_custom_call" | custom-call | flops 838860800 | bytes 1310720 | tf_op jit(solution)/shard_map/attend_second_4/pallas_call | solution.py:315
  170.7 2.5 %collective-permute-start.22 = (bf16[320,128]{1,0:T(8,128)(2,1)S(1)}, bf16[320,128]{1,0:T(8,128)(2,1)S(1)}, u32[]{:S(2)}, u32[]{:S(2)}) collective-permute-start(bf16[320,128]{1,0:T(8,128)(2,1)S(1)} %get-tuple-element.88), channel_id=1, source_target_pairs={{0,5},{1,6},{2,7},{3,0},{4,1},{5,2},{6,3},{7,4},{8,13},{9,14},{10,... | collective-permute-start | bytes 245768 | tf_op jit(solution)/shard_map/ppermute | solution.py:240
  173.1 0.0 collective-permute-start.28
  173.1 0.0 copy-start.4
  173.1 7.9 %attend_second_6.1 = (bf16[320,128]{1,0:T(8,128)(2,1)S(1)}, bf16[320,128]{1,0:T(8,128)(2,1)S(1)}, bf16[320,128]{1,0:T(8,128)(2,1)S(1)}, bf16[320,128]{1,0:T(8,128)(2,1)S(1)}) custom-call(s32[1]{0:T(128)} %get-tuple-element.55.flag, bf16[2,320,128]{2,1,0:T(8,128)(2,1)S(1)} %get-tuple-element.57.refs_0_, ...), custom_call_target="tpu_custom_call" | custom-call | flops 838860800 | bytes 1310720 | tf_op jit(solution)/shard_map/attend_second_6/pallas_call | solution.py:315
  181.1 3.1 %collective-permute-start.25 = (bf16[320,128]{1,0:T(8,128)(2,1)S(1)}, bf16[320,128]{1,0:T(8,128)(2,1)S(1)}, u32[]{:S(2)}, u32[]{:S(2)}) collective-permute-start(bf16[320,128]{1,0:T(8,128)(2,1)S(1)} %get-tuple-element.93), channel_id=1, source_target_pairs={{0,4},{1,5},{2,6},{3,7},{4,0},{5,1},{6,2},{7,3},{8,12},{9,13},{10,... | collective-permute-start | bytes 245768 | tf_op jit(solution)/shard_map/ppermute | solution.py:240
  184.2 3.4 %collective-permute-start.26 = (bf16[320,128]{1,0:T(8,128)(2,1)S(1)}, bf16[320,128]{1,0:T(8,128)(2,1)S(1)}, u32[]{:S(2)}, u32[]{:S(2)}) collective-permute-start(bf16[320,128]{1,0:T(8,128)(2,1)S(1)} %get-tuple-element.94), channel_id=1, source_target_pairs={{0,3},{1,4},{2,5},{3,6},{4,7},{5,0},{6,1},{7,2},{8,11},{9,12},{10,... | collective-permute-start | bytes 245768 | tf_op jit(solution)/shard_map/ppermute | solution.py:240
  187.6 0.5 collective-permute-start.27
  188.1 0.4 join_0.1
  188.5 3.4 %collective-permute-start.36 = (bf16[4,320,128]{2,1,0:T(8,128)(2,1)S(1)}, bf16[4,320,128]{2,1,0:T(8,128)(2,1)S(1)}, u32[]{:S(2)}, u32[]{:S(2)}) collective-permute-start(bf16[4,320,128]{2,1,0:T(8,128)(2,1)S(1)} %join_0.1), channel_id=1, source_target_pairs={{0,128},{8,136},{16,144},{24,152},{32,160},{40,168},{48,176},{56,1... | collective-permute-start | bytes 983048 | tf_op jit(solution)/shard_map/ppermute | solution.py:247
  192.0 1.0 collective-permute-done.26.refs_2_.refs_6_
  193.0 1.9 collective-permute-done.27.refs_0_.refs_7_
  194.8 0.4 join_4.1
  195.3 3.0 %collective-permute-start.37 = (bf16[4,320,128]{2,1,0:T(8,128)(2,1)S(1)}, bf16[4,320,128]{2,1,0:T(8,128)(2,1)S(1)}, u32[]{:S(2)}, u32[]{:S(2)}) collective-permute-start(bf16[4,320,128]{2,1,0:T(8,128)(2,1)S(1)} %join_4.1), channel_id=1, source_target_pairs={{0,128},{8,136},{16,144},{24,152},{32,160},{40,168},{48,176},{56,1... | collective-permute-start | bytes 983048 | tf_op jit(solution)/shard_map/ppermute | solution.py:247
  198.3 2.1 collective-permute-start.29
  200.4 2.0 collective-permute-start.30
  202.4 1.1 collective-permute-start.31
  203.5 3.6 %collective-permute-start.32 = (bf16[320,128]{1,0:T(8,128)(2,1)S(1)}, bf16[320,128]{1,0:T(8,128)(2,1)S(1)}, u32[]{:S(2)}, u32[]{:S(2)}) collective-permute-start(bf16[320,128]{1,0:T(8,128)(2,1)S(1)} %get-tuple-element.101), channel_id=1, source_target_pairs={{0,4},{1,5},{2,6},{3,7},{4,0},{5,1},{6,2},{7,3},{8,12},{9,13},{10,... | collective-permute-start | bytes 245768 | tf_op jit(solution)/shard_map/ppermute | solution.py:240
  207.1 4.0 %collective-permute-start.33 = (bf16[320,128]{1,0:T(8,128)(2,1)S(1)}, bf16[320,128]{1,0:T(8,128)(2,1)S(1)}, u32[]{:S(2)}, u32[]{:S(2)}) collective-permute-start(bf16[320,128]{1,0:T(8,128)(2,1)S(1)} %get-tuple-element.102), channel_id=1, source_target_pairs={{0,3},{1,4},{2,5},{3,6},{4,7},{5,0},{6,1},{7,2},{8,11},{9,12},{10,... | collective-permute-start | bytes 245768 | tf_op jit(solution)/shard_map/ppermute | solution.py:240
  211.1 1.6 collective-permute-start.34
  212.7 2.4 %collective-permute-start.35 = (bf16[320,128]{1,0:T(8,128)(2,1)S(1)}, bf16[320,128]{1,0:T(8,128)(2,1)S(1)}, u32[]{:S(2)}, u32[]{:S(2)}) collective-permute-start(bf16[320,128]{1,0:T(8,128)(2,1)S(1)} %get-tuple-element.104), channel_id=1, source_target_pairs={{0,1},{1,2},{2,3},{3,4},{4,5},{5,6},{6,7},{7,0},{8,9},{9,10},{10,1... | collective-permute-start | bytes 245768 | tf_op jit(solution)/shard_map/ppermute | solution.py:240
  215.1 3.8 %collective-permute-done.34.refs_15_ = bf16[320,128]{1,0:T(8,128)(2,1)S(1)} collective-permute-done((bf16[320,128]{1,0:T(8,128)(2,1)S(1)}, bf16[320,128]{1,0:T(8,128)(2,1)S(1)}, u32[]{:S(2)}, u32[]{:S(2)}) %collective-permute-start.34) | collective-permute-done | bytes 81952 | tf_op jit(solution)/shard_map/ppermute | solution.py:240
  218.9 0.2 collective-permute-done.35.refs_16_
  219.1 2.2 final.1
  (41 shorter events, 0.1 us)
Async XLA Ops:
  0.0 1.5 copy-start
  1.5 1.5 copy-start.2
  3.1 0.7 copy-start.5
  3.8 0.7 copy-start.6
  4.5 0.7 copy-start.7
  5.1 6.4 %copy-start.1 = (bf16[1,320,3072]{2,1,0:T(8,128)(2,1)S(1)}, bf16[1,320,3072]{2,1,0:T(8,128)(2,1)}, u32[]{:S(2)}) copy-start(bf16[1,320,3072]{2,1,0:T(8,128)(2,1)} %refs_0_.6) | copy-start | bytes 5898244
  5.1 6.4 %copy-start.3 = (bf16[1,320,3072]{2,1,0:T(8,128)(2,1)S(1)}, bf16[1,320,3072]{2,1,0:T(8,128)(2,1)}, u32[]{:S(2)}) copy-start(bf16[1,320,3072]{2,1,0:T(8,128)(2,1)} %refs_1_.5) | copy-start | bytes 5898244
  8.2 46.2 %collective-permute-start = (bf16[8,3,320,128]{3,2,1,0:T(8,128)(2,1)S(1)}, bf16[8,3,320,128]{3,2,1,0:T(8,128)(2,1)S(1)}, u32[]{:S(2)}, u32[]{:S(2)}) collective-permute-start(bf16[8,3,320,128]{3,2,1,0:T(8,128)(2,1)S(1)} %get-tuple-element.56), channel_id=1, source_target_pairs={{0,128},{8,136},{16,144},{24,152},{32,160},{40,168},{48,176},{56,1... | collective-permute-start | bytes 5898248 | tf_op jit(solution)/shard_map/ppermute | solution.py:247
  13.1 13.6 %collective-permute-start.9 = (bf16[3,320,128]{2,1,0:T(8,128)(2,1)S(1)}, bf16[3,320,128]{2,1,0:T(8,128)(2,1)S(1)}, u32[]{:S(2)}, u32[]{:S(2)}) collective-permute-start(bf16[3,320,128]{2,1,0:T(8,128)(2,1)S(1)} %get-tuple-element.68), channel_id=1, source_target_pairs={{0,1},{1,2},{2,3},{3,4},{4,5},{5,6},{6,7},{7,0},{8,9},{9,10},{10,1... | collective-permute-start | bytes 737288 | tf_op jit(solution)/shard_map/ppermute | solution.py:240
  15.1 25.6 %collective-permute-start.10 = (bf16[3,320,128]{2,1,0:T(8,128)(2,1)S(1)}, bf16[3,320,128]{2,1,0:T(8,128)(2,1)S(1)}, u32[]{:S(2)}, u32[]{:S(2)}) collective-permute-start(bf16[3,320,128]{2,1,0:T(8,128)(2,1)S(1)} %get-tuple-element.69), channel_id=1, source_target_pairs={{0,2},{1,3},{2,4},{3,5},{4,6},{5,7},{6,0},{7,1},{8,10},{9,11},{10,... | collective-permute-start | bytes 737288 | tf_op jit(solution)/shard_map/ppermute | solution.py:240
  18.3 44.4 %collective-permute-start.11 = (bf16[3,320,128]{2,1,0:T(8,128)(2,1)S(1)}, bf16[3,320,128]{2,1,0:T(8,128)(2,1)S(1)}, u32[]{:S(2)}, u32[]{:S(2)}) collective-permute-start(bf16[3,320,128]{2,1,0:T(8,128)(2,1)S(1)} %get-tuple-element.70), channel_id=1, source_target_pairs={{0,3},{1,4},{2,5},{3,6},{4,7},{5,0},{6,1},{7,2},{8,11},{9,12},{10,... | collective-permute-start | bytes 737288 | tf_op jit(solution)/shard_map/ppermute | solution.py:240
  22.4 40.5 %collective-permute-start.12 = (bf16[3,320,128]{2,1,0:T(8,128)(2,1)S(1)}, bf16[3,320,128]{2,1,0:T(8,128)(2,1)S(1)}, u32[]{:S(2)}, u32[]{:S(2)}) collective-permute-start(bf16[3,320,128]{2,1,0:T(8,128)(2,1)S(1)} %get-tuple-element.71), channel_id=1, source_target_pairs={{0,4},{1,5},{2,6},{3,7},{4,0},{5,1},{6,2},{7,3},{8,12},{9,13},{10,... | collective-permute-start | bytes 737288 | tf_op jit(solution)/shard_map/ppermute | solution.py:240
  26.7 38.5 %collective-permute-start.13 = (bf16[3,320,128]{2,1,0:T(8,128)(2,1)S(1)}, bf16[3,320,128]{2,1,0:T(8,128)(2,1)S(1)}, u32[]{:S(2)}, u32[]{:S(2)}) collective-permute-start(bf16[3,320,128]{2,1,0:T(8,128)(2,1)S(1)} %get-tuple-element.72), channel_id=1, source_target_pairs={{0,5},{1,6},{2,7},{3,0},{4,1},{5,2},{6,3},{7,4},{8,13},{9,14},{10,... | collective-permute-start | bytes 737288 | tf_op jit(solution)/shard_map/ppermute | solution.py:240
  40.7 28.1 %collective-permute-start.14 = (bf16[3,320,128]{2,1,0:T(8,128)(2,1)S(1)}, bf16[3,320,128]{2,1,0:T(8,128)(2,1)S(1)}, u32[]{:S(2)}, u32[]{:S(2)}) collective-permute-start(bf16[3,320,128]{2,1,0:T(8,128)(2,1)S(1)} %get-tuple-element.73), channel_id=1, source_target_pairs={{0,6},{1,7},{2,0},{3,1},{4,2},{5,3},{6,4},{7,5},{8,14},{9,15},{10,... | collective-permute-start | bytes 737288 | tf_op jit(solution)/shard_map/ppermute | solution.py:240
  54.4 5.9 %copy-start.8 = (bf16[8,3,320,128]{3,2,1,0:T(8,128)(2,1)}, bf16[8,3,320,128]{3,2,1,0:T(8,128)(2,1)S(1)}, u32[]{:S(2)}) copy-start(bf16[8,3,320,128]{3,2,1,0:T(8,128)(2,1)S(1)} %collective-permute-done.refs_3_) | copy-start | bytes 5898244
  54.4 15.0 %collective-permute-start.15 = (bf16[3,320,128]{2,1,0:T(8,128)(2,1)S(1)}, bf16[3,320,128]{2,1,0:T(8,128)(2,1)S(1)}, u32[]{:S(2)}, u32[]{:S(2)}) collective-permute-start(bf16[3,320,128]{2,1,0:T(8,128)(2,1)S(1)} %get-tuple-element.74), channel_id=1, source_target_pairs={{0,7},{1,0},{2,1},{3,2},{4,3},{5,4},{6,5},{7,6},{8,15},{9,8},{10,9... | collective-permute-start | bytes 737288 | tf_op jit(solution)/shard_map/ppermute | solution.py:240
  62.7 32.2 %collective-permute-start.1 = (bf16[2,320,128]{2,1,0:T(8,128)(2,1)S(1)}, bf16[2,320,128]{2,1,0:T(8,128)(2,1)S(1)}, u32[]{:S(2)}, u32[]{:S(2)}) collective-permute-start(bf16[2,320,128]{2,1,0:T(8,128)(2,1)S(1)} %get-tuple-element.58), channel_id=1, source_target_pairs={{0,1},{1,2},{2,3},{3,4},{4,5},{5,6},{6,7},{7,0},{8,9},{9,10},{10,1... | collective-permute-start | bytes 491528 | tf_op jit(solution)/shard_map/ppermute | solution.py:240
  62.8 34.9 %collective-permute-start.2 = (bf16[2,320,128]{2,1,0:T(8,128)(2,1)S(1)}, bf16[2,320,128]{2,1,0:T(8,128)(2,1)S(1)}, u32[]{:S(2)}, u32[]{:S(2)}) collective-permute-start(bf16[2,320,128]{2,1,0:T(8,128)(2,1)S(1)} %get-tuple-element.59), channel_id=1, source_target_pairs={{0,2},{1,3},{2,4},{3,5},{4,6},{5,7},{6,0},{7,1},{8,10},{9,11},{10,... | collective-permute-start | bytes 491528 | tf_op jit(solution)/shard_map/ppermute | solution.py:240
  65.2 33.7 %collective-permute-start.3 = (bf16[2,320,128]{2,1,0:T(8,128)(2,1)S(1)}, bf16[2,320,128]{2,1,0:T(8,128)(2,1)S(1)}, u32[]{:S(2)}, u32[]{:S(2)}) collective-permute-start(bf16[2,320,128]{2,1,0:T(8,128)(2,1)S(1)} %get-tuple-element.60), channel_id=1, source_target_pairs={{0,3},{1,4},{2,5},{3,6},{4,7},{5,0},{6,1},{7,2},{8,11},{9,12},{10,... | collective-permute-start | bytes 491528 | tf_op jit(solution)/shard_map/ppermute | solution.py:240
  68.8 30.6 %collective-permute-start.4 = (bf16[2,320,128]{2,1,0:T(8,128)(2,1)S(1)}, bf16[2,320,128]{2,1,0:T(8,128)(2,1)S(1)}, u32[]{:S(2)}, u32[]{:S(2)}) collective-permute-start(bf16[2,320,128]{2,1,0:T(8,128)(2,1)S(1)} %get-tuple-element.61), channel_id=1, source_target_pairs={{0,4},{1,5},{2,6},{3,7},{4,0},{5,1},{6,2},{7,3},{8,12},{9,13},{10,... | collective-permute-start | bytes 491528 | tf_op jit(solution)/shard_map/ppermute | solution.py:240
  69.4 25.5 %collective-permute-start.8 = (bf16[320,128]{1,0:T(8,128)(2,1)S(1)}, bf16[320,128]{1,0:T(8,128)(2,1)S(1)}, u32[]{:S(2)}, u32[]{:S(2)}) collective-permute-start(bf16[320,128]{1,0:T(8,128)(2,1)S(1)} %get-tuple-element.66), channel_id=1, source_target_pairs={{0,1},{1,2},{2,3},{3,4},{4,5},{5,6},{6,7},{7,0},{8,9},{9,10},{10,1... | collective-permute-start | bytes 245768 | tf_op jit(solution)/shard_map/ppermute | solution.py:240
  94.9 28.7 %collective-permute-start.5 = (bf16[2,320,128]{2,1,0:T(8,128)(2,1)S(1)}, bf16[2,320,128]{2,1,0:T(8,128)(2,1)S(1)}, u32[]{:S(2)}, u32[]{:S(2)}) collective-permute-start(bf16[2,320,128]{2,1,0:T(8,128)(2,1)S(1)} %get-tuple-element.62), channel_id=1, source_target_pairs={{0,5},{1,6},{2,7},{3,0},{4,1},{5,2},{6,3},{7,4},{8,13},{9,14},{10,... | collective-permute-start | bytes 491528 | tf_op jit(solution)/shard_map/ppermute | solution.py:240
  94.9 30.5 %collective-permute-start.6 = (bf16[2,320,128]{2,1,0:T(8,128)(2,1)S(1)}, bf16[2,320,128]{2,1,0:T(8,128)(2,1)S(1)}, u32[]{:S(2)}, u32[]{:S(2)}) collective-permute-start(bf16[2,320,128]{2,1,0:T(8,128)(2,1)S(1)} %get-tuple-element.63), channel_id=1, source_target_pairs={{0,6},{1,7},{2,0},{3,1},{4,2},{5,3},{6,4},{7,5},{8,14},{9,15},{10,... | collective-permute-start | bytes 491528 | tf_op jit(solution)/shard_map/ppermute | solution.py:240
  97.8 30.3 %collective-permute-start.7 = (bf16[2,320,128]{2,1,0:T(8,128)(2,1)S(1)}, bf16[2,320,128]{2,1,0:T(8,128)(2,1)S(1)}, u32[]{:S(2)}, u32[]{:S(2)}) collective-permute-start(bf16[2,320,128]{2,1,0:T(8,128)(2,1)S(1)} %get-tuple-element.64), channel_id=1, source_target_pairs={{0,7},{1,0},{2,1},{3,2},{4,3},{5,4},{6,5},{7,6},{8,15},{9,8},{10,9... | collective-permute-start | bytes 491528 | tf_op jit(solution)/shard_map/ppermute | solution.py:240
  98.9 39.4 %collective-permute-start.17 = (bf16[320,128]{1,0:T(8,128)(2,1)S(1)}, bf16[320,128]{1,0:T(8,128)(2,1)S(1)}, u32[]{:S(2)}, u32[]{:S(2)}) collective-permute-start(bf16[320,128]{1,0:T(8,128)(2,1)S(1)} %get-tuple-element.79), channel_id=1, source_target_pairs={{0,7},{1,0},{2,1},{3,2},{4,3},{5,4},{6,5},{7,6},{8,15},{9,8},{10,9... | collective-permute-start | bytes 245768 | tf_op jit(solution)/shard_map/ppermute | solution.py:240
  99.4 42.4 %collective-permute-start.18 = (bf16[320,128]{1,0:T(8,128)(2,1)S(1)}, bf16[320,128]{1,0:T(8,128)(2,1)S(1)}, u32[]{:S(2)}, u32[]{:S(2)}) collective-permute-start(bf16[320,128]{1,0:T(8,128)(2,1)S(1)} %get-tuple-element.80), channel_id=1, source_target_pairs={{0,2},{1,3},{2,4},{3,5},{4,6},{5,7},{6,0},{7,1},{8,10},{9,11},{10,... | collective-permute-start | bytes 245768 | tf_op jit(solution)/shard_map/ppermute | solution.py:240
  123.7 26.5 %collective-permute-start.20 = (bf16[320,128]{1,0:T(8,128)(2,1)S(1)}, bf16[320,128]{1,0:T(8,128)(2,1)S(1)}, u32[]{:S(2)}, u32[]{:S(2)}) collective-permute-start(bf16[320,128]{1,0:T(8,128)(2,1)S(1)} %get-tuple-element.84), channel_id=1, source_target_pairs={{0,6},{1,7},{2,0},{3,1},{4,2},{5,3},{6,4},{7,5},{8,14},{9,15},{10,... | collective-permute-start | bytes 245768 | tf_op jit(solution)/shard_map/ppermute | solution.py:240
  125.4 37.4 %collective-permute-start.21 = (bf16[320,128]{1,0:T(8,128)(2,1)S(1)}, bf16[320,128]{1,0:T(8,128)(2,1)S(1)}, u32[]{:S(2)}, u32[]{:S(2)}) collective-permute-start(bf16[320,128]{1,0:T(8,128)(2,1)S(1)} %get-tuple-element.85), channel_id=1, source_target_pairs={{0,3},{1,4},{2,5},{3,6},{4,7},{5,0},{6,1},{7,2},{8,11},{9,12},{10,... | collective-permute-start | bytes 245768 | tf_op jit(solution)/shard_map/ppermute | solution.py:240
  128.1 45.1 %collective-permute-start.23 = (bf16[320,128]{1,0:T(8,128)(2,1)S(1)}, bf16[320,128]{1,0:T(8,128)(2,1)S(1)}, u32[]{:S(2)}, u32[]{:S(2)}) collective-permute-start(bf16[320,128]{1,0:T(8,128)(2,1)S(1)} %get-tuple-element.89), channel_id=1, source_target_pairs={{0,5},{1,6},{2,7},{3,0},{4,1},{5,2},{6,3},{7,4},{8,13},{9,14},{10,... | collective-permute-start | bytes 245768 | tf_op jit(solution)/shard_map/ppermute | solution.py:240
  138.3 34.9 %collective-permute-start.24 = (bf16[320,128]{1,0:T(8,128)(2,1)S(1)}, bf16[320,128]{1,0:T(8,128)(2,1)S(1)}, u32[]{:S(2)}, u32[]{:S(2)}) collective-permute-start(bf16[320,128]{1,0:T(8,128)(2,1)S(1)} %get-tuple-element.90), channel_id=1, source_target_pairs={{0,4},{1,5},{2,6},{3,7},{4,0},{5,1},{6,2},{7,3},{8,12},{9,13},{10,... | collective-permute-start | bytes 245768 | tf_op jit(solution)/shard_map/ppermute | solution.py:240
  141.7 42.5 %collective-permute-start.16 = (bf16[320,128]{1,0:T(8,128)(2,1)S(1)}, bf16[320,128]{1,0:T(8,128)(2,1)S(1)}, u32[]{:S(2)}, u32[]{:S(2)}) collective-permute-start(bf16[320,128]{1,0:T(8,128)(2,1)S(1)} %get-tuple-element.78), channel_id=1, source_target_pairs={{0,7},{1,0},{2,1},{3,2},{4,3},{5,4},{6,5},{7,6},{8,15},{9,8},{10,9... | collective-permute-start | bytes 245768 | tf_op jit(solution)/shard_map/ppermute | solution.py:240
  150.2 37.4 %collective-permute-start.19 = (bf16[320,128]{1,0:T(8,128)(2,1)S(1)}, bf16[320,128]{1,0:T(8,128)(2,1)S(1)}, u32[]{:S(2)}, u32[]{:S(2)}) collective-permute-start(bf16[320,128]{1,0:T(8,128)(2,1)S(1)} %get-tuple-element.83), channel_id=1, source_target_pairs={{0,6},{1,7},{2,0},{3,1},{4,2},{5,3},{6,4},{7,5},{8,14},{9,15},{10,... | collective-permute-start | bytes 245768 | tf_op jit(solution)/shard_map/ppermute | solution.py:240
  170.7 21.3 %collective-permute-start.22 = (bf16[320,128]{1,0:T(8,128)(2,1)S(1)}, bf16[320,128]{1,0:T(8,128)(2,1)S(1)}, u32[]{:S(2)}, u32[]{:S(2)}) collective-permute-start(bf16[320,128]{1,0:T(8,128)(2,1)S(1)} %get-tuple-element.88), channel_id=1, source_target_pairs={{0,5},{1,6},{2,7},{3,0},{4,1},{5,2},{6,3},{7,4},{8,13},{9,14},{10,... | collective-permute-start | bytes 245768 | tf_op jit(solution)/shard_map/ppermute | solution.py:240
  173.1 15.0 %collective-permute-start.28 = (bf16[320,128]{1,0:T(8,128)(2,1)S(1)}, bf16[320,128]{1,0:T(8,128)(2,1)S(1)}, u32[]{:S(2)}, u32[]{:S(2)}) collective-permute-start(bf16[320,128]{1,0:T(8,128)(2,1)S(1)} %get-tuple-element.96), channel_id=1, source_target_pairs={{0,1},{1,2},{2,3},{3,4},{4,5},{5,6},{6,7},{7,0},{8,9},{9,10},{10,1... | collective-permute-start | bytes 245768 | tf_op jit(solution)/shard_map/ppermute | solution.py:240
  173.1 46.0 %copy-start.4 = (bf16[1,320,3072]{2,1,0:T(8,128)(2,1)S(1)}, bf16[1,320,3072]{2,1,0:T(8,128)(2,1)}, u32[]{:S(2)}) copy-start(bf16[1,320,3072]{2,1,0:T(8,128)(2,1)} %refs_0_.7) | copy-start | bytes 5898244
  181.1 10.9 %collective-permute-start.25 = (bf16[320,128]{1,0:T(8,128)(2,1)S(1)}, bf16[320,128]{1,0:T(8,128)(2,1)S(1)}, u32[]{:S(2)}, u32[]{:S(2)}) collective-permute-start(bf16[320,128]{1,0:T(8,128)(2,1)S(1)} %get-tuple-element.93), channel_id=1, source_target_pairs={{0,4},{1,5},{2,6},{3,7},{4,0},{5,1},{6,2},{7,3},{8,12},{9,13},{10,... | collective-permute-start | bytes 245768 | tf_op jit(solution)/shard_map/ppermute | solution.py:240
  184.2 8.8 %collective-permute-start.26 = (bf16[320,128]{1,0:T(8,128)(2,1)S(1)}, bf16[320,128]{1,0:T(8,128)(2,1)S(1)}, u32[]{:S(2)}, u32[]{:S(2)}) collective-permute-start(bf16[320,128]{1,0:T(8,128)(2,1)S(1)} %get-tuple-element.94), channel_id=1, source_target_pairs={{0,3},{1,4},{2,5},{3,6},{4,7},{5,0},{6,1},{7,2},{8,11},{9,12},{10,... | collective-permute-start | bytes 245768 | tf_op jit(solution)/shard_map/ppermute | solution.py:240
  187.6 7.2 %collective-permute-start.27 = (bf16[320,128]{1,0:T(8,128)(2,1)S(1)}, bf16[320,128]{1,0:T(8,128)(2,1)S(1)}, u32[]{:S(2)}, u32[]{:S(2)}) collective-permute-start(bf16[320,128]{1,0:T(8,128)(2,1)S(1)} %get-tuple-element.95), channel_id=1, source_target_pairs={{0,2},{1,3},{2,4},{3,5},{4,6},{5,7},{6,0},{7,1},{8,10},{9,11},{10,... | collective-permute-start | bytes 245768 | tf_op jit(solution)/shard_map/ppermute | solution.py:240
  188.5 30.6 %collective-permute-start.36 = (bf16[4,320,128]{2,1,0:T(8,128)(2,1)S(1)}, bf16[4,320,128]{2,1,0:T(8,128)(2,1)S(1)}, u32[]{:S(2)}, u32[]{:S(2)}) collective-permute-start(bf16[4,320,128]{2,1,0:T(8,128)(2,1)S(1)} %join_0.1), channel_id=1, source_target_pairs={{0,128},{8,136},{16,144},{24,152},{32,160},{40,168},{48,176},{56,1... | collective-permute-start | bytes 983048 | tf_op jit(solution)/shard_map/ppermute | solution.py:247
  195.3 23.8 %collective-permute-start.37 = (bf16[4,320,128]{2,1,0:T(8,128)(2,1)S(1)}, bf16[4,320,128]{2,1,0:T(8,128)(2,1)S(1)}, u32[]{:S(2)}, u32[]{:S(2)}) collective-permute-start(bf16[4,320,128]{2,1,0:T(8,128)(2,1)S(1)} %join_4.1), channel_id=1, source_target_pairs={{0,128},{8,136},{16,144},{24,152},{32,160},{40,168},{48,176},{56,1... | collective-permute-start | bytes 983048 | tf_op jit(solution)/shard_map/ppermute | solution.py:247
  198.3 5.2 %collective-permute-start.29 = (bf16[320,128]{1,0:T(8,128)(2,1)S(1)}, bf16[320,128]{1,0:T(8,128)(2,1)S(1)}, u32[]{:S(2)}, u32[]{:S(2)}) collective-permute-start(bf16[320,128]{1,0:T(8,128)(2,1)S(1)} %get-tuple-element.98), channel_id=1, source_target_pairs={{0,7},{1,0},{2,1},{3,2},{4,3},{5,4},{6,5},{7,6},{8,15},{9,8},{10,9... | collective-permute-start | bytes 245768 | tf_op jit(solution)/shard_map/ppermute | solution.py:240
  200.4 6.6 %collective-permute-start.30 = (bf16[320,128]{1,0:T(8,128)(2,1)S(1)}, bf16[320,128]{1,0:T(8,128)(2,1)S(1)}, u32[]{:S(2)}, u32[]{:S(2)}) collective-permute-start(bf16[320,128]{1,0:T(8,128)(2,1)S(1)} %get-tuple-element.99), channel_id=1, source_target_pairs={{0,6},{1,7},{2,0},{3,1},{4,2},{5,3},{6,4},{7,5},{8,14},{9,15},{10,... | collective-permute-start | bytes 245768 | tf_op jit(solution)/shard_map/ppermute | solution.py:240
  202.4 8.7 %collective-permute-start.31 = (bf16[320,128]{1,0:T(8,128)(2,1)S(1)}, bf16[320,128]{1,0:T(8,128)(2,1)S(1)}, u32[]{:S(2)}, u32[]{:S(2)}) collective-permute-start(bf16[320,128]{1,0:T(8,128)(2,1)S(1)} %get-tuple-element.100), channel_id=1, source_target_pairs={{0,5},{1,6},{2,7},{3,0},{4,1},{5,2},{6,3},{7,4},{8,13},{9,14},{10,... | collective-permute-start | bytes 245768 | tf_op jit(solution)/shard_map/ppermute | solution.py:240
  203.5 9.2 %collective-permute-start.32 = (bf16[320,128]{1,0:T(8,128)(2,1)S(1)}, bf16[320,128]{1,0:T(8,128)(2,1)S(1)}, u32[]{:S(2)}, u32[]{:S(2)}) collective-permute-start(bf16[320,128]{1,0:T(8,128)(2,1)S(1)} %get-tuple-element.101), channel_id=1, source_target_pairs={{0,4},{1,5},{2,6},{3,7},{4,0},{5,1},{6,2},{7,3},{8,12},{9,13},{10,... | collective-permute-start | bytes 245768 | tf_op jit(solution)/shard_map/ppermute | solution.py:240
  207.1 8.0 %collective-permute-start.33 = (bf16[320,128]{1,0:T(8,128)(2,1)S(1)}, bf16[320,128]{1,0:T(8,128)(2,1)S(1)}, u32[]{:S(2)}, u32[]{:S(2)}) collective-permute-start(bf16[320,128]{1,0:T(8,128)(2,1)S(1)} %get-tuple-element.102), channel_id=1, source_target_pairs={{0,3},{1,4},{2,5},{3,6},{4,7},{5,0},{6,1},{7,2},{8,11},{9,12},{10,... | collective-permute-start | bytes 245768 | tf_op jit(solution)/shard_map/ppermute | solution.py:240
  211.1 7.8 %collective-permute-start.34 = (bf16[320,128]{1,0:T(8,128)(2,1)S(1)}, bf16[320,128]{1,0:T(8,128)(2,1)S(1)}, u32[]{:S(2)}, u32[]{:S(2)}) collective-permute-start(bf16[320,128]{1,0:T(8,128)(2,1)S(1)} %get-tuple-element.103), channel_id=1, source_target_pairs={{0,2},{1,3},{2,4},{3,5},{4,6},{5,7},{6,0},{7,1},{8,10},{9,11},{10,... | collective-permute-start | bytes 245768 | tf_op jit(solution)/shard_map/ppermute | solution.py:240
  212.7 6.4 %collective-permute-start.35 = (bf16[320,128]{1,0:T(8,128)(2,1)S(1)}, bf16[320,128]{1,0:T(8,128)(2,1)S(1)}, u32[]{:S(2)}, u32[]{:S(2)}) collective-permute-start(bf16[320,128]{1,0:T(8,128)(2,1)S(1)} %get-tuple-element.104), channel_id=1, source_target_pairs={{0,1},{1,2},{2,3},{3,4},{4,5},{5,6},{6,7},{7,0},{8,9},{9,10},{10,1... | collective-permute-start | bytes 245768 | tf_op jit(solution)/shard_map/ppermute | solution.py:240

commit v2 on v1

v2 whole, which is shorter than its diff:
```python
import functools
import math

import jax
import jax.numpy as jnp
from jax import lax
from jax.experimental import pallas as pl
from jax.experimental.pallas import tpu as pltpu
from jax.sharding import PartitionSpec as P

HEAD_DIM = 128
GROUPS = 3
SHARED = pltpu.CompilerParams(vmem_limit_bytes=40 << 20)

ANY = pl.BlockSpec(memory_space=pl.ANY)
HBM = pl.BlockSpec(memory_space=pltpu.HBM)
SMEM = pl.BlockSpec(memory_space=pltpu.SMEM)


def ring(pieces):
    order = [0]
    for step in range(1, pieces // 2):
        order += [step, pieces - step]
    if pieces > 1:
        order.append(pieces // 2)
    return order


def head_columns(me, offset, group, pieces):
    head = group * pieces + lax.rem(me + offset, pieces)
    return pl.ds(pl.multiple_of(head * HEAD_DIM, HEAD_DIM), HEAD_DIM)


def run_copies(copies):
    for copy in copies:
        copy.start()
    for copy in copies:
        copy.wait()


def pack_kernel(pieces, offsets, *refs):
    sources, outs, sems = refs[:3], refs[3:-1], refs[-1]
    me = lax.axis_index("seq")
    run_copies(
        [
            pltpu.make_async_copy(
                sources[part].at[0, :, head_columns(me, offset, 0, pieces)],
                outs[i].at[part],
                sems.at[i, part],
            )
            for i, offset in enumerate(offsets)
            for part in range(3)
        ]
    )


def pack_far_kernel(width, assignment, timestep, plan, *refs):
    sources, out, flag, sems = refs[:3], refs[3], refs[4], refs[5]
    copies = [
        pltpu.make_async_copy(
            sources[part].at[0, :, pl.ds((GROUPS - 1) * width, width)], out.at[part], sems.at[part]
        )
        for part in range(3)
    ]
    for copy in copies:
        copy.start()
    request = assignment[lax.axis_index("batch")]
    flag[0] = plan[request, timestep[request]]
    for copy in copies:
        copy.wait()


def pack_second_kernel(pieces, offsets, flag, *refs):
    sources, far = refs[:3], refs[3]
    outs, sems = refs[4:-1], refs[-1]
    me = lax.axis_index("seq")

    def move(own):
        run_copies(
            [
                pltpu.make_async_copy(
                    sources[part].at[0, :, head_columns(me, offset, 1, pieces)]
                    if own
                    else far.at[part, :, head_columns(me, offset, 0, pieces)],
                    outs[i].at[part],
                    sems.at[i, part],
                )
                for i, offset in enumerate(offsets)
                for part in range(3)
            ]
        )

    pl.when(flag[0] > 0)(lambda: move(True))
    pl.when(flag[0] <= 0)(lambda: move(False))


def attend(queries, keys, values, results, scores, block, looped):
    factor = math.log2(math.e) / math.sqrt(HEAD_DIM)
    total_keys = keys.shape[0]
    blocks = queries.shape[0] // block
    step = next(c for c in range(512, total_keys + 1, 128) if total_keys % c == 0)
    spans = [(begin, begin + step) for begin in range(0, total_keys, step)]

    def place(i):
        if isinstance(i, int):
            return pl.ds(i * block, block)
        return pl.ds(pl.multiple_of(i * block, block), block)

    def lanes(value):
        return [value[:, c : c + HEAD_DIM] for c in range(0, value.shape[1], HEAD_DIM)]

    def score(query, span, target, peak):
        part = lax.dot_general(
            query, keys[span[0] : span[1]], (((1,), (1,)), ((), ())), preferred_element_type=jnp.float32
        )
        target[:, span[0] : span[1]] = part
        return functools.reduce(jnp.maximum, lanes(part) + ([] if peak is None else [peak]))

    def weigh(source, span, top, total, mixed):
        shifted = jnp.exp2((source[:, span[0] : span[1]] - top) * factor)
        total = functools.reduce(jnp.add, lanes(shifted) + ([] if total is None else [total]))
        part = jnp.dot(
            shifted.astype(jnp.bfloat16), values[span[0] : span[1]], preferred_element_type=jnp.float32
        )
        return total, part if mixed is None else mixed + part

    def one(i, following, current, upcoming, top):
        peak = total = mixed = None
        if following is not None:
            query = queries[place(following)]
        for span in spans:
            if following is not None:
                peak = score(query, span, upcoming, peak)
            total, mixed = weigh(current, span, top, total, mixed)
        results[place(i)] = (mixed / jnp.sum(total, axis=1, keepdims=True)).astype(jnp.bfloat16)
        return None if following is None else jnp.max(peak, axis=1, keepdims=True)

    peak = None
    query = queries[place(0)]
    for span in spans:
        peak = score(query, span, scores[0], peak)
    top = jnp.max(peak, axis=1, keepdims=True)
    if looped:

        def pair(i, top):
            top = one(2 * i, 2 * i + 1, scores[0], scores[1], top)
            return one(2 * i + 1, jnp.minimum(2 * i + 2, blocks - 1), scores[1], scores[0], top)

        lax.fori_loop(0, blocks // 2, pair, top)
    else:
        for i in range(blocks):
            following = i + 1 if i + 1 < blocks else None
            top = one(i, following, scores[i % 2], scores[(i + 1) % 2], top)


def first_kernel(pieces, rows, *refs):
    ins, outs = refs[:pieces], refs[pieces : 2 * pieces]
    queries, keys, values, results, one_scores, other_scores, sems, out_sems = refs[2 * pieces :]
    run_copies(
        [
            pltpu.make_async_copy(
                ins[i].at[part], (queries, keys, values)[part].at[pl.ds(i * rows, rows)], sems.at[part, i]
            )
            for part in range(3)
            for i in range(pieces)
        ]
    )
    attend(queries, keys, values, results, (one_scores, other_scores), rows, True)
    run_copies(
        [
            pltpu.make_async_copy(results.at[pl.ds(i * rows, rows)], outs[i], out_sems.at[i])
            for i in range(pieces)
        ]
    )


def second_kernel(pieces, rows, offsets, *refs):
    count = len(offsets)
    ins, refs = refs[:pieces], refs[pieces:]
    earlier, outs, refs = refs[:count], refs[count : 2 * count], refs[2 * count :]
    queries, keys, values, results, one_scores, other_scores, sems, query_sems, out_sems = refs
    forwarded = [
        pltpu.make_async_copy(earlier[i], outs[i].at[0], out_sems.at[0, i]) for i in range(count)
    ]
    fetch = [
        pltpu.make_async_copy(
            ins[i].at[1 + part], (keys, values)[part].at[pl.ds(i * rows, rows)], sems.at[part, i]
        )
        for part in range(2)
        for i in range(pieces)
    ] + [
        pltpu.make_async_copy(ins[offset].at[0], queries.at[pl.ds(i * rows, rows)], query_sems.at[i])
        for i, offset in enumerate(offsets)
    ]
    for copy in forwarded:
        copy.start()
    run_copies(fetch)
    attend(queries, keys, values, results, (one_scores, other_scores), rows, False)
    run_copies(
        [
            pltpu.make_async_copy(results.at[pl.ds(i * rows, rows)], outs[i].at[1], out_sems.at[1, i])
            for i in range(count)
        ]
    )
    for copy in forwarded:
        copy.wait()


def join_kernel(count, *refs):
    ins, out, sems = refs[:count], refs[count], refs[count + 1]
    run_copies([pltpu.make_async_copy(ins[i].at[1], out.at[i], sems.at[i]) for i in range(count)])


def final_kernel(pieces, chunks, flag, *refs):
    cached, back = refs[0], refs[1 : 1 + pieces]
    far, out, sems = refs[1 + pieces : 1 + pieces + len(chunks)], refs[-2], refs[-1]
    me = lax.axis_index("seq")

    @pl.when(flag[0] > 0)
    def _():
        copies = []
        for chunk, offsets in enumerate(chunks):
            for i, offset in enumerate(offsets):
                for group, piece in enumerate(
                    (back[offset].at[0], back[offset].at[1], far[chunk].at[i])
                ):
                    copies.append(
                        pltpu.make_async_copy(
                            piece,
                            out.at[0, :, head_columns(me, offset, group, pieces)],
                            sems.at[group, offset],
                        )
                    )
        run_copies(copies)

    @pl.when(flag[0] <= 0)
    def _():
        run_copies([pltpu.make_async_copy(cached, out, sems.at[0, 0])])


def body(query_rows, key_rows, value_rows, cached_rows, plan, timestep, assignment):
    pieces = lax.axis_size("seq")
    slots = lax.axis_size("batch")
    rows = query_rows.shape[1]
    group_width = pieces * HEAD_DIM
    order = ring(pieces)
    kind = query_rows.dtype
    dma = pltpu.SemaphoreType.DMA
    sources = (query_rows, key_rows, value_rows)

    def forward(value, offset):
        if offset == 0:
            return value
        return lax.ppermute(value, "seq", [(s, (s + offset) % pieces) for s in range(pieces)])

    def backward(value, offset):
        return forward(value, (pieces - offset) % pieces)

    def across(value):
        mask = slots // 2
        return lax.ppermute(value, "batch", [(s, s ^ mask) for s in range(slots)])

    def shape(*dims):
        return jax.ShapeDtypeStruct(dims, kind)

    def cost(blocks):
        pairs = blocks * rows * rows * pieces
        return pl.CostEstimate(
            flops=pairs * HEAD_DIM * 4,
            bytes_accessed=(2 * pieces + 2 * blocks) * rows * HEAD_DIM * 2,
            transcendentals=pairs,
        )

    far_out, flag = pl.pallas_call(
        functools.partial(pack_far_kernel, group_width),
        out_shape=(shape(3, rows, group_width), jax.ShapeDtypeStruct((1,), jnp.int32)),
        in_specs=[SMEM] * 3 + [HBM] * 3,
        out_specs=(ANY, SMEM),
        scratch_shapes=[dma((3,))],
        name="pack_far",
    )(assignment, timestep, plan, *sources)
    far_in = across(far_out)

    def ordered(values, after):
        return lax.optimization_barrier((*values, after))[: len(values)]

    def pack_first(offsets, sources):
        return pl.pallas_call(
            functools.partial(pack_kernel, pieces, offsets),
            out_shape=[shape(3, rows, HEAD_DIM)] * len(offsets),
            in_specs=[HBM] * 3,
            out_specs=[ANY] * len(offsets),
            scratch_shapes=[dma((len(offsets), 3))],
            name="pack_first",
        )(*sources)

    def pack_second(offsets, sources):
        return pl.pallas_call(
            functools.partial(pack_second_kernel, pieces, offsets),
            out_shape=[shape(3, rows, HEAD_DIM)] * len(offsets),
            in_specs=[SMEM] + [HBM] * 3 + [ANY],
            out_specs=[ANY] * len(offsets),
            scratch_shapes=[dma((len(offsets), 3))],
            compiler_params=SHARED,
            name="pack_second",
        )(flag, *sources, far_in)

    first_in = [None] * pieces
    early, late = order[:5], order[5:]
    for offset, value in zip(early, pack_first(early, sources)):
        first_in[offset] = forward(value, offset)
    for i, offset in enumerate(late):
        (value,) = pack_first([offset], ordered(sources, first_in[order[1 + i]]))
        first_in[offset] = forward(value, offset)

    second_in = [None] * pieces
    early, late = order[:-1], order[-1:]
    for offset, value in zip(early, pack_second(early, sources)):
        second_in[offset] = forward(value, offset)

    first_result = pl.pallas_call(
        functools.partial(first_kernel, pieces, rows),
        out_shape=[shape(rows, HEAD_DIM)] * pieces,
        in_specs=[ANY] * pieces,
        out_specs=[ANY] * pieces,
        scratch_shapes=[pltpu.VMEM((pieces * rows, HEAD_DIM), kind)] * 4
        + [pltpu.VMEM((rows, pieces * rows), jnp.float32)] * 2
        + [dma((3, pieces)), dma((pieces,))],
        cost_estimate=cost(pieces),
        compiler_params=SHARED,
        name="attend_first",
    )(*ordered(first_in, second_in[order[1]]))

    for offset, value in zip(late, pack_second(late, ordered(sources, first_result[0]))):
        second_in[offset] = forward(value, offset)

    count = 2
    chunks = [order[begin : begin + count] for begin in range(0, pieces, count)]
    back = [None] * pieces
    for offsets in chunks:
        results = pl.pallas_call(
            functools.partial(second_kernel, pieces, rows, offsets),
            out_shape=[shape(2, rows, HEAD_DIM)] * count,
            in_specs=[ANY] * (pieces + count),
            out_specs=[ANY] * count,
            scratch_shapes=[
                pltpu.VMEM((count * rows, HEAD_DIM), kind),
                pltpu.VMEM((pieces * rows, HEAD_DIM), kind),
                pltpu.VMEM((pieces * rows, HEAD_DIM), kind),
                pltpu.VMEM((count * rows, HEAD_DIM), kind),
                pltpu.VMEM((rows, pieces * rows), jnp.float32),
                pltpu.VMEM((rows, pieces * rows), jnp.float32),
                dma((2, pieces)),
                dma((count,)),
                dma((2, count)),
            ],
            cost_estimate=cost(count),
            compiler_params=SHARED,
            name="attend_second",
        )(*second_in, *[first_result[offset] for offset in offsets])
        for offset, value in zip(offsets, results):
            back[offset] = backward(value, offset)

    far_back = []
    for offsets in chunks:
        joined = pl.pallas_call(
            functools.partial(join_kernel, count),
            out_shape=shape(count, rows, HEAD_DIM),
            in_specs=[ANY] * count,
            out_specs=ANY,
            scratch_shapes=[dma((count,))],
            compiler_params=SHARED,
            name="join",
        )(*[back[offset] for offset in offsets])
        far_back.append(across(joined))

    return pl.pallas_call(
        functools.partial(final_kernel, pieces, chunks),
        out_shape=shape(*cached_rows.shape),
        in_specs=[SMEM, HBM] + [ANY] * (pieces + len(chunks)),
        out_specs=ANY,
        scratch_shapes=[dma((GROUPS, pieces))],
        compiler_params=SHARED,
        name="final",
    )(flag, cached_rows, *back, *far_back)


def solution(mesh):
    rows = P("batch", "seq", None)
    return jax.shard_map(
        body,
        mesh=mesh,
        in_specs=(rows, rows, rows, rows, P(), P(), P()),
        out_specs=rows,
        check_vma=False,
    )
```

time: 226 us -> 273 us (1.21)
  the two profiles are of different devices: /device:TPU:2 before, /device:TPU:34 now
where the time goes in v2:
time: 273 us
  Pallas kernels  167 us (61%)
  starting transfers between devices  56.1 us (21%)
  waiting for transfers between devices  46.4 us (17%)
  local copies, waits for them, and re-layouts  3.12 us (1%)
    pallas_call x4, Pallas kernels, pack_first(): pl.pallas_call(functools.partial(pack_kernel, pieces, offsets), out_shape...  64.2 us
    pallas_call x1, Pallas kernels, body(): pl.pallas_call(functools.partial(pack_far_kernel, group_width), out_shape...  62.1 us
    ppermute x21, starting transfers between devices, forward(): lax.ppermute(value, 'seq', [(s, (s + offset) % pieces) for s in range(pie...  48.6 us
    ppermute x21, waiting for transfers between devices, forward(): lax.ppermute(value, 'seq', [(s, (s + offset) % pieces) for s in range(pie...  39.6 us
    pallas_call x4, Pallas kernels, body(): pl.pallas_call(functools.partial(second_kernel, pieces, rows, offsets), o...  20.9 us
    pallas_call x1, Pallas kernels, body(): pl.pallas_call(functools.partial(first_kernel, pieces, rows), out_shape=[...  14.3 us
    ppermute x5, starting transfers between devices, across(): return lax.ppermute(value, 'batch', [(s, s ^ mask) for s in range(slots)])  7.56 us
    ppermute x5, waiting for transfers between devices, across(): return lax.ppermute(value, 'batch', [(s, s ^ mask) for s in range(slots)])  6.79 us
  transfers between devices with their start and end apart: 26, of which 7 were waited for; matrix products, arithmetic and copies ran while one was open for 0% of the time, Pallas kernels for 36%

profile of v2, /device:TPU:34, one launch (start us, length us, event | category | flops | bytes accessed | tf_op | source)
XLA Modules:
  0.0 272.7 jit_solution(4109570363818977342)
XLA Ops:
  0.0 62.1 %pack_far.1 = (bf16[3,320,1024]{2,1,0:T(8,128)(2,1)}, s32[1]{0:T(128)}) custom-call(s32[32]{0:T(128)} %assignment.1, s32[32]{0:T(128)} %timestep.1, s32[32,28]{1,0:T(8,128)} %plan.1, bf16[1,320,3072]{2,1,0:T(8,128)(2,1)} %refs_0_.10, bf16[1,320,3072]{2,1,0:T(8,128)(2,1)} %refs_1_.9, bf16[1,320,3072]{2,1,0:T(8,128)(2,1)} %refs_2_.9), custom_call_target="tpu_custom_call" | custom-call | tf_op jit(solution)/shard_map/pack_far/pallas_call | solution.py:274
  62.2 3.3 %collective-permute-start = (bf16[3,320,1024]{2,1,0:T(8,128)(2,1)}, bf16[3,320,1024]{2,1,0:T(8,128)(2,1)}, u32[]{:S(2)}, u32[]{:S(2)}) collective-permute-start(bf16[3,320,1024]{2,1,0:T(8,128)(2,1)} %get-tuple-element.56), channel_id=1, source_target_pairs={{0,128},{8,136},{16,144},{24,152},{32,160},{40,168},{48,176},{56,1... | collective-permute-start | bytes 5898248 | tf_op jit(solution)/shard_map/ppermute | solution.py:261
  65.4 38.5 %pack_first.4 = (bf16[3,320,128]{2,1,0:T(8,128)(2,1)}, bf16[3,320,128]{2,1,0:T(8,128)(2,1)}, bf16[3,320,128]{2,1,0:T(8,128)(2,1)}, bf16[3,320,128]{2,1,0:T(8,128)(2,1)}, bf16[3,320,128]{2,1,0:T(8,128)(2,1)}) custom-call(bf16[1,320,3072]{2,1,0:T(8,128)(2,1)} %refs_0_.10, bf16[1,320,3072]{2,1,0:T(8,128)(2,1)} %refs_1_.9, bf16[1,320,3072]{2,1,0:T(8,128)(2,1)} %refs_2_.9), custom_call_target="tpu_custom_call" | custom-call | tf_op jit(solution)/shard_map/pack_first/pallas_call | solution.py:288
  103.9 2.0 collective-permute-start.4
  105.9 4.5 %collective-permute-start.5 = (bf16[3,320,128]{2,1,0:T(8,128)(2,1)}, bf16[3,320,128]{2,1,0:T(8,128)(2,1)S(1)}, u32[]{:S(2)}, u32[]{:S(2)}) collective-permute-start(bf16[3,320,128]{2,1,0:T(8,128)(2,1)} %get-tuple-element.63), channel_id=1, source_target_pairs={{0,2},{1,3},{2,4},{3,5},{4,6},{5,7},{6,0},{7,1},{8,10},{9,11},{10,... | collective-permute-start | bytes 737288 | tf_op jit(solution)/shard_map/ppermute | solution.py:254
  110.4 0.0 collective-permute-start.8
  110.4 1.0 collective-permute-start.10
  111.4 5.8 %collective-permute-done.4.refs_1_ = bf16[3,320,128]{2,1,0:T(8,128)(2,1)S(1)} collective-permute-done((bf16[3,320,128]{2,1,0:T(8,128)(2,1)}, bf16[3,320,128]{2,1,0:T(8,128)(2,1)S(1)}, u32[]{:S(2)}, u32[]{:S(2)}) %collective-permute-start.4) | collective-permute-done | bytes 245792 | tf_op jit(solution)/shard_map/ppermute | solution.py:254
  117.2 8.6 %pack_first.5 = bf16[3,320,128]{2,1,0:T(8,128)(2,1)} custom-call(bf16[1,320,3072]{2,1,0:T(8,128)(2,1)} %refs_0_.10, bf16[1,320,3072]{2,1,0:T(8,128)(2,1)} %refs_1_.9, bf16[1,320,3072]{2,1,0:T(8,128)(2,1)} %refs_2_.9), custom_call_target="tpu_custom_call" | custom-call | tf_op jit(solution)/shard_map/pack_first/pallas_call | solution.py:288
  125.7 7.8 %collective-permute-start.6 = (bf16[3,320,128]{2,1,0:T(8,128)(2,1)}, bf16[3,320,128]{2,1,0:T(8,128)(2,1)S(1)}, u32[]{:S(2)}, u32[]{:S(2)}) collective-permute-start(bf16[3,320,128]{2,1,0:T(8,128)(2,1)} %pack_first.5), channel_id=1, source_target_pairs={{0,3},{1,4},{2,5},{3,6},{4,7},{5,0},{6,1},{7,2},{8,11},{9,12},{10,... | collective-permute-start | bytes 737288 | tf_op jit(solution)/shard_map/ppermute | solution.py:254
  133.6 0.0 collective-permute-done.5.refs_2_
  133.6 8.6 %pack_first.6 = bf16[3,320,128]{2,1,0:T(8,128)(2,1)} custom-call(bf16[1,320,3072]{2,1,0:T(8,128)(2,1)} %refs_0_.10, bf16[1,320,3072]{2,1,0:T(8,128)(2,1)} %refs_1_.9, bf16[1,320,3072]{2,1,0:T(8,128)(2,1)} %refs_2_.9), custom_call_target="tpu_custom_call" | custom-call | tf_op jit(solution)/shard_map/pack_first/pallas_call | solution.py:288
  142.2 0.0 copy-start
  142.2 0.1 collective-permute-start.7
  142.3 8.6 %pack_first.7 = bf16[3,320,128]{2,1,0:T(8,128)(2,1)} custom-call(bf16[1,320,3072]{2,1,0:T(8,128)(2,1)} %refs_0_.10, bf16[1,320,3072]{2,1,0:T(8,128)(2,1)} %refs_1_.9, bf16[1,320,3072]{2,1,0:T(8,128)(2,1)} %refs_2_.9), custom_call_target="tpu_custom_call" | custom-call | tf_op jit(solution)/shard_map/pack_first/pallas_call | solution.py:288
  150.9 3.3 %collective-permute-start.9 = (bf16[3,320,128]{2,1,0:T(8,128)(2,1)}, bf16[3,320,128]{2,1,0:T(8,128)(2,1)S(1)}, u32[]{:S(2)}, u32[]{:S(2)}) collective-permute-start(bf16[3,320,128]{2,1,0:T(8,128)(2,1)} %pack_first.7), channel_id=1, source_target_pairs={{0,5},{1,6},{2,7},{3,0},{4,1},{5,2},{6,3},{7,4},{8,13},{9,14},{10,... | collective-permute-start | bytes 737288 | tf_op jit(solution)/shard_map/ppermute | solution.py:254
  154.2 0.0 collective-permute-done.refs_3_
  154.2 1.5 copy-done.1
  155.7 1.5 copy-done.3
  157.3 1.4 pack_second.2
  158.6 2.6 collective-permute-start.1
  161.2 0.0 collective-permute-done.10.refs_6_
  161.2 0.0 collective-permute-start.2
  161.3 0.0 collective-permute-done.6.refs_3_
  161.3 1.5 collective-permute-start.3
  162.7 1.3 collective-permute-done.7.refs_4_
  164.1 2.3 collective-permute-start.12
  166.4 9.0 %collective-permute-done.9.refs_5_ = bf16[3,320,128]{2,1,0:T(8,128)(2,1)S(1)} collective-permute-done((bf16[3,320,128]{2,1,0:T(8,128)(2,1)}, bf16[3,320,128]{2,1,0:T(8,128)(2,1)S(1)}, u32[]{:S(2)}, u32[]{:S(2)}) %collective-permute-start.9) | collective-permute-done | bytes 245792 | tf_op jit(solution)/shard_map/ppermute | solution.py:254
  175.4 6.8 %collective-permute-start.13 = (bf16[3,320,128]{2,1,0:T(8,128)(2,1)S(1)}, bf16[3,320,128]{2,1,0:T(8,128)(2,1)S(1)}, u32[]{:S(2)}, u32[]{:S(2)}) collective-permute-start(bf16[3,320,128]{2,1,0:T(8,128)(2,1)S(1)} %get-tuple-element.88), channel_id=1, source_target_pairs={{0,6},{1,7},{2,0},{3,1},{4,2},{5,3},{6,4},{7,5},{8,14},{9,15},{10,... | collective-permute-start | bytes 737288 | tf_op jit(solution)/shard_map/ppermute | solution.py:254
  182.2 0.0 collective-permute-done.1.refs_1_
  182.2 0.0 collective-permute-start.14
  182.2 0.0 copy-start.2
  182.2 0.0 copy-start.4
  182.2 14.3 %attend_first.1 = (bf16[320,128]{1,0:T(8,128)(2,1)S(1)}, bf16[320,128]{1,0:T(8,128)(2,1)S(1)}, bf16[320,128]{1,0:T(8,128)(2,1)S(1)}, bf16[320,128]{1,0:T(8,128)(...) custom-call(bf16[3,320,128]{2,1,0:T(8,128)(2,1)S(1)} %copy-done.6, ...), custom_call_target="tpu_custom_call" | custom-call | flops 3355443200 | bytes 2621440 | tf_op jit(solution)/shard_map/attend_first/pallas_call | solution.py:321
  196.5 0.8 pack_second.3
  197.3 4.7 %collective-permute-start.11 = (bf16[3,320,128]{2,1,0:T(8,128)(2,1)S(1)}, bf16[3,320,128]{2,1,0:T(8,128)(2,1)S(1)}, u32[]{:S(2)}, u32[]{:S(2)}) collective-permute-start(bf16[3,320,128]{2,1,0:T(8,128)(2,1)S(1)} %pack_second.3), channel_id=1, source_target_pairs={{0,4},{1,5},{2,6},{3,7},{4,0},{5,1},{6,2},{7,3},{8,12},{9,13},{10,... | collective-permute-start | bytes 737288 | tf_op jit(solution)/shard_map/ppermute | solution.py:254
  202.0 0.0 collective-permute-done.14.refs_7_
  202.0 13.0 %collective-permute-done.11.refs_4_ = bf16[3,320,128]{2,1,0:T(8,128)(2,1)S(1)} collective-permute-done((bf16[3,320,128]{2,1,0:T(8,128)(2,1)S(1)}, bf16[3,320,128]{2,1,0:T(8,128)(2,1)S(1)}, u32[]{:S(2)}, u32[]{:S(2)}) %collective-permute-start.11) | collective-permute-done | bytes 245792 | tf_op jit(solution)/shard_map/ppermute | solution.py:254
  215.0 5.2 %attend_second.5 = (bf16[2,320,128]{2,1,0:T(8,128)(2,1)S(1)}, bf16[2,320,128]{2,1,0:T(8,128)(2,1)S(1)}) custom-call(bf16[3,320,128]{2,1,0:T(8,128)(2,1)S(1)} %get-tuple-element.57.refs_0_, bf16[3,320,128]{2,1,0:T(8,128)(2,1)S(1)} %collective-permute-done.1.refs_1_, bf16[3,320,128]{2,1,0:T(8,128)(2,1)S(1)} %collective-permute-done.2.refs_2_, ...), custom_call_target="tpu_custom_call" | custom-call | flops 838860800 | bytes 1638400 | tf_op jit(solution)/shard_map/attend_second/pallas_call | solution.py:341
  220.2 0.1 collective-permute-start.16
  220.3 0.1 collective-permute-start.21
  220.4 5.2 %attend_second.4 = (bf16[2,320,128]{2,1,0:T(8,128)(2,1)S(1)}, bf16[2,320,128]{2,1,0:T(8,128)(2,1)S(1)}) custom-call(bf16[3,320,128]{2,1,0:T(8,128)(2,1)S(1)} %get-tuple-element.57.refs_0_, bf16[3,320,128]{2,1,0:T(8,128)(2,1)S(1)} %collective-permute-done.1.refs_1_, bf16[3,320,128]{2,1,0:T(8,128)(2,1)S(1)} %collective-permute-done.2.refs_2_, ...), custom_call_target="tpu_custom_call" | custom-call | flops 838860800 | bytes 1638400 | tf_op jit(solution)/shard_map/attend_second/pallas_call | solution.py:341
  225.7 2.3 collective-permute-start.15
  227.9 5.2 %attend_second.6 = (bf16[2,320,128]{2,1,0:T(8,128)(2,1)S(1)}, bf16[2,320,128]{2,1,0:T(8,128)(2,1)S(1)}) custom-call(bf16[3,320,128]{2,1,0:T(8,128)(2,1)S(1)} %get-tuple-element.57.refs_0_, bf16[3,320,128]{2,1,0:T(8,128)(2,1)S(1)} %collective-permute-done.1.refs_1_, bf16[3,320,128]{2,1,0:T(8,128)(2,1)S(1)} %collective-permute-done.2.refs_2_, ...), custom_call_target="tpu_custom_call" | custom-call | flops 838860800 | bytes 1638400 | tf_op jit(solution)/shard_map/attend_second/pallas_call | solution.py:341
  233.1 1.5 collective-permute-start.17
  234.7 1.5 collective-permute-start.20
  236.1 5.2 %attend_second.7 = (bf16[2,320,128]{2,1,0:T(8,128)(2,1)S(1)}, bf16[2,320,128]{2,1,0:T(8,128)(2,1)S(1)}) custom-call(bf16[3,320,128]{2,1,0:T(8,128)(2,1)S(1)} %get-tuple-element.57.refs_0_, bf16[3,320,128]{2,1,0:T(8,128)(2,1)S(1)} %collective-permute-done.1.refs_1_, bf16[3,320,128]{2,1,0:T(8,128)(2,1)S(1)} %collective-permute-done.2.refs_2_, ...), custom_call_target="tpu_custom_call" | custom-call | flops 838860800 | bytes 1638400 | tf_op jit(solution)/shard_map/attend_second/pallas_call | solution.py:341
  241.4 0.0 collective-permute-done.16.refs_1_.refs_3_
  241.4 4.5 %collective-permute-start.18 = (bf16[2,320,128]{2,1,0:T(8,128)(2,1)S(1)}, bf16[2,320,128]{2,1,0:T(8,128)(2,1)S(1)}, u32[]{:S(2)}, u32[]{:S(2)}) collective-permute-start(bf16[2,320,128]{2,1,0:T(8,128)(2,1)S(1)} %get-tuple-element.101), channel_id=1, source_target_pairs={{0,4},{1,5},{2,6},{3,7},{4,0},{5,1},{6,2},{7,3},{8,12},{9,13},{10,... | collective-permute-start | bytes 491528 | tf_op jit(solution)/shard_map/ppermute | solution.py:254
  245.9 0.0 collective-permute-done.21.refs_0_.refs_8_
  245.9 2.0 collective-permute-start.19
  247.9 0.2 join.5
  248.1 0.5 collective-permute-start.23
  248.6 0.2 join.4
  248.8 3.2 %collective-permute-start.22 = (bf16[2,320,128]{2,1,0:T(8,128)(2,1)S(1)}, bf16[2,320,128]{2,1,0:T(8,128)(2,1)S(1)}, u32[]{:S(2)}, u32[]{:S(2)}) collective-permute-start(bf16[2,320,128]{2,1,0:T(8,128)(2,1)S(1)} %join.4), channel_id=1, source_target_pairs={{0,128},{8,136},{16,144},{24,152},{32,160},{40,168},{48,176},{56,1... | collective-permute-start | bytes 491528 | tf_op jit(solution)/shard_map/ppermute | solution.py:261
  252.0 0.2 join.6
  252.3 0.5 collective-permute-start.24
  252.7 2.1 collective-permute-done.18.refs_1_.refs_5_
  254.8 8.4 %collective-permute-done.19.refs_0_.refs_6_ = bf16[2,320,128]{2,1,0:T(8,128)(2,1)S(1)} collective-permute-done((bf16[2,320,128]{2,1,0:T(8,128)(2,1)S(1)}, bf16[2,320,128]{2,1,0:T(8,128)(2,1)S(1)}, u32[]{:S(2)}, u32[]{:S(2)}) %collective-permute-start.19) | collective-permute-done | bytes 163872 | tf_op jit(solution)/shard_map/ppermute | solution.py:254
  263.2 0.2 join.7
  263.5 0.1 collective-permute-start.25
  263.6 0.0 collective-permute-done.23.refs_10_
  263.6 6.8 %collective-permute-done.25.refs_12_ = bf16[2,320,128]{2,1,0:T(8,128)(2,1)S(1)} collective-permute-done((bf16[2,320,128]{2,1,0:T(8,128)(2,1)S(1)}, bf16[2,320,128]{2,1,0:T(8,128)(2,1)S(1)}, u32[]{:S(2)}, u32[]{:S(2)}) %collective-permute-start.25) | collective-permute-done | bytes 163872 | tf_op jit(solution)/shard_map/ppermute | solution.py:261
  270.4 2.1 final.1
  (19 shorter events, 0.0 us)
Async XLA Ops:
  62.2 92.0 %collective-permute-start = (bf16[3,320,1024]{2,1,0:T(8,128)(2,1)}, bf16[3,320,1024]{2,1,0:T(8,128)(2,1)}, u32[]{:S(2)}, u32[]{:S(2)}) collective-permute-start(bf16[3,320,1024]{2,1,0:T(8,128)(2,1)} %get-tuple-element.56), channel_id=1, source_target_pairs={{0,128},{8,136},{16,144},{24,152},{32,160},{40,168},{48,176},{56,1... | collective-permute-start | bytes 5898248 | tf_op jit(solution)/shard_map/ppermute | solution.py:261
  103.9 13.3 %collective-permute-start.4 = (bf16[3,320,128]{2,1,0:T(8,128)(2,1)}, bf16[3,320,128]{2,1,0:T(8,128)(2,1)S(1)}, u32[]{:S(2)}, u32[]{:S(2)}) collective-permute-start(bf16[3,320,128]{2,1,0:T(8,128)(2,1)} %get-tuple-element.62), channel_id=1, source_target_pairs={{0,1},{1,2},{2,3},{3,4},{4,5},{5,6},{6,7},{7,0},{8,9},{9,10},{10,1... | collective-permute-start | bytes 737288 | tf_op jit(solution)/shard_map/ppermute | solution.py:254
  105.9 27.7 %collective-permute-start.5 = (bf16[3,320,128]{2,1,0:T(8,128)(2,1)}, bf16[3,320,128]{2,1,0:T(8,128)(2,1)S(1)}, u32[]{:S(2)}, u32[]{:S(2)}) collective-permute-start(bf16[3,320,128]{2,1,0:T(8,128)(2,1)} %get-tuple-element.63), channel_id=1, source_target_pairs={{0,2},{1,3},{2,4},{3,5},{4,6},{5,7},{6,0},{7,1},{8,10},{9,11},{10,... | collective-permute-start | bytes 737288 | tf_op jit(solution)/shard_map/ppermute | solution.py:254
  110.4 31.9 %collective-permute-start.8 = (bf16[3,320,128]{2,1,0:T(8,128)(2,1)}, bf16[3,320,128]{2,1,0:T(8,128)(2,1)S(1)}, u32[]{:S(2)}, u32[]{:S(2)}) collective-permute-start(bf16[3,320,128]{2,1,0:T(8,128)(2,1)} %get-tuple-element.70), channel_id=1, source_target_pairs={{0,7},{1,0},{2,1},{3,2},{4,3},{5,4},{6,5},{7,6},{8,15},{9,8},{10,9... | collective-permute-start | bytes 737288 | tf_op jit(solution)/shard_map/ppermute | solution.py:254
  110.4 50.9 %collective-permute-start.10 = (bf16[3,320,128]{2,1,0:T(8,128)(2,1)}, bf16[3,320,128]{2,1,0:T(8,128)(2,1)S(1)}, u32[]{:S(2)}, u32[]{:S(2)}) collective-permute-start(bf16[3,320,128]{2,1,0:T(8,128)(2,1)} %get-tuple-element.74), channel_id=1, source_target_pairs={{0,6},{1,7},{2,0},{3,1},{4,2},{5,3},{6,4},{7,5},{8,14},{9,15},{10,... | collective-permute-start | bytes 737288 | tf_op jit(solution)/shard_map/ppermute | solution.py:254
  125.7 35.5 %collective-permute-start.6 = (bf16[3,320,128]{2,1,0:T(8,128)(2,1)}, bf16[3,320,128]{2,1,0:T(8,128)(2,1)S(1)}, u32[]{:S(2)}, u32[]{:S(2)}) collective-permute-start(bf16[3,320,128]{2,1,0:T(8,128)(2,1)} %pack_first.5), channel_id=1, source_target_pairs={{0,3},{1,4},{2,5},{3,6},{4,7},{5,0},{6,1},{7,2},{8,11},{9,12},{10,... | collective-permute-start | bytes 737288 | tf_op jit(solution)/shard_map/ppermute | solution.py:254
  142.2 12.0 %copy-start = (bf16[1,320,3072]{2,1,0:T(8,128)(2,1)S(1)}, bf16[1,320,3072]{2,1,0:T(8,128)(2,1)}, u32[]{:S(2)}) copy-start(bf16[1,320,3072]{2,1,0:T(8,128)(2,1)} %refs_0_.10) | copy-start | bytes 5898244
  142.2 21.9 %collective-permute-start.7 = (bf16[3,320,128]{2,1,0:T(8,128)(2,1)}, bf16[3,320,128]{2,1,0:T(8,128)(2,1)S(1)}, u32[]{:S(2)}, u32[]{:S(2)}) collective-permute-start(bf16[3,320,128]{2,1,0:T(8,128)(2,1)} %pack_first.6), channel_id=1, source_target_pairs={{0,4},{1,5},{2,6},{3,7},{4,0},{5,1},{6,2},{7,3},{8,12},{9,13},{10,... | collective-permute-start | bytes 737288 | tf_op jit(solution)/shard_map/ppermute | solution.py:254
  150.9 24.5 %collective-permute-start.9 = (bf16[3,320,128]{2,1,0:T(8,128)(2,1)}, bf16[3,320,128]{2,1,0:T(8,128)(2,1)S(1)}, u32[]{:S(2)}, u32[]{:S(2)}) collective-permute-start(bf16[3,320,128]{2,1,0:T(8,128)(2,1)} %pack_first.7), channel_id=1, source_target_pairs={{0,5},{1,6},{2,7},{3,0},{4,1},{5,2},{6,3},{7,4},{8,13},{9,14},{10,... | collective-permute-start | bytes 737288 | tf_op jit(solution)/shard_map/ppermute | solution.py:254
  154.2 1.5 copy-start.1
  155.7 1.5 copy-start.3
  157.3 25.0 %copy-start.6 = (bf16[3,320,128]{2,1,0:T(8,128)(2,1)S(1)}, bf16[3,320,128]{2,1,0:T(8,128)(2,1)}, u32[]{:S(2)}) copy-start(bf16[3,320,128]{2,1,0:T(8,128)(2,1)} %get-tuple-element.75.refs_0_) | copy-start | bytes 737284
  158.6 23.6 %collective-permute-start.1 = (bf16[3,320,128]{2,1,0:T(8,128)(2,1)S(1)}, bf16[3,320,128]{2,1,0:T(8,128)(2,1)S(1)}, u32[]{:S(2)}, u32[]{:S(2)}) collective-permute-start(bf16[3,320,128]{2,1,0:T(8,128)(2,1)S(1)} %get-tuple-element.58), channel_id=1, source_target_pairs={{0,1},{1,2},{2,3},{3,4},{4,5},{5,6},{6,7},{7,0},{8,9},{9,10},{10,1... | collective-permute-start | bytes 737288 | tf_op jit(solution)/shard_map/ppermute | solution.py:254
  161.2 36.0 %collective-permute-start.2 = (bf16[3,320,128]{2,1,0:T(8,128)(2,1)S(1)}, bf16[3,320,128]{2,1,0:T(8,128)(2,1)S(1)}, u32[]{:S(2)}, u32[]{:S(2)}) collective-permute-start(bf16[3,320,128]{2,1,0:T(8,128)(2,1)S(1)} %get-tuple-element.59), channel_id=1, source_target_pairs={{0,2},{1,3},{2,4},{3,5},{4,6},{5,7},{6,0},{7,1},{8,10},{9,11},{10,... | collective-permute-start | bytes 737288 | tf_op jit(solution)/shard_map/ppermute | solution.py:254
  161.3 40.7 %collective-permute-start.3 = (bf16[3,320,128]{2,1,0:T(8,128)(2,1)S(1)}, bf16[3,320,128]{2,1,0:T(8,128)(2,1)S(1)}, u32[]{:S(2)}, u32[]{:S(2)}) collective-permute-start(bf16[3,320,128]{2,1,0:T(8,128)(2,1)S(1)} %get-tuple-element.60), channel_id=1, source_target_pairs={{0,3},{1,4},{2,5},{3,6},{4,7},{5,0},{6,1},{7,2},{8,11},{9,12},{10,... | collective-permute-start | bytes 737288 | tf_op jit(solution)/shard_map/ppermute | solution.py:254
  164.1 37.9 %collective-permute-start.12 = (bf16[3,320,128]{2,1,0:T(8,128)(2,1)S(1)}, bf16[3,320,128]{2,1,0:T(8,128)(2,1)S(1)}, u32[]{:S(2)}, u32[]{:S(2)}) collective-permute-start(bf16[3,320,128]{2,1,0:T(8,128)(2,1)S(1)} %get-tuple-element.87), channel_id=1, source_target_pairs={{0,5},{1,6},{2,7},{3,0},{4,1},{5,2},{6,3},{7,4},{8,13},{9,14},{10,... | collective-permute-start | bytes 737288 | tf_op jit(solution)/shard_map/ppermute | solution.py:254
  175.4 26.6 %collective-permute-start.13 = (bf16[3,320,128]{2,1,0:T(8,128)(2,1)S(1)}, bf16[3,320,128]{2,1,0:T(8,128)(2,1)S(1)}, u32[]{:S(2)}, u32[]{:S(2)}) collective-permute-start(bf16[3,320,128]{2,1,0:T(8,128)(2,1)S(1)} %get-tuple-element.88), channel_id=1, source_target_pairs={{0,6},{1,7},{2,0},{3,1},{4,2},{5,3},{6,4},{7,5},{8,14},{9,15},{10,... | collective-permute-start | bytes 737288 | tf_op jit(solution)/shard_map/ppermute | solution.py:254
  182.2 19.8 %collective-permute-start.14 = (bf16[3,320,128]{2,1,0:T(8,128)(2,1)S(1)}, bf16[3,320,128]{2,1,0:T(8,128)(2,1)S(1)}, u32[]{:S(2)}, u32[]{:S(2)}) collective-permute-start(bf16[3,320,128]{2,1,0:T(8,128)(2,1)S(1)} %get-tuple-element.89), channel_id=1, source_target_pairs={{0,7},{1,0},{2,1},{3,2},{4,3},{5,4},{6,5},{7,6},{8,15},{9,8},{10,9... | collective-permute-start | bytes 737288 | tf_op jit(solution)/shard_map/ppermute | solution.py:254
  182.2 14.3 %copy-start.2 = (bf16[1,320,3072]{2,1,0:T(8,128)(2,1)S(1)}, bf16[1,320,3072]{2,1,0:T(8,128)(2,1)}, u32[]{:S(2)}) copy-start(bf16[1,320,3072]{2,1,0:T(8,128)(2,1)} %refs_1_.9) | copy-start | bytes 5898244
  182.2 14.3 %copy-start.4 = (bf16[1,320,3072]{2,1,0:T(8,128)(2,1)S(1)}, bf16[1,320,3072]{2,1,0:T(8,128)(2,1)}, u32[]{:S(2)}) copy-start(bf16[1,320,3072]{2,1,0:T(8,128)(2,1)} %refs_2_.9) | copy-start | bytes 5898244
  197.3 17.7 %collective-permute-start.11 = (bf16[3,320,128]{2,1,0:T(8,128)(2,1)S(1)}, bf16[3,320,128]{2,1,0:T(8,128)(2,1)S(1)}, u32[]{:S(2)}, u32[]{:S(2)}) collective-permute-start(bf16[3,320,128]{2,1,0:T(8,128)(2,1)S(1)} %pack_second.3), channel_id=1, source_target_pairs={{0,4},{1,5},{2,6},{3,7},{4,0},{5,1},{6,2},{7,3},{8,12},{9,13},{10,... | collective-permute-start | bytes 737288 | tf_op jit(solution)/shard_map/ppermute | solution.py:254
  220.2 21.1 %collective-permute-start.16 = (bf16[2,320,128]{2,1,0:T(8,128)(2,1)S(1)}, bf16[2,320,128]{2,1,0:T(8,128)(2,1)S(1)}, u32[]{:S(2)}, u32[]{:S(2)}) collective-permute-start(bf16[2,320,128]{2,1,0:T(8,128)(2,1)S(1)} %get-tuple-element.95), channel_id=1, source_target_pairs={{0,6},{1,7},{2,0},{3,1},{4,2},{5,3},{6,4},{7,5},{8,14},{9,15},{10,... | collective-permute-start | bytes 491528 | tf_op jit(solution)/shard_map/ppermute | solution.py:254
  220.3 25.5 %collective-permute-start.21 = (bf16[2,320,128]{2,1,0:T(8,128)(2,1)S(1)}, bf16[2,320,128]{2,1,0:T(8,128)(2,1)S(1)}, u32[]{:S(2)}, u32[]{:S(2)}) collective-permute-start(bf16[2,320,128]{2,1,0:T(8,128)(2,1)S(1)} %get-tuple-element.104), channel_id=1, source_target_pairs={{0,1},{1,2},{2,3},{3,4},{4,5},{5,6},{6,7},{7,0},{8,9},{9,10},{10,1... | collective-permute-start | bytes 491528 | tf_op jit(solution)/shard_map/ppermute | solution.py:254
  225.7 22.5 %collective-permute-start.15 = (bf16[2,320,128]{2,1,0:T(8,128)(2,1)S(1)}, bf16[2,320,128]{2,1,0:T(8,128)(2,1)S(1)}, u32[]{:S(2)}, u32[]{:S(2)}) collective-permute-start(bf16[2,320,128]{2,1,0:T(8,128)(2,1)S(1)} %get-tuple-element.92), channel_id=1, source_target_pairs={{0,7},{1,0},{2,1},{3,2},{4,3},{5,4},{6,5},{7,6},{8,15},{9,8},{10,9... | collective-permute-start | bytes 491528 | tf_op jit(solution)/shard_map/ppermute | solution.py:254
  233.1 15.7 %collective-permute-start.17 = (bf16[2,320,128]{2,1,0:T(8,128)(2,1)S(1)}, bf16[2,320,128]{2,1,0:T(8,128)(2,1)S(1)}, u32[]{:S(2)}, u32[]{:S(2)}) collective-permute-start(bf16[2,320,128]{2,1,0:T(8,128)(2,1)S(1)} %get-tuple-element.98), channel_id=1, source_target_pairs={{0,5},{1,6},{2,7},{3,0},{4,1},{5,2},{6,3},{7,4},{8,13},{9,14},{10,... | collective-permute-start | bytes 491528 | tf_op jit(solution)/shard_map/ppermute | solution.py:254
  234.7 17.4 %collective-permute-start.20 = (bf16[2,320,128]{2,1,0:T(8,128)(2,1)S(1)}, bf16[2,320,128]{2,1,0:T(8,128)(2,1)S(1)}, u32[]{:S(2)}, u32[]{:S(2)}) collective-permute-start(bf16[2,320,128]{2,1,0:T(8,128)(2,1)S(1)} %get-tuple-element.103), channel_id=1, source_target_pairs={{0,2},{1,3},{2,4},{3,5},{4,6},{5,7},{6,0},{7,1},{8,10},{9,11},{10,... | collective-permute-start | bytes 491528 | tf_op jit(solution)/shard_map/ppermute | solution.py:254
  236.1 34.2 %copy-start.5 = (bf16[1,320,3072]{2,1,0:T(8,128)(2,1)S(1)}, bf16[1,320,3072]{2,1,0:T(8,128)(2,1)}, u32[]{:S(2)}) copy-start(bf16[1,320,3072]{2,1,0:T(8,128)(2,1)} %refs_0_.11) | copy-start | bytes 5898244
  241.4 13.4 %collective-permute-start.18 = (bf16[2,320,128]{2,1,0:T(8,128)(2,1)S(1)}, bf16[2,320,128]{2,1,0:T(8,128)(2,1)S(1)}, u32[]{:S(2)}, u32[]{:S(2)}) collective-permute-start(bf16[2,320,128]{2,1,0:T(8,128)(2,1)S(1)} %get-tuple-element.101), channel_id=1, source_target_pairs={{0,4},{1,5},{2,6},{3,7},{4,0},{5,1},{6,2},{7,3},{8,12},{9,13},{10,... | collective-permute-start | bytes 491528 | tf_op jit(solution)/shard_map/ppermute | solution.py:254
  245.9 17.4 %collective-permute-start.19 = (bf16[2,320,128]{2,1,0:T(8,128)(2,1)S(1)}, bf16[2,320,128]{2,1,0:T(8,128)(2,1)S(1)}, u32[]{:S(2)}, u32[]{:S(2)}) collective-permute-start(bf16[2,320,128]{2,1,0:T(8,128)(2,1)S(1)} %get-tuple-element.102), channel_id=1, source_target_pairs={{0,3},{1,4},{2,5},{3,6},{4,7},{5,0},{6,1},{7,2},{8,11},{9,12},{10,... | collective-permute-start | bytes 491528 | tf_op jit(solution)/shard_map/ppermute | solution.py:254
  248.1 15.4 %collective-permute-start.23 = (bf16[2,320,128]{2,1,0:T(8,128)(2,1)S(1)}, bf16[2,320,128]{2,1,0:T(8,128)(2,1)S(1)}, u32[]{:S(2)}, u32[]{:S(2)}) collective-permute-start(bf16[2,320,128]{2,1,0:T(8,128)(2,1)S(1)} %join.5), channel_id=1, source_target_pairs={{0,128},{8,136},{16,144},{24,152},{32,160},{40,168},{48,176},{56,1... | collective-permute-start | bytes 491528 | tf_op jit(solution)/shard_map/ppermute | solution.py:261
  248.8 14.8 %collective-permute-start.22 = (bf16[2,320,128]{2,1,0:T(8,128)(2,1)S(1)}, bf16[2,320,128]{2,1,0:T(8,128)(2,1)S(1)}, u32[]{:S(2)}, u32[]{:S(2)}) collective-permute-start(bf16[2,320,128]{2,1,0:T(8,128)(2,1)S(1)} %join.4), channel_id=1, source_target_pairs={{0,128},{8,136},{16,144},{24,152},{32,160},{40,168},{48,176},{56,1... | collective-permute-start | bytes 491528 | tf_op jit(solution)/shard_map/ppermute | solution.py:261
  252.3 11.3 %collective-permute-start.24 = (bf16[2,320,128]{2,1,0:T(8,128)(2,1)S(1)}, bf16[2,320,128]{2,1,0:T(8,128)(2,1)S(1)}, u32[]{:S(2)}, u32[]{:S(2)}) collective-permute-start(bf16[2,320,128]{2,1,0:T(8,128)(2,1)S(1)} %join.6), channel_id=1, source_target_pairs={{0,128},{8,136},{16,144},{24,152},{32,160},{40,168},{48,176},{56,1... | collective-permute-start | bytes 491528 | tf_op jit(solution)/shard_map/ppermute | solution.py:261
  263.5 6.9 %collective-permute-start.25 = (bf16[2,320,128]{2,1,0:T(8,128)(2,1)S(1)}, bf16[2,320,128]{2,1,0:T(8,128)(2,1)S(1)}, u32[]{:S(2)}, u32[]{:S(2)}) collective-permute-start(bf16[2,320,128]{2,1,0:T(8,128)(2,1)S(1)} %join.7), channel_id=1, source_target_pairs={{0,128},{8,136},{16,144},{24,152},{32,160},{40,168},{48,176},{56,1... | collective-permute-start | bytes 491528 | tf_op jit(solution)/shard_map/ppermute | solution.py:261

commit v3 on v2

--- a/solution.py
+++ b/solution.py
@@ -14,6 +14,7 @@
 
 ANY = pl.BlockSpec(memory_space=pl.ANY)
 HBM = pl.BlockSpec(memory_space=pltpu.HBM)
+VMEM = pl.BlockSpec(memory_space=pltpu.VMEM)
 SMEM = pl.BlockSpec(memory_space=pltpu.SMEM)
 
 
@@ -38,15 +39,28 @@
         copy.wait()
 
 
+def run_staged(pairs):
+    for load, _ in pairs:
+        load.start()
+    for load, store in pairs:
+        load.wait()
+        store.start()
+    for _, store in pairs:
+        store.wait()
+
+
 def pack_kernel(pieces, offsets, *refs):
-    sources, outs, sems = refs[:3], refs[3:-1], refs[-1]
+    sources, outs, stage, sems, out_sems = refs[:3], refs[3:-3], refs[-3], refs[-2], refs[-1]
     me = lax.axis_index("seq")
-    run_copies(
+    run_staged(
         [
-            pltpu.make_async_copy(
-                sources[part].at[0, :, head_columns(me, offset, 0, pieces)],
-                outs[i].at[part],
-                sems.at[i, part],
+            (
+                pltpu.make_async_copy(
+                    sources[part].at[0, :, head_columns(me, offset, 0, pieces)],
+                    stage.at[i, part],
+                    sems.at[i, part],
+                ),
+                pltpu.make_async_copy(stage.at[i, part], outs[i].at[part], out_sems.at[i, part]),
             )
             for i, offset in enumerate(offsets)
             for part in range(3)
@@ -55,19 +69,22 @@
 
 
 def pack_far_kernel(width, assignment, timestep, plan, *refs):
-    sources, out, flag, sems = refs[:3], refs[3], refs[4], refs[5]
-    copies = [
-        pltpu.make_async_copy(
-            sources[part].at[0, :, pl.ds((GROUPS - 1) * width, width)], out.at[part], sems.at[part]
-        )
-        for part in range(3)
-    ]
-    for copy in copies:
-        copy.start()
+    sources, out, flag, stage, sems, out_sems = refs[:3], *refs[3:]
     request = assignment[lax.axis_index("batch")]
     flag[0] = plan[request, timestep[request]]
-    for copy in copies:
-        copy.wait()
+    run_staged(
+        [
+            (
+                pltpu.make_async_copy(
+                    sources[part].at[0, :, pl.ds((GROUPS - 1) * width, width)],
+                    stage.at[part],
+                    sems.at[part],
+                ),
+                pltpu.make_async_copy(stage.at[part], out.at[part], out_sems.at[part]),
+            )
+            for part in range(3)
+        ]
+    )
 
 
 def pack_second_kernel(pieces, offsets, flag, *refs):
@@ -153,62 +170,35 @@
             top = one(i, following, scores[i % 2], scores[(i + 1) % 2], top)
 
 
+def gather_rows(ins, rows, part, target):
+    for i, piece in enumerate(ins):
+        target[i * rows : (i + 1) * rows] = piece[part]
+
+
 def first_kernel(pieces, rows, *refs):
-    ins, outs = refs[:pieces], refs[pieces : 2 * pieces]
-    queries, keys, values, results, one_scores, other_scores, sems, out_sems = refs[2 * pieces :]
-    run_copies(
-        [
-            pltpu.make_async_copy(
-                ins[i].at[part], (queries, keys, values)[part].at[pl.ds(i * rows, rows)], sems.at[part, i]
-            )
-            for part in range(3)
-            for i in range(pieces)
-        ]
-    )
+    ins, results = refs[:pieces], refs[pieces]
+    queries, keys, values, one_scores, other_scores = refs[pieces + 1 :]
+    for part, target in enumerate((queries, keys, values)):
+        gather_rows(ins, rows, part, target)
     attend(queries, keys, values, results, (one_scores, other_scores), rows, True)
-    run_copies(
-        [
-            pltpu.make_async_copy(results.at[pl.ds(i * rows, rows)], outs[i], out_sems.at[i])
-            for i in range(pieces)
-        ]
-    )
-
-
-def second_kernel(pieces, rows, offsets, *refs):
-    count = len(offsets)
-    ins, refs = refs[:pieces], refs[pieces:]
-    earlier, outs, refs = refs[:count], refs[count : 2 * count], refs[2 * count :]
-    queries, keys, values, results, one_scores, other_scores, sems, query_sems, out_sems = refs
-    forwarded = [
-        pltpu.make_async_copy(earlier[i], outs[i].at[0], out_sems.at[0, i]) for i in range(count)
-    ]
-    fetch = [
-        pltpu.make_async_copy(
-            ins[i].at[1 + part], (keys, values)[part].at[pl.ds(i * rows, rows)], sems.at[part, i]
-        )
-        for part in range(2)
-        for i in range(pieces)
-    ] + [
-        pltpu.make_async_copy(ins[offset].at[0], queries.at[pl.ds(i * rows, rows)], query_sems.at[i])
-        for i, offset in enumerate(offsets)
-    ]
-    for copy in forwarded:
-        copy.start()
-    run_copies(fetch)
+
+
+def second_kernel(pieces, rows, positions, *refs):
+    count = len(positions)
+    ins, earlier, outs = refs[:pieces], refs[pieces], refs[pieces + 1 : pieces + 1 + count]
+    queries, keys, values, results, one_scores, other_scores = refs[pieces + 1 + count :]
+    gather_rows(ins, rows, 1, keys)
+    gather_rows(ins, rows, 2, values)
+    gather_rows([ins[p] for p in positions], rows, 0, queries)
     attend(queries, keys, values, results, (one_scores, other_scores), rows, False)
-    run_copies(
-        [
-            pltpu.make_async_copy(results.at[pl.ds(i * rows, rows)], outs[i].at[1], out_sems.at[1, i])
-            for i in range(count)
-        ]
-    )
-    for copy in forwarded:
-        copy.wait()
+    for i, position in enumerate(positions):
+        outs[i][0] = earlier[position * rows : (position + 1) * rows]
+        outs[i][1] = results[i * rows : (i + 1) * rows]
 
 
 def join_kernel(count, *refs):
-    ins, out, sems = refs[:count], refs[count], refs[count + 1]
-    run_copies([pltpu.make_async_copy(ins[i].at[1], out.at[i], sems.at[i]) for i in range(count)])
+    for i in range(count):
+        refs[count][i] = refs[i][1]
 
 
 def final_kernel(pieces, chunks, flag, *refs):
@@ -276,7 +266,7 @@
         out_shape=(shape(3, rows, group_width), jax.ShapeDtypeStruct((1,), jnp.int32)),
         in_specs=[SMEM] * 3 + [HBM] * 3,
         out_specs=(ANY, SMEM),
-        scratch_shapes=[dma((3,))],
+        scratch_shapes=[pltpu.VMEM((3, rows, group_width), kind), dma((3,)), dma((3,))],
         name="pack_far",
     )(assignment, timestep, plan, *sources)
     far_in = across(far_out)
@@ -290,7 +280,11 @@
             out_shape=[shape(3, rows, HEAD_DIM)] * len(offsets),
             in_specs=[HBM] * 3,
             out_specs=[ANY] * len(offsets),
-            scratch_shapes=[dma((len(offsets), 3))],
+            scratch_shapes=[
+                pltpu.VMEM((len(offsets), 3, rows, HEAD_DIM), kind),
+                dma((len(offsets), 3)),
+                dma((len(offsets), 3)),
+            ],
             name="pack_first",
         )(*sources)
 
@@ -318,20 +312,19 @@
     for offset, value in zip(early, pack_second(early, sources)):
         second_in[offset] = forward(value, offset)
 
+    score_buffers = [pltpu.VMEM((rows, pieces * rows), jnp.float32)] * 2
     first_result = pl.pallas_call(
         functools.partial(first_kernel, pieces, rows),
-        out_shape=[shape(rows, HEAD_DIM)] * pieces,
-        in_specs=[ANY] * pieces,
-        out_specs=[ANY] * pieces,
-        scratch_shapes=[pltpu.VMEM((pieces * rows, HEAD_DIM), kind)] * 4
-        + [pltpu.VMEM((rows, pieces * rows), jnp.float32)] * 2
-        + [dma((3, pieces)), dma((pieces,))],
+        out_shape=shape(pieces * rows, HEAD_DIM),
+        in_specs=[VMEM] * pieces,
+        out_specs=VMEM,
+        scratch_shapes=[pltpu.VMEM((pieces * rows, HEAD_DIM), kind)] * 3 + score_buffers,
+        compiler_params=SHARED,
         cost_estimate=cost(pieces),
-        compiler_params=SHARED,
         name="attend_first",
     )(*ordered(first_in, second_in[order[1]]))
 
-    for offset, value in zip(late, pack_second(late, ordered(sources, first_result[0]))):
+    for offset, value in zip(late, pack_second(late, ordered(sources, first_result))):
         second_in[offset] = forward(value, offset)
 
     count = 2
@@ -341,23 +334,19 @@
         results = pl.pallas_call(
             functools.partial(second_kernel, pieces, rows, offsets),
             out_shape=[shape(2, rows, HEAD_DIM)] * count,
-            in_specs=[ANY] * (pieces + count),
-            out_specs=[ANY] * count,
+            in_specs=[VMEM] * (pieces + 1),
+            out_specs=[VMEM] * count,
             scratch_shapes=[
                 pltpu.VMEM((count * rows, HEAD_DIM), kind),
                 pltpu.VMEM((pieces * rows, HEAD_DIM), kind),
                 pltpu.VMEM((pieces * rows, HEAD_DIM), kind),
                 pltpu.VMEM((count * rows, HEAD_DIM), kind),
-                pltpu.VMEM((rows, pieces * rows), jnp.float32),
-                pltpu.VMEM((rows, pieces * rows), jnp.float32),
-                dma((2, pieces)),
-                dma((count,)),
-                dma((2, count)),
+                *score_buffers,
             ],
+            compiler_params=SHARED,
             cost_estimate=cost(count),
-            compiler_params=SHARED,
             name="attend_second",
-        )(*second_in, *[first_result[offset] for offset in offsets])
+        )(*second_in, first_result)
         for offset, value in zip(offsets, results):
             back[offset] = backward(value, offset)
 
@@ -366,9 +355,8 @@
         joined = pl.pallas_call(
             functools.partial(join_kernel, count),
             out_shape=shape(count, rows, HEAD_DIM),
-            in_specs=[ANY] * count,
-            out_specs=ANY,
-            scratch_shapes=[dma((count,))],
+            in_specs=[VMEM] * count,
+            out_specs=VMEM,
             compiler_params=SHARED,
             name="join",
         )(*[back[offset] for offset in offsets])

time: 273 us -> 160 us (0.59)
  Pallas kernels: 167 us -> 38.9 us
  starting transfers between devices: 56.1 us -> 70.5 us
    pallas_call x1, Pallas kernels: 62.1 us -> 3.86 us  [body(): pl.pallas_call(functools.partial(pack_far_kernel, group_width), out_shape...]
    pallas_call x4, Pallas kernels: 64.2 us -> 7.27 us  [pack_first(): pl.pallas_call(functools.partial(pack_kernel, pieces, offsets), out_shape...]
    ppermute x21, starting transfers between devices: 48.6 us -> 59.9 us  [forward(): lax.ppermute(value, 'seq', [(s, (s + offset) % pieces) for s in range(pie...]
    ppermute x21, waiting for transfers between devices: 39.6 us -> 29.4 us  [forward(): lax.ppermute(value, 'seq', [(s, (s + offset) % pieces) for s in range(pie...]
    ppermute x5, waiting for transfers between devices: 6.79 us -> 16.8 us  [across(): return lax.ppermute(value, 'batch', [(s, s ^ mask) for s in range(slots)])]
    pallas_call x4, Pallas kernels: 20.9 us -> 11.1 us  [body(): pl.pallas_call(functools.partial(second_kernel, pieces, rows, offsets), o...]
    pallas_call x1, Pallas kernels: 14.3 us -> 10.6 us  [body(): pl.pallas_call(functools.partial(first_kernel, pieces, rows), out_shape=s...]
    ppermute x5, starting transfers between devices: 7.56 us -> 10.6 us  [across(): return lax.ppermute(value, 'batch', [(s, s ^ mask) for s in range(slots)])]
  transfers between devices with their start and end apart: 26 -> 26, of which waited for: 7 -> 12; matrix products, arithmetic and copies ran while one was open for 0% -> 0% of each run, Pallas kernels for 36% -> 19%
where the time goes in v3:
time: 160 us; the launch traced here: 159 us
  starting transfers between devices  70.5 us (44%)
  waiting for transfers between devices  46.1 us (29%)
  Pallas kernels  38.9 us (24%)
  local copies, waits for them, and re-layouts  3.11 us (2%)
    ppermute x21, starting transfers between devices, forward(): lax.ppermute(value, 'seq', [(s, (s + offset) % pieces) for s in range(pie...  59.9 us
    ppermute x21, waiting for transfers between devices, forward(): lax.ppermute(value, 'seq', [(s, (s + offset) % pieces) for s in range(pie...  29.4 us
    ppermute x5, waiting for transfers between devices, across(): return lax.ppermute(value, 'batch', [(s, s ^ mask) for s in range(slots)])  16.8 us
    pallas_call x4, Pallas kernels, body(): pl.pallas_call(functools.partial(second_kernel, pieces, rows, offsets), o...  11.1 us
    ppermute x5, starting transfers between devices, across(): return lax.ppermute(value, 'batch', [(s, s ^ mask) for s in range(slots)])  10.6 us
    pallas_call x1, Pallas kernels, body(): pl.pallas_call(functools.partial(first_kernel, pieces, rows), out_shape=s...  10.6 us
    pallas_call x4, Pallas kernels, pack_first(): pl.pallas_call(functools.partial(pack_kernel, pieces, offsets), out_shape...  7.27 us
    pallas_call x2, Pallas kernels, pack_second(): pl.pallas_call(functools.partial(pack_second_kernel, pieces, offsets), ou...  3.94 us
  transfers between devices with their start and end apart: 26, of which 12 were waited for; matrix products, arithmetic and copies ran while one was open for 0% of the time, Pallas kernels for 19%

profile of v3, /device:TPU:34, one launch (start us, length us, event | category | flops | bytes accessed | tf_op | source)
XLA Modules:
  0.0 159.0 jit_solution(12735703131463658884)
XLA Ops:
  0.0 3.9 %pack_far.1 = (bf16[3,320,1024]{2,1,0:T(8,128)(2,1)}, s32[1]{0:T(128)}) custom-call(s32[32]{0:T(128)} %assignment.1, s32[32]{0:T(128)} %timestep.1, s32[32,28]{1,0:T(8,128)} %plan.1, bf16[1,320,3072]{2,1,0:T(8,128)(2,1)} %refs_0_.10, bf16[1,320,3072]{2,1,0:T(8,128)(2,1)} %refs_1_.9, bf16[1,320,3072]{2,1,0:T(8,128)(2,1)} %refs_2_.9), custom_call_target="tpu_custom_call" | custom-call | tf_op jit(solution)/shard_map/pack_far/pallas_call | solution.py:264
  3.9 3.3 %collective-permute-start = (bf16[3,320,1024]{2,1,0:T(8,128)(2,1)}, bf16[3,320,1024]{2,1,0:T(8,128)(2,1)}, u32[]{:S(2)}, u32[]{:S(2)}) collective-permute-start(bf16[3,320,1024]{2,1,0:T(8,128)(2,1)} %get-tuple-element.48), channel_id=1, source_target_pairs={{0,128},{8,136},{16,144},{24,152},{32,160},{40,168},{48,176},{56,1... | collective-permute-start | bytes 5898248 | tf_op jit(solution)/shard_map/ppermute | solution.py:251
  7.2 2.3 %pack_first.4 = (bf16[3,320,128]{2,1,0:T(8,128)(2,1)}, bf16[3,320,128]{2,1,0:T(8,128)(2,1)}, bf16[3,320,128]{2,1,0:T(8,128)(2,1)}, bf16[3,320,128]{2,1,0:T(8,128)(2,1)}, bf16[3,320,128]{2,1,0:T(8,128)(2,1)}) custom-call(bf16[1,320,3072]{2,1,0:T(8,128)(2,1)} %refs_0_.10, bf16[1,320,3072]{2,1,0:T(8,128)(2,1)} %refs_1_.9, bf16[1,320,3072]{2,1,0:T(8,128)(2,1)} %refs_2_.9), custom_call_target="tpu_custom_call" | custom-call | tf_op jit(solution)/shard_map/pack_first/pallas_call | solution.py:278
  9.5 2.0 %collective-permute-start.4 = (bf16[3,320,128]{2,1,0:T(8,128)(2,1)}, bf16[3,320,128]{2,1,0:T(8,128)(2,1)S(1)}, u32[]{:S(2)}, u32[]{:S(2)}) collective-permute-start(bf16[3,320,128]{2,1,0:T(8,128)(2,1)} %get-tuple-element.54), channel_id=1, source_target_pairs={{0,1},{1,2},{2,3},{3,4},{4,5},{5,6},{6,7},{7,0},{8,9},{9,10},{10,1... | collective-permute-start | bytes 737288 | tf_op jit(solution)/shard_map/ppermute | solution.py:244
  11.5 4.5 %collective-permute-start.5 = (bf16[3,320,128]{2,1,0:T(8,128)(2,1)}, bf16[3,320,128]{2,1,0:T(8,128)(2,1)S(1)}, u32[]{:S(2)}, u32[]{:S(2)}) collective-permute-start(bf16[3,320,128]{2,1,0:T(8,128)(2,1)} %get-tuple-element.55), channel_id=1, source_target_pairs={{0,2},{1,3},{2,4},{3,5},{4,6},{5,7},{6,0},{7,1},{8,10},{9,11},{10,... | collective-permute-start | bytes 737288 | tf_op jit(solution)/shard_map/ppermute | solution.py:244
  15.9 0.0 collective-permute-start.8
  15.9 1.0 collective-permute-start.10
  17.0 5.8 %collective-permute-done.4.refs_1_ = bf16[3,320,128]{2,1,0:T(8,128)(2,1)S(1)} collective-permute-done((bf16[3,320,128]{2,1,0:T(8,128)(2,1)}, bf16[3,320,128]{2,1,0:T(8,128)(2,1)S(1)}, u32[]{:S(2)}, u32[]{:S(2)}) %collective-permute-start.4) | collective-permute-done | bytes 245792 | tf_op jit(solution)/shard_map/ppermute | solution.py:244
  22.7 1.7 %pack_first.5 = bf16[3,320,128]{2,1,0:T(8,128)(2,1)} custom-call(bf16[1,320,3072]{2,1,0:T(8,128)(2,1)} %refs_0_.10, bf16[1,320,3072]{2,1,0:T(8,128)(2,1)} %refs_1_.9, bf16[1,320,3072]{2,1,0:T(8,128)(2,1)} %refs_2_.9), custom_call_target="tpu_custom_call" | custom-call | tf_op jit(solution)/shard_map/pack_first/pallas_call | solution.py:278
  24.4 7.8 %collective-permute-start.6 = (bf16[3,320,128]{2,1,0:T(8,128)(2,1)}, bf16[3,320,128]{2,1,0:T(8,128)(2,1)S(1)}, u32[]{:S(2)}, u32[]{:S(2)}) collective-permute-start(bf16[3,320,128]{2,1,0:T(8,128)(2,1)} %pack_first.5), channel_id=1, source_target_pairs={{0,3},{1,4},{2,5},{3,6},{4,7},{5,0},{6,1},{7,2},{8,11},{9,12},{10,... | collective-permute-start | bytes 737288 | tf_op jit(solution)/shard_map/ppermute | solution.py:244
  32.2 1.0 collective-permute-done.5.refs_2_
  33.2 1.7 %pack_first.6 = bf16[3,320,128]{2,1,0:T(8,128)(2,1)} custom-call(bf16[1,320,3072]{2,1,0:T(8,128)(2,1)} %refs_0_.10, bf16[1,320,3072]{2,1,0:T(8,128)(2,1)} %refs_1_.9, bf16[1,320,3072]{2,1,0:T(8,128)(2,1)} %refs_2_.9), custom_call_target="tpu_custom_call" | custom-call | tf_op jit(solution)/shard_map/pack_first/pallas_call | solution.py:278
  34.9 0.0 copy-start
  34.9 7.5 %collective-permute-start.7 = (bf16[3,320,128]{2,1,0:T(8,128)(2,1)}, bf16[3,320,128]{2,1,0:T(8,128)(2,1)S(1)}, u32[]{:S(2)}, u32[]{:S(2)}) collective-permute-start(bf16[3,320,128]{2,1,0:T(8,128)(2,1)} %pack_first.6), channel_id=1, source_target_pairs={{0,4},{1,5},{2,6},{3,7},{4,0},{5,1},{6,2},{7,3},{8,12},{9,13},{10,... | collective-permute-start | bytes 737288 | tf_op jit(solution)/shard_map/ppermute | solution.py:244
  42.4 0.0 collective-permute-done.8.refs_7_
  42.4 1.7 %pack_first.7 = bf16[3,320,128]{2,1,0:T(8,128)(2,1)} custom-call(bf16[1,320,3072]{2,1,0:T(8,128)(2,1)} %refs_0_.10, bf16[1,320,3072]{2,1,0:T(8,128)(2,1)} %refs_1_.9, bf16[1,320,3072]{2,1,0:T(8,128)(2,1)} %refs_2_.9), custom_call_target="tpu_custom_call" | custom-call | tf_op jit(solution)/shard_map/pack_first/pallas_call | solution.py:278
  44.1 0.1 collective-permute-start.9
  44.2 6.1 %collective-permute-done.refs_3_ = bf16[3,320,1024]{2,1,0:T(8,128)(2,1)} collective-permute-done((bf16[3,320,1024]{2,1,0:T(8,128)(2,1)}, bf16[3,320,1024]{2,1,0:T(8,128)(2,1)}, u32[]{:S(2)}, u32[]{:S(2)}) %collective-permute-start) | collective-permute-done | bytes 1966112 | tf_op jit(solution)/shard_map/ppermute | solution.py:251
  50.3 1.5 copy-done.1
  51.9 1.5 copy-done.3
  53.4 2.4 %pack_second.2 = (bf16[3,320,128]{2,1,0:T(8,128)(2,1)S(1)}, bf16[3,320,128]{2,1,0:T(8,128)(2,1)S(1)}, bf16[3,320,128]{2,1,0:T(8,128)(2,1)S(1)}, bf16[3,320,128]{...) custom-call(s32[1]{0:T(128)} %get-tuple-element.47.flag, ...), custom_call_target="tpu_custom_call" | custom-call | tf_op jit(solution)/shard_map/pack_second/pallas_call | solution.py:292
  55.8 2.0 %collective-permute-start.1 = (bf16[3,320,128]{2,1,0:T(8,128)(2,1)S(1)}, bf16[3,320,128]{2,1,0:T(8,128)(2,1)S(1)}, u32[]{:S(2)}, u32[]{:S(2)}) collective-permute-start(bf16[3,320,128]{2,1,0:T(8,128)(2,1)S(1)} %get-tuple-element.50), channel_id=1, source_target_pairs={{0,1},{1,2},{2,3},{3,4},{4,5},{5,6},{6,7},{7,0},{8,9},{9,10},{10,1... | collective-permute-start | bytes 737288 | tf_op jit(solution)/shard_map/ppermute | solution.py:244
  57.8 0.0 collective-permute-done.10.refs_6_
  57.8 4.5 %collective-permute-start.2 = (bf16[3,320,128]{2,1,0:T(8,128)(2,1)S(1)}, bf16[3,320,128]{2,1,0:T(8,128)(2,1)S(1)}, u32[]{:S(2)}, u32[]{:S(2)}) collective-permute-start(bf16[3,320,128]{2,1,0:T(8,128)(2,1)S(1)} %get-tuple-element.51), channel_id=1, source_target_pairs={{0,2},{1,3},{2,4},{3,5},{4,6},{5,7},{6,0},{7,1},{8,10},{9,11},{10,... | collective-permute-start | bytes 737288 | tf_op jit(solution)/shard_map/ppermute | solution.py:244
  62.3 0.0 collective-permute-done.6.refs_3_
  62.3 1.9 %collective-permute-start.3 = (bf16[3,320,128]{2,1,0:T(8,128)(2,1)S(1)}, bf16[3,320,128]{2,1,0:T(8,128)(2,1)S(1)}, u32[]{:S(2)}, u32[]{:S(2)}) collective-permute-start(bf16[3,320,128]{2,1,0:T(8,128)(2,1)S(1)} %get-tuple-element.52), channel_id=1, source_target_pairs={{0,3},{1,4},{2,5},{3,6},{4,7},{5,0},{6,1},{7,2},{8,11},{9,12},{10,... | collective-permute-start | bytes 737288 | tf_op jit(solution)/shard_map/ppermute | solution.py:244
  64.2 0.0 collective-permute-done.7.refs_4_
  64.2 3.1 %collective-permute-start.12 = (bf16[3,320,128]{2,1,0:T(8,128)(2,1)S(1)}, bf16[3,320,128]{2,1,0:T(8,128)(2,1)S(1)}, u32[]{:S(2)}, u32[]{:S(2)}) collective-permute-start(bf16[3,320,128]{2,1,0:T(8,128)(2,1)S(1)} %get-tuple-element.78), channel_id=1, source_target_pairs={{0,5},{1,6},{2,7},{3,0},{4,1},{5,2},{6,3},{7,4},{8,13},{9,14},{10,... | collective-permute-start | bytes 737288 | tf_op jit(solution)/shard_map/ppermute | solution.py:244
  67.3 0.0 collective-permute-done.9.refs_5_
  67.3 1.0 collective-permute-start.13
  68.3 2.0 %collective-permute-start.14 = (bf16[3,320,128]{2,1,0:T(8,128)(2,1)S(1)}, bf16[3,320,128]{2,1,0:T(8,128)(2,1)S(1)}, u32[]{:S(2)}, u32[]{:S(2)}) collective-permute-start(bf16[3,320,128]{2,1,0:T(8,128)(2,1)S(1)} %get-tuple-element.80), channel_id=1, source_target_pairs={{0,7},{1,0},{2,1},{3,2},{4,3},{5,4},{6,5},{7,6},{8,15},{9,8},{10,9... | collective-permute-start | bytes 737288 | tf_op jit(solution)/shard_map/ppermute | solution.py:244
  70.3 10.6 %attend_first.1.refs_8_ = bf16[2560,128]{1,0:T(8,128)(2,1)S(1)} custom-call(bf16[3,320,128]{2,1,0:T(8,128)(2,1)S(1)} %copy-done.6, bf16[3,320,128]{2,1,0:T(8,128)(2,1)S(1)} %collective-permute-done.4.refs_1_, bf16[3,320,128]{2,1,0:T(8,128)(2,1)S(1)} %collective-permute-done.5.refs_2_, bf16[3,320,128]{2,1,0:T(8,128)(2,1)S(1)} %collective-permute-done.6.refs_3_, ...), custom_call_target="tpu_custom_call" | custom-call | flops 3355443200 | bytes 2621440 | tf_op jit(solution)/shard_map/attend_first/pallas_call | solution.py:316
  80.9 1.6 pack_second.3
  82.5 0.0 collective-permute-done.2.refs_2_
  82.5 8.6 %collective-permute-start.11 = (bf16[3,320,128]{2,1,0:T(8,128)(2,1)S(1)}, bf16[3,320,128]{2,1,0:T(8,128)(2,1)S(1)}, u32[]{:S(2)}, u32[]{:S(2)}) collective-permute-start(bf16[3,320,128]{2,1,0:T(8,128)(2,1)S(1)} %pack_second.3), channel_id=1, source_target_pairs={{0,4},{1,5},{2,6},{3,7},{4,0},{5,1},{6,2},{7,3},{8,12},{9,13},{10,... | collective-permute-start | bytes 737288 | tf_op jit(solution)/shard_map/ppermute | solution.py:244
  91.1 10.2 %collective-permute-done.3.refs_3_ = bf16[3,320,128]{2,1,0:T(8,128)(2,1)S(1)} collective-permute-done((bf16[3,320,128]{2,1,0:T(8,128)(2,1)S(1)}, bf16[3,320,128]{2,1,0:T(8,128)(2,1)S(1)}, u32[]{:S(2)}, u32[]{:S(2)}) %collective-permute-start.3) | collective-permute-done | bytes 245792 | tf_op jit(solution)/shard_map/ppermute | solution.py:244
  101.2 2.1 %collective-permute-done.14.refs_7_ = bf16[3,320,128]{2,1,0:T(8,128)(2,1)S(1)} collective-permute-done((bf16[3,320,128]{2,1,0:T(8,128)(2,1)S(1)}, bf16[3,320,128]{2,1,0:T(8,128)(2,1)S(1)}, u32[]{:S(2)}, u32[]{:S(2)}) %collective-permute-start.14) | collective-permute-done | bytes 245792 | tf_op jit(solution)/shard_map/ppermute | solution.py:244
  103.4 6.5 %collective-permute-done.11.refs_4_ = bf16[3,320,128]{2,1,0:T(8,128)(2,1)S(1)} collective-permute-done((bf16[3,320,128]{2,1,0:T(8,128)(2,1)S(1)}, bf16[3,320,128]{2,1,0:T(8,128)(2,1)S(1)}, u32[]{:S(2)}, u32[]{:S(2)}) %collective-permute-start.11) | collective-permute-done | bytes 245792 | tf_op jit(solution)/shard_map/ppermute | solution.py:244
  109.8 2.8 %attend_second.7 = (bf16[2,320,128]{2,1,0:T(8,128)(2,1)S(1)}, bf16[2,320,128]{2,1,0:T(8,128)(2,1)S(1)}) custom-call(bf16[3,320,128]{2,1,0:T(8,128)(2,1)S(1)} %get-tuple-element.49.refs_0_, bf16[3,320,128]{2,1,0:T(8,128)(2,1)S(1)} %collective-permute-done.1.refs_1_, bf16[3,320,128]{2,1,0:T(8,128)(2,1)S(1)} %collective-permute-done.2.refs_2_, ...), custom_call_target="tpu_custom_call" | custom-call | flops 838860800 | bytes 1638400 | tf_op jit(solution)/shard_map/attend_second/pallas_call | solution.py:334
  112.6 4.1 %collective-permute-start.18 = (bf16[2,320,128]{2,1,0:T(8,128)(2,1)S(1)}, bf16[2,320,128]{2,1,0:T(8,128)(2,1)S(1)}, u32[]{:S(2)}, u32[]{:S(2)}) collective-permute-start(bf16[2,320,128]{2,1,0:T(8,128)(2,1)S(1)} %get-tuple-element.85), channel_id=1, source_target_pairs={{0,4},{1,5},{2,6},{3,7},{4,0},{5,1},{6,2},{7,3},{8,12},{9,13},{10,... | collective-permute-start | bytes 491528 | tf_op jit(solution)/shard_map/ppermute | solution.py:244
  116.7 0.0 collective-permute-start.19
  116.7 2.8 %attend_second.6 = (bf16[2,320,128]{2,1,0:T(8,128)(2,1)S(1)}, bf16[2,320,128]{2,1,0:T(8,128)(2,1)S(1)}) custom-call(bf16[3,320,128]{2,1,0:T(8,128)(2,1)S(1)} %get-tuple-element.49.refs_0_, bf16[3,320,128]{2,1,0:T(8,128)(2,1)S(1)} %collective-permute-done.1.refs_1_, bf16[3,320,128]{2,1,0:T(8,128)(2,1)S(1)} %collective-permute-done.2.refs_2_, ...), custom_call_target="tpu_custom_call" | custom-call | flops 838860800 | bytes 1638400 | tf_op jit(solution)/shard_map/attend_second/pallas_call | solution.py:334
  119.5 5.1 %collective-permute-start.17 = (bf16[2,320,128]{2,1,0:T(8,128)(2,1)S(1)}, bf16[2,320,128]{2,1,0:T(8,128)(2,1)S(1)}, u32[]{:S(2)}, u32[]{:S(2)}) collective-permute-start(bf16[2,320,128]{2,1,0:T(8,128)(2,1)S(1)} %get-tuple-element.84), channel_id=1, source_target_pairs={{0,5},{1,6},{2,7},{3,0},{4,1},{5,2},{6,3},{7,4},{8,13},{9,14},{10,... | collective-permute-start | bytes 491528 | tf_op jit(solution)/shard_map/ppermute | solution.py:244
  124.6 0.0 collective-permute-start.20
  124.6 2.8 %attend_second.5 = (bf16[2,320,128]{2,1,0:T(8,128)(2,1)S(1)}, bf16[2,320,128]{2,1,0:T(8,128)(2,1)S(1)}) custom-call(bf16[3,320,128]{2,1,0:T(8,128)(2,1)S(1)} %get-tuple-element.49.refs_0_, bf16[3,320,128]{2,1,0:T(8,128)(2,1)S(1)} %collective-permute-done.1.refs_1_, bf16[3,320,128]{2,1,0:T(8,128)(2,1)S(1)} %collective-permute-done.2.refs_2_, ...), custom_call_target="tpu_custom_call" | custom-call | flops 838860800 | bytes 1638400 | tf_op jit(solution)/shard_map/attend_second/pallas_call | solution.py:334
  127.4 0.0 copy-start.5
  127.4 4.2 %collective-permute-start.16 = (bf16[2,320,128]{2,1,0:T(8,128)(2,1)S(1)}, bf16[2,320,128]{2,1,0:T(8,128)(2,1)S(1)}, u32[]{:S(2)}, u32[]{:S(2)}) collective-permute-start(bf16[2,320,128]{2,1,0:T(8,128)(2,1)S(1)} %get-tuple-element.83), channel_id=1, source_target_pairs={{0,6},{1,7},{2,0},{3,1},{4,2},{5,3},{6,4},{7,5},{8,14},{9,15},{10,... | collective-permute-start | bytes 491528 | tf_op jit(solution)/shard_map/ppermute | solution.py:244
  131.6 2.8 %attend_second.4 = (bf16[2,320,128]{2,1,0:T(8,128)(2,1)S(1)}, bf16[2,320,128]{2,1,0:T(8,128)(2,1)S(1)}) custom-call(bf16[3,320,128]{2,1,0:T(8,128)(2,1)S(1)} %get-tuple-element.49.refs_0_, bf16[3,320,128]{2,1,0:T(8,128)(2,1)S(1)} %collective-permute-done.1.refs_1_, bf16[3,320,128]{2,1,0:T(8,128)(2,1)S(1)} %collective-permute-done.2.refs_2_, ...), custom_call_target="tpu_custom_call" | custom-call | flops 838860800 | bytes 1638400 | tf_op jit(solution)/shard_map/attend_second/pallas_call | solution.py:334
  134.4 0.0 collective-permute-done.18.refs_1_.refs_5_
  134.4 0.1 collective-permute-start.21
  134.5 1.6 %collective-permute-done.19.refs_0_.refs_6_ = bf16[2,320,128]{2,1,0:T(8,128)(2,1)S(1)} collective-permute-done((bf16[2,320,128]{2,1,0:T(8,128)(2,1)S(1)}, bf16[2,320,128]{2,1,0:T(8,128)(2,1)S(1)}, u32[]{:S(2)}, u32[]{:S(2)}) %collective-permute-start.19) | collective-permute-done | bytes 163872 | tf_op jit(solution)/shard_map/ppermute | solution.py:244
  136.1 0.4 collective-permute-start.15
  136.5 2.2 %collective-permute-done.17.refs_1_.refs_4_ = bf16[2,320,128]{2,1,0:T(8,128)(2,1)S(1)} collective-permute-done((bf16[2,320,128]{2,1,0:T(8,128)(2,1)S(1)}, bf16[2,320,128]{2,1,0:T(8,128)(2,1)S(1)}, u32[]{:S(2)}, u32[]{:S(2)}) %collective-permute-start.17) | collective-permute-done | bytes 163872 | tf_op jit(solution)/shard_map/ppermute | solution.py:244
  138.7 1.2 collective-permute-start.25
  139.9 2.4 %collective-permute-start.24 = (bf16[2,320,128]{2,1,0:T(8,128)(2,1)S(1)}, bf16[2,320,128]{2,1,0:T(8,128)(2,1)S(1)}, u32[]{:S(2)}, u32[]{:S(2)}) collective-permute-start(bf16[2,320,128]{2,1,0:T(8,128)(2,1)S(1)} %join.6), channel_id=1, source_target_pairs={{0,128},{8,136},{16,144},{24,152},{32,160},{40,168},{48,176},{56,1... | collective-permute-start | bytes 491528 | tf_op jit(solution)/shard_map/ppermute | solution.py:251
  142.4 0.0 collective-permute-done.16.refs_1_.refs_3_
  142.4 0.0 collective-permute-done.21.refs_0_.refs_8_
  142.4 1.3 collective-permute-start.23
  143.7 2.4 %collective-permute-start.22 = (bf16[2,320,128]{2,1,0:T(8,128)(2,1)S(1)}, bf16[2,320,128]{2,1,0:T(8,128)(2,1)S(1)}, u32[]{:S(2)}, u32[]{:S(2)}) collective-permute-start(bf16[2,320,128]{2,1,0:T(8,128)(2,1)S(1)} %join.4), channel_id=1, source_target_pairs={{0,128},{8,136},{16,144},{24,152},{32,160},{40,168},{48,176},{56,1... | collective-permute-start | bytes 491528 | tf_op jit(solution)/shard_map/ppermute | solution.py:251
  146.1 1.2 collective-permute-done.25.refs_12_
  147.3 3.5 %collective-permute-done.24.refs_11_ = bf16[2,320,128]{2,1,0:T(8,128)(2,1)S(1)} collective-permute-done((bf16[2,320,128]{2,1,0:T(8,128)(2,1)S(1)}, bf16[2,320,128]{2,1,0:T(8,128)(2,1)S(1)}, u32[]{:S(2)}, u32[]{:S(2)}) %collective-permute-start.24) | collective-permute-done | bytes 163872 | tf_op jit(solution)/shard_map/ppermute | solution.py:251
  150.8 3.5 %collective-permute-done.23.refs_10_ = bf16[2,320,128]{2,1,0:T(8,128)(2,1)S(1)} collective-permute-done((bf16[2,320,128]{2,1,0:T(8,128)(2,1)S(1)}, bf16[2,320,128]{2,1,0:T(8,128)(2,1)S(1)}, u32[]{:S(2)}, u32[]{:S(2)}) %collective-permute-start.23) | collective-permute-done | bytes 163872 | tf_op jit(solution)/shard_map/ppermute | solution.py:251
  154.3 2.4 %collective-permute-done.22.refs_9_ = bf16[2,320,128]{2,1,0:T(8,128)(2,1)S(1)} collective-permute-done((bf16[2,320,128]{2,1,0:T(8,128)(2,1)S(1)}, bf16[2,320,128]{2,1,0:T(8,128)(2,1)S(1)}, u32[]{:S(2)}, u32[]{:S(2)}) %collective-permute-start.22) | collective-permute-done | bytes 163872 | tf_op jit(solution)/shard_map/ppermute | solution.py:251
  156.7 2.1 %final.1 = bf16[1,320,3072]{2,1,0:T(8,128)(2,1)} custom-call(s32[1]{0:T(128)} %get-tuple-element.47.flag, bf16[1,320,3072]{2,1,0:T(8,128)(2,1)S(1)} %copy-done.5, bf16[2,320,128]{2,1,0:T(8,128)(2,1)S(1)} %get-tuple-element.81.refs_0_.refs_1_, bf16[2,320,128]{2,1,0:T(8,128)(2,1)S(1)} %collective-permute-done.15.refs_1_.refs_2_, ...), custom_call_target="tpu_custom_call" | custom-call | tf_op jit(solution)/shard_map/final/pallas_call | solution.py:365
  (19 shorter events, 0.1 us)
Async XLA Ops:
  3.9 46.5 %collective-permute-start = (bf16[3,320,1024]{2,1,0:T(8,128)(2,1)}, bf16[3,320,1024]{2,1,0:T(8,128)(2,1)}, u32[]{:S(2)}, u32[]{:S(2)}) collective-permute-start(bf16[3,320,1024]{2,1,0:T(8,128)(2,1)} %get-tuple-element.48), channel_id=1, source_target_pairs={{0,128},{8,136},{16,144},{24,152},{32,160},{40,168},{48,176},{56,1... | collective-permute-start | bytes 5898248 | tf_op jit(solution)/shard_map/ppermute | solution.py:251
  9.5 13.3 %collective-permute-start.4 = (bf16[3,320,128]{2,1,0:T(8,128)(2,1)}, bf16[3,320,128]{2,1,0:T(8,128)(2,1)S(1)}, u32[]{:S(2)}, u32[]{:S(2)}) collective-permute-start(bf16[3,320,128]{2,1,0:T(8,128)(2,1)} %get-tuple-element.54), channel_id=1, source_target_pairs={{0,1},{1,2},{2,3},{3,4},{4,5},{5,6},{6,7},{7,0},{8,9},{9,10},{10,1... | collective-permute-start | bytes 737288 | tf_op jit(solution)/shard_map/ppermute | solution.py:244
  11.5 21.8 %collective-permute-start.5 = (bf16[3,320,128]{2,1,0:T(8,128)(2,1)}, bf16[3,320,128]{2,1,0:T(8,128)(2,1)S(1)}, u32[]{:S(2)}, u32[]{:S(2)}) collective-permute-start(bf16[3,320,128]{2,1,0:T(8,128)(2,1)} %get-tuple-element.55), channel_id=1, source_target_pairs={{0,2},{1,3},{2,4},{3,5},{4,6},{5,7},{6,0},{7,1},{8,10},{9,11},{10,... | collective-permute-start | bytes 737288 | tf_op jit(solution)/shard_map/ppermute | solution.py:244
  15.9 26.5 %collective-permute-start.8 = (bf16[3,320,128]{2,1,0:T(8,128)(2,1)}, bf16[3,320,128]{2,1,0:T(8,128)(2,1)S(1)}, u32[]{:S(2)}, u32[]{:S(2)}) collective-permute-start(bf16[3,320,128]{2,1,0:T(8,128)(2,1)} %get-tuple-element.62), channel_id=1, source_target_pairs={{0,7},{1,0},{2,1},{3,2},{4,3},{5,4},{6,5},{7,6},{8,15},{9,8},{10,9... | collective-permute-start | bytes 737288 | tf_op jit(solution)/shard_map/ppermute | solution.py:244
  15.9 41.9 %collective-permute-start.10 = (bf16[3,320,128]{2,1,0:T(8,128)(2,1)}, bf16[3,320,128]{2,1,0:T(8,128)(2,1)S(1)}, u32[]{:S(2)}, u32[]{:S(2)}) collective-permute-start(bf16[3,320,128]{2,1,0:T(8,128)(2,1)} %get-tuple-element.66), channel_id=1, source_target_pairs={{0,6},{1,7},{2,0},{3,1},{4,2},{5,3},{6,4},{7,5},{8,14},{9,15},{10,... | collective-permute-start | bytes 737288 | tf_op jit(solution)/shard_map/ppermute | solution.py:244
  24.4 37.9 %collective-permute-start.6 = (bf16[3,320,128]{2,1,0:T(8,128)(2,1)}, bf16[3,320,128]{2,1,0:T(8,128)(2,1)S(1)}, u32[]{:S(2)}, u32[]{:S(2)}) collective-permute-start(bf16[3,320,128]{2,1,0:T(8,128)(2,1)} %pack_first.5), channel_id=1, source_target_pairs={{0,3},{1,4},{2,5},{3,6},{4,7},{5,0},{6,1},{7,2},{8,11},{9,12},{10,... | collective-permute-start | bytes 737288 | tf_op jit(solution)/shard_map/ppermute | solution.py:244
  34.9 15.4 %copy-start = (bf16[1,320,3072]{2,1,0:T(8,128)(2,1)S(1)}, bf16[1,320,3072]{2,1,0:T(8,128)(2,1)}, u32[]{:S(2)}) copy-start(bf16[1,320,3072]{2,1,0:T(8,128)(2,1)} %refs_0_.10) | copy-start | bytes 5898244
  34.9 29.3 %collective-permute-start.7 = (bf16[3,320,128]{2,1,0:T(8,128)(2,1)}, bf16[3,320,128]{2,1,0:T(8,128)(2,1)S(1)}, u32[]{:S(2)}, u32[]{:S(2)}) collective-permute-start(bf16[3,320,128]{2,1,0:T(8,128)(2,1)} %pack_first.6), channel_id=1, source_target_pairs={{0,4},{1,5},{2,6},{3,7},{4,0},{5,1},{6,2},{7,3},{8,12},{9,13},{10,... | collective-permute-start | bytes 737288 | tf_op jit(solution)/shard_map/ppermute | solution.py:244
  44.1 23.2 %collective-permute-start.9 = (bf16[3,320,128]{2,1,0:T(8,128)(2,1)}, bf16[3,320,128]{2,1,0:T(8,128)(2,1)S(1)}, u32[]{:S(2)}, u32[]{:S(2)}) collective-permute-start(bf16[3,320,128]{2,1,0:T(8,128)(2,1)} %pack_first.7), channel_id=1, source_target_pairs={{0,5},{1,6},{2,7},{3,0},{4,1},{5,2},{6,3},{7,4},{8,13},{9,14},{10,... | collective-permute-start | bytes 737288 | tf_op jit(solution)/shard_map/ppermute | solution.py:244
  50.3 1.5 copy-start.1
  51.9 1.5 copy-start.3
  53.4 16.9 %copy-start.6 = (bf16[3,320,128]{2,1,0:T(8,128)(2,1)S(1)}, bf16[3,320,128]{2,1,0:T(8,128)(2,1)}, u32[]{:S(2)}) copy-start(bf16[3,320,128]{2,1,0:T(8,128)(2,1)} %get-tuple-element.67.refs_0_) | copy-start | bytes 737284
  55.8 12.5 %collective-permute-start.1 = (bf16[3,320,128]{2,1,0:T(8,128)(2,1)S(1)}, bf16[3,320,128]{2,1,0:T(8,128)(2,1)S(1)}, u32[]{:S(2)}, u32[]{:S(2)}) collective-permute-start(bf16[3,320,128]{2,1,0:T(8,128)(2,1)S(1)} %get-tuple-element.50), channel_id=1, source_target_pairs={{0,1},{1,2},{2,3},{3,4},{4,5},{5,6},{6,7},{7,0},{8,9},{9,10},{10,1... | collective-permute-start | bytes 737288 | tf_op jit(solution)/shard_map/ppermute | solution.py:244
  57.8 24.7 %collective-permute-start.2 = (bf16[3,320,128]{2,1,0:T(8,128)(2,1)S(1)}, bf16[3,320,128]{2,1,0:T(8,128)(2,1)S(1)}, u32[]{:S(2)}, u32[]{:S(2)}) collective-permute-start(bf16[3,320,128]{2,1,0:T(8,128)(2,1)S(1)} %get-tuple-element.51), channel_id=1, source_target_pairs={{0,2},{1,3},{2,4},{3,5},{4,6},{5,7},{6,0},{7,1},{8,10},{9,11},{10,... | collective-permute-start | bytes 737288 | tf_op jit(solution)/shard_map/ppermute | solution.py:244
  62.3 38.9 %collective-permute-start.3 = (bf16[3,320,128]{2,1,0:T(8,128)(2,1)S(1)}, bf16[3,320,128]{2,1,0:T(8,128)(2,1)S(1)}, u32[]{:S(2)}, u32[]{:S(2)}) collective-permute-start(bf16[3,320,128]{2,1,0:T(8,128)(2,1)S(1)} %get-tuple-element.52), channel_id=1, source_target_pairs={{0,3},{1,4},{2,5},{3,6},{4,7},{5,0},{6,1},{7,2},{8,11},{9,12},{10,... | collective-permute-start | bytes 737288 | tf_op jit(solution)/shard_map/ppermute | solution.py:244
  64.2 37.0 %collective-permute-start.12 = (bf16[3,320,128]{2,1,0:T(8,128)(2,1)S(1)}, bf16[3,320,128]{2,1,0:T(8,128)(2,1)S(1)}, u32[]{:S(2)}, u32[]{:S(2)}) collective-permute-start(bf16[3,320,128]{2,1,0:T(8,128)(2,1)S(1)} %get-tuple-element.78), channel_id=1, source_target_pairs={{0,5},{1,6},{2,7},{3,0},{4,1},{5,2},{6,3},{7,4},{8,13},{9,14},{10,... | collective-permute-start | bytes 737288 | tf_op jit(solution)/shard_map/ppermute | solution.py:244
  67.3 33.9 %collective-permute-start.13 = (bf16[3,320,128]{2,1,0:T(8,128)(2,1)S(1)}, bf16[3,320,128]{2,1,0:T(8,128)(2,1)S(1)}, u32[]{:S(2)}, u32[]{:S(2)}) collective-permute-start(bf16[3,320,128]{2,1,0:T(8,128)(2,1)S(1)} %get-tuple-element.79), channel_id=1, source_target_pairs={{0,6},{1,7},{2,0},{3,1},{4,2},{5,3},{6,4},{7,5},{8,14},{9,15},{10,... | collective-permute-start | bytes 737288 | tf_op jit(solution)/shard_map/ppermute | solution.py:244
  68.3 35.1 %collective-permute-start.14 = (bf16[3,320,128]{2,1,0:T(8,128)(2,1)S(1)}, bf16[3,320,128]{2,1,0:T(8,128)(2,1)S(1)}, u32[]{:S(2)}, u32[]{:S(2)}) collective-permute-start(bf16[3,320,128]{2,1,0:T(8,128)(2,1)S(1)} %get-tuple-element.80), channel_id=1, source_target_pairs={{0,7},{1,0},{2,1},{3,2},{4,3},{5,4},{6,5},{7,6},{8,15},{9,8},{10,9... | collective-permute-start | bytes 737288 | tf_op jit(solution)/shard_map/ppermute | solution.py:244
  70.3 10.6 %copy-start.2 = (bf16[1,320,3072]{2,1,0:T(8,128)(2,1)S(1)}, bf16[1,320,3072]{2,1,0:T(8,128)(2,1)}, u32[]{:S(2)}) copy-start(bf16[1,320,3072]{2,1,0:T(8,128)(2,1)} %refs_1_.9) | copy-start | bytes 5898244
  70.3 10.6 %copy-start.4 = (bf16[1,320,3072]{2,1,0:T(8,128)(2,1)S(1)}, bf16[1,320,3072]{2,1,0:T(8,128)(2,1)}, u32[]{:S(2)}) copy-start(bf16[1,320,3072]{2,1,0:T(8,128)(2,1)} %refs_2_.9) | copy-start | bytes 5898244
  82.5 27.3 %collective-permute-start.11 = (bf16[3,320,128]{2,1,0:T(8,128)(2,1)S(1)}, bf16[3,320,128]{2,1,0:T(8,128)(2,1)S(1)}, u32[]{:S(2)}, u32[]{:S(2)}) collective-permute-start(bf16[3,320,128]{2,1,0:T(8,128)(2,1)S(1)} %pack_second.3), channel_id=1, source_target_pairs={{0,4},{1,5},{2,6},{3,7},{4,0},{5,1},{6,2},{7,3},{8,12},{9,13},{10,... | collective-permute-start | bytes 737288 | tf_op jit(solution)/shard_map/ppermute | solution.py:244
  112.6 21.8 %collective-permute-start.18 = (bf16[2,320,128]{2,1,0:T(8,128)(2,1)S(1)}, bf16[2,320,128]{2,1,0:T(8,128)(2,1)S(1)}, u32[]{:S(2)}, u32[]{:S(2)}) collective-permute-start(bf16[2,320,128]{2,1,0:T(8,128)(2,1)S(1)} %get-tuple-element.85), channel_id=1, source_target_pairs={{0,4},{1,5},{2,6},{3,7},{4,0},{5,1},{6,2},{7,3},{8,12},{9,13},{10,... | collective-permute-start | bytes 491528 | tf_op jit(solution)/shard_map/ppermute | solution.py:244
  116.7 19.4 %collective-permute-start.19 = (bf16[2,320,128]{2,1,0:T(8,128)(2,1)S(1)}, bf16[2,320,128]{2,1,0:T(8,128)(2,1)S(1)}, u32[]{:S(2)}, u32[]{:S(2)}) collective-permute-start(bf16[2,320,128]{2,1,0:T(8,128)(2,1)S(1)} %get-tuple-element.86), channel_id=1, source_target_pairs={{0,3},{1,4},{2,5},{3,6},{4,7},{5,0},{6,1},{7,2},{8,11},{9,12},{10,... | collective-permute-start | bytes 491528 | tf_op jit(solution)/shard_map/ppermute | solution.py:244
  119.5 19.2 %collective-permute-start.17 = (bf16[2,320,128]{2,1,0:T(8,128)(2,1)S(1)}, bf16[2,320,128]{2,1,0:T(8,128)(2,1)S(1)}, u32[]{:S(2)}, u32[]{:S(2)}) collective-permute-start(bf16[2,320,128]{2,1,0:T(8,128)(2,1)S(1)} %get-tuple-element.84), channel_id=1, source_target_pairs={{0,5},{1,6},{2,7},{3,0},{4,1},{5,2},{6,3},{7,4},{8,13},{9,14},{10,... | collective-permute-start | bytes 491528 | tf_op jit(solution)/shard_map/ppermute | solution.py:244
  124.6 15.3 %collective-permute-start.20 = (bf16[2,320,128]{2,1,0:T(8,128)(2,1)S(1)}, bf16[2,320,128]{2,1,0:T(8,128)(2,1)S(1)}, u32[]{:S(2)}, u32[]{:S(2)}) collective-permute-start(bf16[2,320,128]{2,1,0:T(8,128)(2,1)S(1)} %get-tuple-element.87), channel_id=1, source_target_pairs={{0,2},{1,3},{2,4},{3,5},{4,6},{5,7},{6,0},{7,1},{8,10},{9,11},{10,... | collective-permute-start | bytes 491528 | tf_op jit(solution)/shard_map/ppermute | solution.py:244
  127.4 29.3 %copy-start.5 = (bf16[1,320,3072]{2,1,0:T(8,128)(2,1)S(1)}, bf16[1,320,3072]{2,1,0:T(8,128)(2,1)}, u32[]{:S(2)}) copy-start(bf16[1,320,3072]{2,1,0:T(8,128)(2,1)} %refs_0_.11) | copy-start | bytes 5898244
  127.4 14.9 %collective-permute-start.16 = (bf16[2,320,128]{2,1,0:T(8,128)(2,1)S(1)}, bf16[2,320,128]{2,1,0:T(8,128)(2,1)S(1)}, u32[]{:S(2)}, u32[]{:S(2)}) collective-permute-start(bf16[2,320,128]{2,1,0:T(8,128)(2,1)S(1)} %get-tuple-element.83), channel_id=1, source_target_pairs={{0,6},{1,7},{2,0},{3,1},{4,2},{5,3},{6,4},{7,5},{8,14},{9,15},{10,... | collective-permute-start | bytes 491528 | tf_op jit(solution)/shard_map/ppermute | solution.py:244
  134.4 8.0 %collective-permute-start.21 = (bf16[2,320,128]{2,1,0:T(8,128)(2,1)S(1)}, bf16[2,320,128]{2,1,0:T(8,128)(2,1)S(1)}, u32[]{:S(2)}, u32[]{:S(2)}) collective-permute-start(bf16[2,320,128]{2,1,0:T(8,128)(2,1)S(1)} %get-tuple-element.88), channel_id=1, source_target_pairs={{0,1},{1,2},{2,3},{3,4},{4,5},{5,6},{6,7},{7,0},{8,9},{9,10},{10,1... | collective-permute-start | bytes 491528 | tf_op jit(solution)/shard_map/ppermute | solution.py:244
  136.1 7.5 %collective-permute-start.15 = (bf16[2,320,128]{2,1,0:T(8,128)(2,1)S(1)}, bf16[2,320,128]{2,1,0:T(8,128)(2,1)S(1)}, u32[]{:S(2)}, u32[]{:S(2)}) collective-permute-start(bf16[2,320,128]{2,1,0:T(8,128)(2,1)S(1)} %get-tuple-element.82), channel_id=1, source_target_pairs={{0,7},{1,0},{2,1},{3,2},{4,3},{5,4},{6,5},{7,6},{8,15},{9,8},{10,9... | collective-permute-start | bytes 491528 | tf_op jit(solution)/shard_map/ppermute | solution.py:244
  138.7 8.6 %collective-permute-start.25 = (bf16[2,320,128]{2,1,0:T(8,128)(2,1)S(1)}, bf16[2,320,128]{2,1,0:T(8,128)(2,1)S(1)}, u32[]{:S(2)}, u32[]{:S(2)}) collective-permute-start(bf16[2,320,128]{2,1,0:T(8,128)(2,1)S(1)} %join.7), channel_id=1, source_target_pairs={{0,128},{8,136},{16,144},{24,152},{32,160},{40,168},{48,176},{56,1... | collective-permute-start | bytes 491528 | tf_op jit(solution)/shard_map/ppermute | solution.py:251
  139.9 10.9 %collective-permute-start.24 = (bf16[2,320,128]{2,1,0:T(8,128)(2,1)S(1)}, bf16[2,320,128]{2,1,0:T(8,128)(2,1)S(1)}, u32[]{:S(2)}, u32[]{:S(2)}) collective-permute-start(bf16[2,320,128]{2,1,0:T(8,128)(2,1)S(1)} %join.6), channel_id=1, source_target_pairs={{0,128},{8,136},{16,144},{24,152},{32,160},{40,168},{48,176},{56,1... | collective-permute-start | bytes 491528 | tf_op jit(solution)/shard_map/ppermute | solution.py:251
  142.4 12.0 %collective-permute-start.23 = (bf16[2,320,128]{2,1,0:T(8,128)(2,1)S(1)}, bf16[2,320,128]{2,1,0:T(8,128)(2,1)S(1)}, u32[]{:S(2)}, u32[]{:S(2)}) collective-permute-start(bf16[2,320,128]{2,1,0:T(8,128)(2,1)S(1)} %join.5), channel_id=1, source_target_pairs={{0,128},{8,136},{16,144},{24,152},{32,160},{40,168},{48,176},{56,1... | collective-permute-start | bytes 491528 | tf_op jit(solution)/shard_map/ppermute | solution.py:251
  143.7 13.0 %collective-permute-start.22 = (bf16[2,320,128]{2,1,0:T(8,128)(2,1)S(1)}, bf16[2,320,128]{2,1,0:T(8,128)(2,1)S(1)}, u32[]{:S(2)}, u32[]{:S(2)}) collective-permute-start(bf16[2,320,128]{2,1,0:T(8,128)(2,1)S(1)} %join.4), channel_id=1, source_target_pairs={{0,128},{8,136},{16,144},{24,152},{32,160},{40,168},{48,176},{56,1... | collective-permute-start | bytes 491528 | tf_op jit(solution)/shard_map/ppermute | solution.py:251

commit v4 on v3

--- a/solution.py
+++ b/solution.py
@@ -10,6 +10,7 @@
 
 HEAD_DIM = 128
 GROUPS = 3
+PACK = pltpu.CompilerParams(vmem_limit_bytes=48 << 20)
 SHARED = pltpu.CompilerParams(vmem_limit_bytes=40 << 20)
 
 ANY = pl.BlockSpec(memory_space=pl.ANY)
@@ -19,12 +20,8 @@
 
 
 def ring(pieces):
-    order = [0]
-    for step in range(1, pieces // 2):
-        order += [step, pieces - step]
-    if pieces > 1:
-        order.append(pieces // 2)
-    return order
+    half = pieces // 2
+    return [step for near in range(1, half) for step in (near, pieces - near)] + [half]
 
 
 def head_columns(me, offset, group, pieces):
@@ -39,28 +36,15 @@
         copy.wait()
 
 
-def run_staged(pairs):
-    for load, _ in pairs:
-        load.start()
-    for load, store in pairs:
-        load.wait()
-        store.start()
-    for _, store in pairs:
-        store.wait()
-
-
 def pack_kernel(pieces, offsets, *refs):
-    sources, outs, stage, sems, out_sems = refs[:3], refs[3:-3], refs[-3], refs[-2], refs[-1]
+    sources, outs, sems = refs[:3], refs[3:-1], refs[-1]
     me = lax.axis_index("seq")
-    run_staged(
+    run_copies(
         [
-            (
-                pltpu.make_async_copy(
-                    sources[part].at[0, :, head_columns(me, offset, 0, pieces)],
-                    stage.at[i, part],
-                    sems.at[i, part],
-                ),
-                pltpu.make_async_copy(stage.at[i, part], outs[i].at[part], out_sems.at[i, part]),
+            pltpu.make_async_copy(
+                sources[part].at[0, :, head_columns(me, offset, 0, pieces)],
+                outs[i].at[part],
+                sems.at[i, part],
             )
             for i, offset in enumerate(offsets)
             for part in range(3)
@@ -68,23 +52,21 @@
     )
 
 
-def pack_far_kernel(width, assignment, timestep, plan, *refs):
-    sources, out, flag, stage, sems, out_sems = refs[:3], *refs[3:]
-    request = assignment[lax.axis_index("batch")]
-    flag[0] = plan[request, timestep[request]]
-    run_staged(
+def pack_far_kernel(width, *refs):
+    sources, out, sems = refs[:3], refs[3], refs[4]
+    run_copies(
         [
-            (
-                pltpu.make_async_copy(
-                    sources[part].at[0, :, pl.ds((GROUPS - 1) * width, width)],
-                    stage.at[part],
-                    sems.at[part],
-                ),
-                pltpu.make_async_copy(stage.at[part], out.at[part], out_sems.at[part]),
+            pltpu.make_async_copy(
+                sources[part].at[0, :, pl.ds((GROUPS - 1) * width, width)], out.at[part], sems.at[part]
             )
             for part in range(3)
         ]
     )
+
+
+def flag_kernel(assignment, timestep, plan, flag):
+    request = assignment[lax.axis_index("batch")]
+    flag[0] = plan[request, timestep[request]]
 
 
 def pack_second_kernel(pieces, offsets, flag, *refs):
@@ -196,23 +178,23 @@
         outs[i][1] = results[i * rows : (i + 1) * rows]
 
 
-def join_kernel(count, *refs):
-    for i in range(count):
-        refs[count][i] = refs[i][1]
-
-
-def final_kernel(pieces, chunks, flag, *refs):
+def join_kernel(*refs):
+    for i, piece in enumerate(refs[:-1]):
+        refs[-1][i] = piece[1]
+
+
+def final_kernel(pieces, joins, flag, *refs):
     cached, back = refs[0], refs[1 : 1 + pieces]
-    far, out, sems = refs[1 + pieces : 1 + pieces + len(chunks)], refs[-2], refs[-1]
+    far, out, sems = refs[1 + pieces : 1 + pieces + len(joins)], refs[-2], refs[-1]
     me = lax.axis_index("seq")
 
     @pl.when(flag[0] > 0)
     def _():
         copies = []
-        for chunk, offsets in enumerate(chunks):
+        for join, offsets in enumerate(joins):
             for i, offset in enumerate(offsets):
                 for group, piece in enumerate(
-                    (back[offset].at[0], back[offset].at[1], far[chunk].at[i])
+                    (back[offset].at[0], back[offset].at[1], far[join].at[i])
                 ):
                     copies.append(
                         pltpu.make_async_copy(
@@ -261,14 +243,14 @@
             transcendentals=pairs,
         )
 
-    far_out, flag = pl.pallas_call(
+    far_out = pl.pallas_call(
         functools.partial(pack_far_kernel, group_width),
-        out_shape=(shape(3, rows, group_width), jax.ShapeDtypeStruct((1,), jnp.int32)),
-        in_specs=[SMEM] * 3 + [HBM] * 3,
-        out_specs=(ANY, SMEM),
-        scratch_shapes=[pltpu.VMEM((3, rows, group_width), kind), dma((3,)), dma((3,))],
+        out_shape=shape(3, rows, group_width),
+        in_specs=[HBM] * 3,
+        out_specs=VMEM,
+        scratch_shapes=[dma((3,))],
         name="pack_far",
-    )(assignment, timestep, plan, *sources)
+    )(*sources)
     far_in = across(far_out)
 
     def ordered(values, after):
@@ -279,12 +261,8 @@
             functools.partial(pack_kernel, pieces, offsets),
             out_shape=[shape(3, rows, HEAD_DIM)] * len(offsets),
             in_specs=[HBM] * 3,
-            out_specs=[ANY] * len(offsets),
-            scratch_shapes=[
-                pltpu.VMEM((len(offsets), 3, rows, HEAD_DIM), kind),
-                dma((len(offsets), 3)),
-                dma((len(offsets), 3)),
-            ],
+            out_specs=[VMEM] * len(offsets),
+            scratch_shapes=[dma((len(offsets), 3))],
             name="pack_first",
         )(*sources)
 
@@ -293,22 +271,28 @@
             functools.partial(pack_second_kernel, pieces, offsets),
             out_shape=[shape(3, rows, HEAD_DIM)] * len(offsets),
             in_specs=[SMEM] + [HBM] * 3 + [ANY],
-            out_specs=[ANY] * len(offsets),
+            out_specs=[VMEM] * len(offsets),
             scratch_shapes=[dma((len(offsets), 3))],
-            compiler_params=SHARED,
+            compiler_params=PACK,
             name="pack_second",
         )(flag, *sources, far_in)
 
     first_in = [None] * pieces
-    early, late = order[:5], order[5:]
-    for offset, value in zip(early, pack_first(early, sources)):
-        first_in[offset] = forward(value, offset)
-    for i, offset in enumerate(late):
-        (value,) = pack_first([offset], ordered(sources, first_in[order[1 + i]]))
-        first_in[offset] = forward(value, offset)
+    for offsets, awaited in (([*order[:4], 0], None), ([order[4]], order[0]), ([order[5]], order[1]), ([order[6]], order[2])):
+        values = sources if awaited is None else ordered(sources, first_in[awaited])
+        for offset, value in zip(offsets, pack_first(offsets, values)):
+            first_in[offset] = forward(value, offset)
+
+    flag = pl.pallas_call(
+        flag_kernel,
+        out_shape=jax.ShapeDtypeStruct((1,), jnp.int32),
+        in_specs=[SMEM] * 3,
+        out_specs=SMEM,
+        name="flag",
+    )(*ordered((assignment, timestep, plan), first_in[order[2]]))
 
     second_in = [None] * pieces
-    early, late = order[:-1], order[-1:]
+    early, late = [*order[:-1], 0], order[-1:]
     for offset, value in zip(early, pack_second(early, sources)):
         second_in[offset] = forward(value, offset)
 
@@ -322,13 +306,14 @@
         compiler_params=SHARED,
         cost_estimate=cost(pieces),
         name="attend_first",
-    )(*ordered(first_in, second_in[order[1]]))
+    )(*ordered(first_in, second_in[order[0]]))
 
     for offset, value in zip(late, pack_second(late, ordered(sources, first_result))):
         second_in[offset] = forward(value, offset)
 
     count = 2
-    chunks = [order[begin : begin + count] for begin in range(0, pieces, count)]
+    sends = [order[6], order[4], order[5], *order[2:4], *order[:2], 0]
+    chunks = [sends[begin : begin + count] for begin in range(0, pieces, count)]
     back = [None] * pieces
     for offsets in chunks:
         results = pl.pallas_call(
@@ -350,12 +335,13 @@
         for offset, value in zip(offsets, results):
             back[offset] = backward(value, offset)
 
+    joins = [chunks[0] + chunks[1], *chunks[2:]]
     far_back = []
-    for offsets in chunks:
+    for offsets in joins:
         joined = pl.pallas_call(
-            functools.partial(join_kernel, count),
-            out_shape=shape(count, rows, HEAD_DIM),
-            in_specs=[VMEM] * count,
+            join_kernel,
+            out_shape=shape(len(offsets), rows, HEAD_DIM),
+            in_specs=[VMEM] * len(offsets),
             out_specs=VMEM,
             compiler_params=SHARED,
             name="join",
@@ -363,9 +349,9 @@
         far_back.append(across(joined))
 
     return pl.pallas_call(
-        functools.partial(final_kernel, pieces, chunks),
+        functools.partial(final_kernel, pieces, joins),
         out_shape=shape(*cached_rows.shape),
-        in_specs=[SMEM, HBM] + [ANY] * (pieces + len(chunks)),
+        in_specs=[SMEM, HBM] + [ANY] * (pieces + len(joins)),
         out_specs=ANY,
         scratch_shapes=[dma((GROUPS, pieces))],
         compiler_params=SHARED,

time: 160 us -> 158 us (0.988)
  starting transfers between devices: 70.5 us -> 55.5 us
  waiting for transfers between devices: 46.1 us -> 57.3 us
  Pallas kernels: 38.9 us -> 41 us
    ppermute x21, waiting for transfers between devices: 29.4 us -> 45.6 us  [forward(): lax.ppermute(value, 'seq', [(s, (s + offset) % pieces) for s in range(pie...]
    ppermute x21, starting transfers between devices: 59.9 us -> 45.7 us  [forward(): lax.ppermute(value, 'seq', [(s, (s + offset) % pieces) for s in range(pie...]
    ppermute x5 -> x4, waiting for transfers between devices: 16.8 us -> 11.7 us  [across(): return lax.ppermute(value, 'batch', [(s, s ^ mask) for s in range(slots)])]
    ppermute x5 -> x4, starting transfers between devices: 10.6 us -> 9.83 us  [across(): return lax.ppermute(value, 'batch', [(s, s ^ mask) for s in range(slots)])]
  transfers between devices with their start and end apart: 26 -> 25, of which waited for: 12 -> 10; matrix products, arithmetic and copies ran while one was open for 0% -> 0% of each run, Pallas kernels for 19% -> 21%
where the time goes in v4:
time: 158 us; the launch traced here: 156 us
  waiting for transfers between devices  57.3 us (36%)
  starting transfers between devices  55.5 us (35%)
  Pallas kernels  41 us (26%)
    ppermute x21, starting transfers between devices, forward(): lax.ppermute(value, 'seq', [(s, (s + offset) % pieces) for s in range(pie...  45.7 us
    ppermute x21, waiting for transfers between devices, forward(): lax.ppermute(value, 'seq', [(s, (s + offset) % pieces) for s in range(pie...  45.6 us
    pallas_call x1, Pallas kernels, body(): pl.pallas_call(functools.partial(first_kernel, pieces, rows), out_shape=s...  11.7 us
    ppermute x4, waiting for transfers between devices, across(): return lax.ppermute(value, 'batch', [(s, s ^ mask) for s in range(slots)])  11.7 us
    pallas_call x4, Pallas kernels, body(): pl.pallas_call(functools.partial(second_kernel, pieces, rows, offsets), o...  11.1 us
    ppermute x4, starting transfers between devices, across(): return lax.ppermute(value, 'batch', [(s, s ^ mask) for s in range(slots)])  9.83 us
    pallas_call x4, Pallas kernels, pack_first(): pl.pallas_call(functools.partial(pack_kernel, pieces, offsets), out_shape...  7.58 us
    pallas_call x2, Pallas kernels, pack_second(): pl.pallas_call(functools.partial(pack_second_kernel, pieces, offsets), ou...  4.15 us
  transfers between devices with their start and end apart: 25, of which 10 were waited for; matrix products, arithmetic and copies ran while one was open for 0% of the time, Pallas kernels for 21%

profile of v4, /device:TPU:34, one launch (start us, length us, event | category | flops | bytes accessed | tf_op | source)
XLA Modules:
  0.0 155.8 jit_solution(16529037938710809248)
XLA Ops:
  0.0 2.8 %pack_far.1 = bf16[3,320,1024]{2,1,0:T(8,128)(2,1)} custom-call(bf16[1,320,3072]{2,1,0:T(8,128)(2,1)} %refs_0_.10, bf16[1,320,3072]{2,1,0:T(8,128)(2,1)} %refs_1_.9, bf16[1,320,3072]{2,1,0:T(8,128)(2,1)} %refs_2_.9), custom_call_target="tpu_custom_call" | custom-call | tf_op jit(solution)/shard_map/pack_far/pallas_call | solution.py:246
  2.8 3.3 %collective-permute-start.1 = (bf16[3,320,1024]{2,1,0:T(8,128)(2,1)}, bf16[3,320,1024]{2,1,0:T(8,128)(2,1)}, u32[]{:S(2)}, u32[]{:S(2)}) collective-permute-start(bf16[3,320,1024]{2,1,0:T(8,128)(2,1)} %pack_far.1), channel_id=1, source_target_pairs={{0,128},{8,136},{16,144},{24,152},{32,160},{40,168},{48,176},{56,1... | collective-permute-start | bytes 5898248 | tf_op jit(solution)/shard_map/ppermute | solution.py:233
  6.1 2.5 %pack_first.4 = (bf16[3,320,128]{2,1,0:T(8,128)(2,1)}, bf16[3,320,128]{2,1,0:T(8,128)(2,1)}, bf16[3,320,128]{2,1,0:T(8,128)(2,1)}, bf16[3,320,128]{2,1,0:T(8,128)(2,1)}, bf16[3,320,128]{2,1,0:T(8,128)(2,1)}) custom-call(bf16[1,320,3072]{2,1,0:T(8,128)(2,1)} %refs_0_.10, bf16[1,320,3072]{2,1,0:T(8,128)(2,1)} %refs_1_.9, bf16[1,320,3072]{2,1,0:T(8,128)(2,1)} %refs_2_.9), custom_call_target="tpu_custom_call" | custom-call | tf_op jit(solution)/shard_map/pack_first/pallas_call | solution.py:260
  8.6 3.3 %collective-permute-start = (bf16[3,320,128]{2,1,0:T(8,128)(2,1)}, bf16[3,320,128]{2,1,0:T(8,128)(2,1)S(1)}, u32[]{:S(2)}, u32[]{:S(2)}) collective-permute-start(bf16[3,320,128]{2,1,0:T(8,128)(2,1)} %get-tuple-element.48), channel_id=1, source_target_pairs={{0,2},{1,3},{2,4},{3,5},{4,6},{5,7},{6,0},{7,1},{8,10},{9,11},{10,... | collective-permute-start | bytes 737288 | tf_op jit(solution)/shard_map/ppermute | solution.py:226
  12.0 3.1 %collective-permute-start.5 = (bf16[3,320,128]{2,1,0:T(8,128)(2,1)}, bf16[3,320,128]{2,1,0:T(8,128)(2,1)S(1)}, u32[]{:S(2)}, u32[]{:S(2)}) collective-permute-start(bf16[3,320,128]{2,1,0:T(8,128)(2,1)} %get-tuple-element.57), channel_id=1, source_target_pairs={{0,1},{1,2},{2,3},{3,4},{4,5},{5,6},{6,7},{7,0},{8,9},{9,10},{10,1... | collective-permute-start | bytes 737288 | tf_op jit(solution)/shard_map/ppermute | solution.py:226
  15.1 0.0 collective-permute-start.8
  15.1 1.1 collective-permute-start.10
  16.2 9.3 %collective-permute-done.refs_2_ = bf16[3,320,128]{2,1,0:T(8,128)(2,1)S(1)} collective-permute-done((bf16[3,320,128]{2,1,0:T(8,128)(2,1)}, bf16[3,320,128]{2,1,0:T(8,128)(2,1)S(1)}, u32[]{:S(2)}, u32[]{:S(2)}) %collective-permute-start) | collective-permute-done | bytes 245792 | tf_op jit(solution)/shard_map/ppermute | solution.py:226
  25.5 1.7 %pack_first.6 = bf16[3,320,128]{2,1,0:T(8,128)(2,1)} custom-call(bf16[1,320,3072]{2,1,0:T(8,128)(2,1)} %refs_0_.10, bf16[1,320,3072]{2,1,0:T(8,128)(2,1)} %refs_1_.9, bf16[1,320,3072]{2,1,0:T(8,128)(2,1)} %refs_2_.9), custom_call_target="tpu_custom_call" | custom-call | tf_op jit(solution)/shard_map/pack_first/pallas_call | solution.py:260
  27.2 5.3 %collective-permute-start.7 = (bf16[3,320,128]{2,1,0:T(8,128)(2,1)}, bf16[3,320,128]{2,1,0:T(8,128)(2,1)S(1)}, u32[]{:S(2)}, u32[]{:S(2)}) collective-permute-start(bf16[3,320,128]{2,1,0:T(8,128)(2,1)} %pack_first.6), channel_id=1, source_target_pairs={{0,4},{1,5},{2,6},{3,7},{4,0},{5,1},{6,2},{7,3},{8,12},{9,13},{10,... | collective-permute-start | bytes 737288 | tf_op jit(solution)/shard_map/ppermute | solution.py:226
  32.5 0.0 collective-permute-done.5.refs_1_
  32.5 1.7 %pack_first.5 = bf16[3,320,128]{2,1,0:T(8,128)(2,1)} custom-call(bf16[1,320,3072]{2,1,0:T(8,128)(2,1)} %refs_0_.10, bf16[1,320,3072]{2,1,0:T(8,128)(2,1)} %refs_1_.9, bf16[1,320,3072]{2,1,0:T(8,128)(2,1)} %refs_2_.9), custom_call_target="tpu_custom_call" | custom-call | tf_op jit(solution)/shard_map/pack_first/pallas_call | solution.py:260
  34.2 0.0 copy-start
  34.2 2.4 %collective-permute-start.6 = (bf16[3,320,128]{2,1,0:T(8,128)(2,1)}, bf16[3,320,128]{2,1,0:T(8,128)(2,1)S(1)}, u32[]{:S(2)}, u32[]{:S(2)}) collective-permute-start(bf16[3,320,128]{2,1,0:T(8,128)(2,1)} %pack_first.5), channel_id=1, source_target_pairs={{0,3},{1,4},{2,5},{3,6},{4,7},{5,0},{6,1},{7,2},{8,11},{9,12},{10,... | collective-permute-start | bytes 737288 | tf_op jit(solution)/shard_map/ppermute | solution.py:226
  36.6 0.0 collective-permute-done.8.refs_7_
  36.6 1.7 %pack_first.7 = bf16[3,320,128]{2,1,0:T(8,128)(2,1)} custom-call(bf16[1,320,3072]{2,1,0:T(8,128)(2,1)} %refs_0_.10, bf16[1,320,3072]{2,1,0:T(8,128)(2,1)} %refs_1_.9, bf16[1,320,3072]{2,1,0:T(8,128)(2,1)} %refs_2_.9), custom_call_target="tpu_custom_call" | custom-call | tf_op jit(solution)/shard_map/pack_first/pallas_call | solution.py:260
  38.3 2.8 %collective-permute-start.9 = (bf16[3,320,128]{2,1,0:T(8,128)(2,1)}, bf16[3,320,128]{2,1,0:T(8,128)(2,1)}, u32[]{:S(2)}, u32[]{:S(2)}) collective-permute-start(bf16[3,320,128]{2,1,0:T(8,128)(2,1)} %pack_first.7), channel_id=1, source_target_pairs={{0,5},{1,6},{2,7},{3,0},{4,1},{5,2},{6,3},{7,4},{8,13},{9,14},{10,... | collective-permute-start | bytes 737288 | tf_op jit(solution)/shard_map/ppermute | solution.py:226
  41.1 1.5 flag.1
  42.6 6.7 %collective-permute-done.1.refs_3_ = bf16[3,320,1024]{2,1,0:T(8,128)(2,1)} collective-permute-done((bf16[3,320,1024]{2,1,0:T(8,128)(2,1)}, bf16[3,320,1024]{2,1,0:T(8,128)(2,1)}, u32[]{:S(2)}, u32[]{:S(2)}) %collective-permute-start.1) | collective-permute-done | bytes 1966112 | tf_op jit(solution)/shard_map/ppermute | solution.py:233
  49.3 1.5 copy-done.1
  50.8 2.5 %pack_second.2 = (bf16[3,320,128]{2,1,0:T(8,128)(2,1)S(1)}, bf16[3,320,128]{2,1,0:T(8,128)(2,1)S(1)}, bf16[3,320,128]{2,1,0:T(8,128)(2,1)S(1)}, bf16[3,320,128]{...) custom-call(s32[1]{0:T(128)} %flag.1, ...), custom_call_target="tpu_custom_call" | custom-call | tf_op jit(solution)/shard_map/pack_second/pallas_call | solution.py:270
  53.3 2.0 %collective-permute-start.2 = (bf16[3,320,128]{2,1,0:T(8,128)(2,1)S(1)}, bf16[3,320,128]{2,1,0:T(8,128)(2,1)S(1)}, u32[]{:S(2)}, u32[]{:S(2)}) collective-permute-start(bf16[3,320,128]{2,1,0:T(8,128)(2,1)S(1)} %get-tuple-element.53), channel_id=1, source_target_pairs={{0,1},{1,2},{2,3},{3,4},{4,5},{5,6},{6,7},{7,0},{8,9},{9,10},{10,1... | collective-permute-start | bytes 737288 | tf_op jit(solution)/shard_map/ppermute | solution.py:226
  55.3 0.0 collective-permute-done.10.refs_6_
  55.3 4.5 %collective-permute-start.3 = (bf16[3,320,128]{2,1,0:T(8,128)(2,1)S(1)}, bf16[3,320,128]{2,1,0:T(8,128)(2,1)S(1)}, u32[]{:S(2)}, u32[]{:S(2)}) collective-permute-start(bf16[3,320,128]{2,1,0:T(8,128)(2,1)S(1)} %get-tuple-element.54), channel_id=1, source_target_pairs={{0,2},{1,3},{2,4},{3,5},{4,6},{5,7},{6,0},{7,1},{8,10},{9,11},{10,... | collective-permute-start | bytes 737288 | tf_op jit(solution)/shard_map/ppermute | solution.py:226
  59.8 0.0 collective-permute-done.7.refs_4_
  59.8 1.9 %collective-permute-start.4 = (bf16[3,320,128]{2,1,0:T(8,128)(2,1)S(1)}, bf16[3,320,128]{2,1,0:T(8,128)(2,1)S(1)}, u32[]{:S(2)}, u32[]{:S(2)}) collective-permute-start(bf16[3,320,128]{2,1,0:T(8,128)(2,1)S(1)} %get-tuple-element.55), channel_id=1, source_target_pairs={{0,3},{1,4},{2,5},{3,6},{4,7},{5,0},{6,1},{7,2},{8,11},{9,12},{10,... | collective-permute-start | bytes 737288 | tf_op jit(solution)/shard_map/ppermute | solution.py:226
  61.7 0.0 collective-permute-done.6.refs_3_
  61.7 3.1 %collective-permute-start.12 = (bf16[3,320,128]{2,1,0:T(8,128)(2,1)S(1)}, bf16[3,320,128]{2,1,0:T(8,128)(2,1)S(1)}, u32[]{:S(2)}, u32[]{:S(2)}) collective-permute-start(bf16[3,320,128]{2,1,0:T(8,128)(2,1)S(1)} %get-tuple-element.80), channel_id=1, source_target_pairs={{0,5},{1,6},{2,7},{3,0},{4,1},{5,2},{6,3},{7,4},{8,13},{9,14},{10,... | collective-permute-start | bytes 737288 | tf_op jit(solution)/shard_map/ppermute | solution.py:226
  64.8 0.0 collective-permute-done.9.refs_5_
  64.8 1.2 collective-permute-done.2.refs_1_
  66.0 1.7 %collective-permute-start.14 = (bf16[3,320,128]{2,1,0:T(8,128)(2,1)S(1)}, bf16[3,320,128]{2,1,0:T(8,128)(2,1)S(1)}, u32[]{:S(2)}, u32[]{:S(2)}) collective-permute-start(bf16[3,320,128]{2,1,0:T(8,128)(2,1)S(1)} %get-tuple-element.82), channel_id=1, source_target_pairs={{0,7},{1,0},{2,1},{3,2},{4,3},{5,4},{6,5},{7,6},{8,15},{9,8},{10,9... | collective-permute-start | bytes 737288 | tf_op jit(solution)/shard_map/ppermute | solution.py:226
  67.7 11.7 %attend_first.1.refs_8_ = bf16[2560,128]{1,0:T(8,128)(2,1)S(1)} custom-call(bf16[3,320,128]{2,1,0:T(8,128)(2,1)S(1)} %copy-done.4, bf16[3,320,128]{2,1,0:T(8,128)(2,1)S(1)} %collective-permute-done.5.refs_1_, bf16[3,320,128]{2,1,0:T(8,128)(2,1)S(1)} %collective-permute-done.refs_2_, bf16[3,320,128]{2,1,0:T(8,128)(2,1)S(1)} %collective-permute-done.6.refs_3_, ...), custom_call_target="tpu_custom_call" | custom-call | flops 3355443200 | bytes 2621440 | tf_op jit(solution)/shard_map/attend_first/pallas_call | solution.py:300
  79.4 1.7 %pack_second.3 = bf16[3,320,128]{2,1,0:T(8,128)(2,1)S(1)} custom-call(s32[1]{0:T(128)} %flag.1, bf16[1,320,3072]{2,1,0:T(8,128)(2,1)S(1)} %copy-done, bf16[1,320,3072]{2,1,0:T(8,128)(2,1)S(1)} %copy-done.1, bf16[1,320,3072]{2,1,0:T(8,128)(2,1)S(1)} %copy-done.2, bf16[3,320,1024]{2,1,0:T(8,128)(2,1)} %collective-permute-done.1.refs_3_), custom_call_target="tpu_custom_call" | custom-call | tf_op jit(solution)/shard_map/pack_second/pallas_call | solution.py:270
  81.1 0.0 collective-permute-done.3.refs_2_
  81.1 4.8 %collective-permute-start.11 = (bf16[3,320,128]{2,1,0:T(8,128)(2,1)S(1)}, bf16[3,320,128]{2,1,0:T(8,128)(2,1)S(1)}, u32[]{:S(2)}, u32[]{:S(2)}) collective-permute-start(bf16[3,320,128]{2,1,0:T(8,128)(2,1)S(1)} %pack_second.3), channel_id=1, source_target_pairs={{0,4},{1,5},{2,6},{3,7},{4,0},{5,1},{6,2},{7,3},{8,12},{9,13},{10,... | collective-permute-start | bytes 737288 | tf_op jit(solution)/shard_map/ppermute | solution.py:226
  86.0 9.2 %collective-permute-done.4.refs_3_ = bf16[3,320,128]{2,1,0:T(8,128)(2,1)S(1)} collective-permute-done((bf16[3,320,128]{2,1,0:T(8,128)(2,1)S(1)}, bf16[3,320,128]{2,1,0:T(8,128)(2,1)S(1)}, u32[]{:S(2)}, u32[]{:S(2)}) %collective-permute-start.4) | collective-permute-done | bytes 245792 | tf_op jit(solution)/shard_map/ppermute | solution.py:226
  95.2 0.0 collective-permute-done.12.refs_5_
  95.2 0.0 collective-permute-done.13.refs_6_
  95.2 4.0 %collective-permute-done.14.refs_7_ = bf16[3,320,128]{2,1,0:T(8,128)(2,1)S(1)} collective-permute-done((bf16[3,320,128]{2,1,0:T(8,128)(2,1)S(1)}, bf16[3,320,128]{2,1,0:T(8,128)(2,1)S(1)}, u32[]{:S(2)}, u32[]{:S(2)}) %collective-permute-start.14) | collective-permute-done | bytes 245792 | tf_op jit(solution)/shard_map/ppermute | solution.py:226
  99.1 8.2 %collective-permute-done.11.refs_4_ = bf16[3,320,128]{2,1,0:T(8,128)(2,1)S(1)} collective-permute-done((bf16[3,320,128]{2,1,0:T(8,128)(2,1)S(1)}, bf16[3,320,128]{2,1,0:T(8,128)(2,1)S(1)}, u32[]{:S(2)}, u32[]{:S(2)}) %collective-permute-start.11) | collective-permute-done | bytes 245792 | tf_op jit(solution)/shard_map/ppermute | solution.py:226
  107.4 2.8 %attend_second.7 = (bf16[2,320,128]{2,1,0:T(8,128)(2,1)S(1)}, bf16[2,320,128]{2,1,0:T(8,128)(2,1)S(1)}) custom-call(bf16[3,320,128]{2,1,0:T(8,128)(2,1)S(1)} %get-tuple-element.52.refs_0_, bf16[3,320,128]{2,1,0:T(8,128)(2,1)S(1)} %collective-permute-done.2.refs_1_, bf16[3,320,128]{2,1,0:T(8,128)(2,1)S(1)} %collective-permute-done.3.refs_2_, ...), custom_call_target="tpu_custom_call" | custom-call | flops 838860800 | bytes 1638400 | tf_op jit(solution)/shard_map/attend_second/pallas_call | solution.py:319
  110.1 0.1 collective-permute-start.17
  110.2 4.1 %collective-permute-start.18 = (bf16[2,320,128]{2,1,0:T(8,128)(2,1)S(1)}, bf16[2,320,128]{2,1,0:T(8,128)(2,1)S(1)}, u32[]{:S(2)}, u32[]{:S(2)}) collective-permute-start(bf16[2,320,128]{2,1,0:T(8,128)(2,1)S(1)} %get-tuple-element.87), channel_id=1, source_target_pairs={{0,4},{1,5},{2,6},{3,7},{4,0},{5,1},{6,2},{7,3},{8,12},{9,13},{10,... | collective-permute-start | bytes 491528 | tf_op jit(solution)/shard_map/ppermute | solution.py:226
  114.3 2.8 %attend_second.6 = (bf16[2,320,128]{2,1,0:T(8,128)(2,1)S(1)}, bf16[2,320,128]{2,1,0:T(8,128)(2,1)S(1)}) custom-call(bf16[3,320,128]{2,1,0:T(8,128)(2,1)S(1)} %get-tuple-element.52.refs_0_, bf16[3,320,128]{2,1,0:T(8,128)(2,1)S(1)} %collective-permute-done.2.refs_1_, bf16[3,320,128]{2,1,0:T(8,128)(2,1)S(1)} %collective-permute-done.3.refs_2_, ...), custom_call_target="tpu_custom_call" | custom-call | flops 838860800 | bytes 1638400 | tf_op jit(solution)/shard_map/attend_second/pallas_call | solution.py:319
  117.1 0.1 collective-permute-start.16
  117.2 5.2 %collective-permute-start.19 = (bf16[2,320,128]{2,1,0:T(8,128)(2,1)S(1)}, bf16[2,320,128]{2,1,0:T(8,128)(2,1)S(1)}, u32[]{:S(2)}, u32[]{:S(2)}) collective-permute-start(bf16[2,320,128]{2,1,0:T(8,128)(2,1)S(1)} %get-tuple-element.88), channel_id=1, source_target_pairs={{0,3},{1,4},{2,5},{3,6},{4,7},{5,0},{6,1},{7,2},{8,11},{9,12},{10,... | collective-permute-start | bytes 491528 | tf_op jit(solution)/shard_map/ppermute | solution.py:226
  122.4 2.8 %attend_second.5 = (bf16[2,320,128]{2,1,0:T(8,128)(2,1)S(1)}, bf16[2,320,128]{2,1,0:T(8,128)(2,1)S(1)}) custom-call(bf16[3,320,128]{2,1,0:T(8,128)(2,1)S(1)} %get-tuple-element.52.refs_0_, bf16[3,320,128]{2,1,0:T(8,128)(2,1)S(1)} %collective-permute-done.2.refs_1_, bf16[3,320,128]{2,1,0:T(8,128)(2,1)S(1)} %collective-permute-done.3.refs_2_, ...), custom_call_target="tpu_custom_call" | custom-call | flops 838860800 | bytes 1638400 | tf_op jit(solution)/shard_map/attend_second/pallas_call | solution.py:319
  125.2 0.0 copy-start.3
  125.2 0.1 collective-permute-start.15
  125.3 2.8 %attend_second.4 = (bf16[2,320,128]{2,1,0:T(8,128)(2,1)S(1)}, bf16[2,320,128]{2,1,0:T(8,128)(2,1)S(1)}) custom-call(bf16[3,320,128]{2,1,0:T(8,128)(2,1)S(1)} %get-tuple-element.52.refs_0_, bf16[3,320,128]{2,1,0:T(8,128)(2,1)S(1)} %collective-permute-done.2.refs_1_, bf16[3,320,128]{2,1,0:T(8,128)(2,1)S(1)} %collective-permute-done.3.refs_2_, ...), custom_call_target="tpu_custom_call" | custom-call | flops 838860800 | bytes 1638400 | tf_op jit(solution)/shard_map/attend_second/pallas_call | solution.py:319
  128.1 7.3 %collective-permute-done.17.refs_1_.refs_4_ = bf16[2,320,128]{2,1,0:T(8,128)(2,1)S(1)} collective-permute-done((bf16[2,320,128]{2,1,0:T(8,128)(2,1)S(1)}, bf16[2,320,128]{2,1,0:T(8,128)(2,1)S(1)}, u32[]{:S(2)}, u32[]{:S(2)}) %collective-permute-start.17) | collective-permute-done | bytes 163872 | tf_op jit(solution)/shard_map/ppermute | solution.py:226
  135.4 0.0 collective-permute-done.18.refs_0_.refs_5_
  135.4 0.0 collective-permute-start.21
  135.4 0.0 collective-permute-done.16.refs_3_
  135.4 0.0 collective-permute-done.19.refs_2_.refs_6_
  135.5 2.8 %collective-permute-start.22 = (bf16[4,320,128]{2,1,0:T(8,128)(2,1)S(1)}, bf16[4,320,128]{2,1,0:T(8,128)(2,1)S(1)}, u32[]{:S(2)}, u32[]{:S(2)}) collective-permute-start(bf16[4,320,128]{2,1,0:T(8,128)(2,1)S(1)} %join.3), channel_id=1, source_target_pairs={{0,128},{8,136},{16,144},{24,152},{32,160},{40,168},{48,176},{56,1... | collective-permute-start | bytes 983048 | tf_op jit(solution)/shard_map/ppermute | solution.py:233
  138.3 0.0 collective-permute-done.15.refs_1_.refs_2_
  138.3 6.3 %collective-permute-done.20.refs_0_.refs_7_ = bf16[2,320,128]{2,1,0:T(8,128)(2,1)S(1)} collective-permute-done((bf16[2,320,128]{2,1,0:T(8,128)(2,1)S(1)}, bf16[2,320,128]{2,1,0:T(8,128)(2,1)S(1)}, u32[]{:S(2)}, u32[]{:S(2)}) %collective-permute-start.20) | collective-permute-done | bytes 163872 | tf_op jit(solution)/shard_map/ppermute | solution.py:226
  144.7 1.8 %collective-permute-start.23 = (bf16[2,320,128]{2,1,0:T(8,128)(2,1)S(1)}, bf16[2,320,128]{2,1,0:T(8,128)(2,1)S(1)}, u32[]{:S(2)}, u32[]{:S(2)}) collective-permute-start(bf16[2,320,128]{2,1,0:T(8,128)(2,1)S(1)} %join.4), channel_id=1, source_target_pairs={{0,128},{8,136},{16,144},{24,152},{32,160},{40,168},{48,176},{56,1... | collective-permute-start | bytes 491528 | tf_op jit(solution)/shard_map/ppermute | solution.py:233
  146.5 1.9 %collective-permute-start.24 = (bf16[2,320,128]{2,1,0:T(8,128)(2,1)S(1)}, bf16[2,320,128]{2,1,0:T(8,128)(2,1)S(1)}, u32[]{:S(2)}, u32[]{:S(2)}) collective-permute-start(bf16[2,320,128]{2,1,0:T(8,128)(2,1)S(1)} %join.5), channel_id=1, source_target_pairs={{0,128},{8,136},{16,144},{24,152},{32,160},{40,168},{48,176},{56,1... | collective-permute-start | bytes 491528 | tf_op jit(solution)/shard_map/ppermute | solution.py:233
  148.4 3.2 %collective-permute-done.23.refs_10_ = bf16[2,320,128]{2,1,0:T(8,128)(2,1)S(1)} collective-permute-done((bf16[2,320,128]{2,1,0:T(8,128)(2,1)S(1)}, bf16[2,320,128]{2,1,0:T(8,128)(2,1)S(1)}, u32[]{:S(2)}, u32[]{:S(2)}) %collective-permute-start.23) | collective-permute-done | bytes 163872 | tf_op jit(solution)/shard_map/ppermute | solution.py:233
  151.6 1.8 %collective-permute-done.24.refs_11_ = bf16[2,320,128]{2,1,0:T(8,128)(2,1)S(1)} collective-permute-done((bf16[2,320,128]{2,1,0:T(8,128)(2,1)S(1)}, bf16[2,320,128]{2,1,0:T(8,128)(2,1)S(1)}, u32[]{:S(2)}, u32[]{:S(2)}) %collective-permute-start.24) | collective-permute-done | bytes 163872 | tf_op jit(solution)/shard_map/ppermute | solution.py:233
  153.4 0.0 collective-permute-done.22.refs_9_
  153.4 2.2 %final.1 = bf16[1,320,3072]{2,1,0:T(8,128)(2,1)} custom-call(s32[1]{0:T(128)} %flag.1, bf16[1,320,3072]{2,1,0:T(8,128)(2,1)S(1)} %copy-done.3, bf16[2,320,128]{2,1,0:T(8,128)(2,1)S(1)} %get-tuple-element.83.refs_1_, bf16[2,320,128]{2,1,0:T(8,128)(2,1)S(1)} %collective-permute-done.15.refs_1_.refs_2_, ...), custom_call_target="tpu_custom_call" | custom-call | tf_op jit(solution)/shard_map/final/pallas_call | solution.py:351
  (13 shorter events, 0.1 us)
Async XLA Ops:
  2.8 46.5 %collective-permute-start.1 = (bf16[3,320,1024]{2,1,0:T(8,128)(2,1)}, bf16[3,320,1024]{2,1,0:T(8,128)(2,1)}, u32[]{:S(2)}, u32[]{:S(2)}) collective-permute-start(bf16[3,320,1024]{2,1,0:T(8,128)(2,1)} %pack_far.1), channel_id=1, source_target_pairs={{0,128},{8,136},{16,144},{24,152},{32,160},{40,168},{48,176},{56,1... | collective-permute-start | bytes 5898248 | tf_op jit(solution)/shard_map/ppermute | solution.py:233
  8.6 16.9 %collective-permute-start = (bf16[3,320,128]{2,1,0:T(8,128)(2,1)}, bf16[3,320,128]{2,1,0:T(8,128)(2,1)S(1)}, u32[]{:S(2)}, u32[]{:S(2)}) collective-permute-start(bf16[3,320,128]{2,1,0:T(8,128)(2,1)} %get-tuple-element.48), channel_id=1, source_target_pairs={{0,2},{1,3},{2,4},{3,5},{4,6},{5,7},{6,0},{7,1},{8,10},{9,11},{10,... | collective-permute-start | bytes 737288 | tf_op jit(solution)/shard_map/ppermute | solution.py:226
  12.0 20.6 %collective-permute-start.5 = (bf16[3,320,128]{2,1,0:T(8,128)(2,1)}, bf16[3,320,128]{2,1,0:T(8,128)(2,1)S(1)}, u32[]{:S(2)}, u32[]{:S(2)}) collective-permute-start(bf16[3,320,128]{2,1,0:T(8,128)(2,1)} %get-tuple-element.57), channel_id=1, source_target_pairs={{0,1},{1,2},{2,3},{3,4},{4,5},{5,6},{6,7},{7,0},{8,9},{9,10},{10,1... | collective-permute-start | bytes 737288 | tf_op jit(solution)/shard_map/ppermute | solution.py:226
  15.1 21.5 %collective-permute-start.8 = (bf16[3,320,128]{2,1,0:T(8,128)(2,1)}, bf16[3,320,128]{2,1,0:T(8,128)(2,1)S(1)}, u32[]{:S(2)}, u32[]{:S(2)}) collective-permute-start(bf16[3,320,128]{2,1,0:T(8,128)(2,1)} %get-tuple-element.64), channel_id=1, source_target_pairs={{0,7},{1,0},{2,1},{3,2},{4,3},{5,4},{6,5},{7,6},{8,15},{9,8},{10,9... | collective-permute-start | bytes 737288 | tf_op jit(solution)/shard_map/ppermute | solution.py:226
  15.1 40.2 %collective-permute-start.10 = (bf16[3,320,128]{2,1,0:T(8,128)(2,1)}, bf16[3,320,128]{2,1,0:T(8,128)(2,1)S(1)}, u32[]{:S(2)}, u32[]{:S(2)}) collective-permute-start(bf16[3,320,128]{2,1,0:T(8,128)(2,1)} %get-tuple-element.68), channel_id=1, source_target_pairs={{0,6},{1,7},{2,0},{3,1},{4,2},{5,3},{6,4},{7,5},{8,14},{9,15},{10,... | collective-permute-start | bytes 737288 | tf_op jit(solution)/shard_map/ppermute | solution.py:226
  27.2 32.6 %collective-permute-start.7 = (bf16[3,320,128]{2,1,0:T(8,128)(2,1)}, bf16[3,320,128]{2,1,0:T(8,128)(2,1)S(1)}, u32[]{:S(2)}, u32[]{:S(2)}) collective-permute-start(bf16[3,320,128]{2,1,0:T(8,128)(2,1)} %pack_first.6), channel_id=1, source_target_pairs={{0,4},{1,5},{2,6},{3,7},{4,0},{5,1},{6,2},{7,3},{8,12},{9,13},{10,... | collective-permute-start | bytes 737288 | tf_op jit(solution)/shard_map/ppermute | solution.py:226
  34.2 15.1 %copy-start = (bf16[1,320,3072]{2,1,0:T(8,128)(2,1)S(1)}, bf16[1,320,3072]{2,1,0:T(8,128)(2,1)}, u32[]{:S(2)}) copy-start(bf16[1,320,3072]{2,1,0:T(8,128)(2,1)} %refs_0_.10) | copy-start | bytes 5898244
  34.2 27.5 %collective-permute-start.6 = (bf16[3,320,128]{2,1,0:T(8,128)(2,1)}, bf16[3,320,128]{2,1,0:T(8,128)(2,1)S(1)}, u32[]{:S(2)}, u32[]{:S(2)}) collective-permute-start(bf16[3,320,128]{2,1,0:T(8,128)(2,1)} %pack_first.5), channel_id=1, source_target_pairs={{0,3},{1,4},{2,5},{3,6},{4,7},{5,0},{6,1},{7,2},{8,11},{9,12},{10,... | collective-permute-start | bytes 737288 | tf_op jit(solution)/shard_map/ppermute | solution.py:226
  38.3 26.5 %collective-permute-start.9 = (bf16[3,320,128]{2,1,0:T(8,128)(2,1)}, bf16[3,320,128]{2,1,0:T(8,128)(2,1)}, u32[]{:S(2)}, u32[]{:S(2)}) collective-permute-start(bf16[3,320,128]{2,1,0:T(8,128)(2,1)} %pack_first.7), channel_id=1, source_target_pairs={{0,5},{1,6},{2,7},{3,0},{4,1},{5,2},{6,3},{7,4},{8,13},{9,14},{10,... | collective-permute-start | bytes 737288 | tf_op jit(solution)/shard_map/ppermute | solution.py:226
  49.3 1.5 copy-start.1
  50.8 16.9 %copy-start.4 = (bf16[3,320,128]{2,1,0:T(8,128)(2,1)S(1)}, bf16[3,320,128]{2,1,0:T(8,128)(2,1)}, u32[]{:S(2)}) copy-start(bf16[3,320,128]{2,1,0:T(8,128)(2,1)} %get-tuple-element.69.refs_0_) | copy-start | bytes 737284
  53.3 12.7 %collective-permute-start.2 = (bf16[3,320,128]{2,1,0:T(8,128)(2,1)S(1)}, bf16[3,320,128]{2,1,0:T(8,128)(2,1)S(1)}, u32[]{:S(2)}, u32[]{:S(2)}) collective-permute-start(bf16[3,320,128]{2,1,0:T(8,128)(2,1)S(1)} %get-tuple-element.53), channel_id=1, source_target_pairs={{0,1},{1,2},{2,3},{3,4},{4,5},{5,6},{6,7},{7,0},{8,9},{9,10},{10,1... | collective-permute-start | bytes 737288 | tf_op jit(solution)/shard_map/ppermute | solution.py:226
  55.3 25.9 %collective-permute-start.3 = (bf16[3,320,128]{2,1,0:T(8,128)(2,1)S(1)}, bf16[3,320,128]{2,1,0:T(8,128)(2,1)S(1)}, u32[]{:S(2)}, u32[]{:S(2)}) collective-permute-start(bf16[3,320,128]{2,1,0:T(8,128)(2,1)S(1)} %get-tuple-element.54), channel_id=1, source_target_pairs={{0,2},{1,3},{2,4},{3,5},{4,6},{5,7},{6,0},{7,1},{8,10},{9,11},{10,... | collective-permute-start | bytes 737288 | tf_op jit(solution)/shard_map/ppermute | solution.py:226
  59.8 35.4 %collective-permute-start.4 = (bf16[3,320,128]{2,1,0:T(8,128)(2,1)S(1)}, bf16[3,320,128]{2,1,0:T(8,128)(2,1)S(1)}, u32[]{:S(2)}, u32[]{:S(2)}) collective-permute-start(bf16[3,320,128]{2,1,0:T(8,128)(2,1)S(1)} %get-tuple-element.55), channel_id=1, source_target_pairs={{0,3},{1,4},{2,5},{3,6},{4,7},{5,0},{6,1},{7,2},{8,11},{9,12},{10,... | collective-permute-start | bytes 737288 | tf_op jit(solution)/shard_map/ppermute | solution.py:226
  61.7 33.5 %collective-permute-start.12 = (bf16[3,320,128]{2,1,0:T(8,128)(2,1)S(1)}, bf16[3,320,128]{2,1,0:T(8,128)(2,1)S(1)}, u32[]{:S(2)}, u32[]{:S(2)}) collective-permute-start(bf16[3,320,128]{2,1,0:T(8,128)(2,1)S(1)} %get-tuple-element.80), channel_id=1, source_target_pairs={{0,5},{1,6},{2,7},{3,0},{4,1},{5,2},{6,3},{7,4},{8,13},{9,14},{10,... | collective-permute-start | bytes 737288 | tf_op jit(solution)/shard_map/ppermute | solution.py:226
  64.8 30.4 %collective-permute-start.13 = (bf16[3,320,128]{2,1,0:T(8,128)(2,1)S(1)}, bf16[3,320,128]{2,1,0:T(8,128)(2,1)S(1)}, u32[]{:S(2)}, u32[]{:S(2)}) collective-permute-start(bf16[3,320,128]{2,1,0:T(8,128)(2,1)S(1)} %get-tuple-element.81), channel_id=1, source_target_pairs={{0,6},{1,7},{2,0},{3,1},{4,2},{5,3},{6,4},{7,5},{8,14},{9,15},{10,... | collective-permute-start | bytes 737288 | tf_op jit(solution)/shard_map/ppermute | solution.py:226
  66.0 33.1 %collective-permute-start.14 = (bf16[3,320,128]{2,1,0:T(8,128)(2,1)S(1)}, bf16[3,320,128]{2,1,0:T(8,128)(2,1)S(1)}, u32[]{:S(2)}, u32[]{:S(2)}) collective-permute-start(bf16[3,320,128]{2,1,0:T(8,128)(2,1)S(1)} %get-tuple-element.82), channel_id=1, source_target_pairs={{0,7},{1,0},{2,1},{3,2},{4,3},{5,4},{6,5},{7,6},{8,15},{9,8},{10,9... | collective-permute-start | bytes 737288 | tf_op jit(solution)/shard_map/ppermute | solution.py:226
  67.7 11.7 %copy-start.2 = (bf16[1,320,3072]{2,1,0:T(8,128)(2,1)S(1)}, bf16[1,320,3072]{2,1,0:T(8,128)(2,1)}, u32[]{:S(2)}) copy-start(bf16[1,320,3072]{2,1,0:T(8,128)(2,1)} %refs_2_.9) | copy-start | bytes 5898244
  81.1 26.2 %collective-permute-start.11 = (bf16[3,320,128]{2,1,0:T(8,128)(2,1)S(1)}, bf16[3,320,128]{2,1,0:T(8,128)(2,1)S(1)}, u32[]{:S(2)}, u32[]{:S(2)}) collective-permute-start(bf16[3,320,128]{2,1,0:T(8,128)(2,1)S(1)} %pack_second.3), channel_id=1, source_target_pairs={{0,4},{1,5},{2,6},{3,7},{4,0},{5,1},{6,2},{7,3},{8,12},{9,13},{10,... | collective-permute-start | bytes 737288 | tf_op jit(solution)/shard_map/ppermute | solution.py:226
  110.1 25.3 %collective-permute-start.17 = (bf16[2,320,128]{2,1,0:T(8,128)(2,1)S(1)}, bf16[2,320,128]{2,1,0:T(8,128)(2,1)S(1)}, u32[]{:S(2)}, u32[]{:S(2)}) collective-permute-start(bf16[2,320,128]{2,1,0:T(8,128)(2,1)S(1)} %get-tuple-element.86), channel_id=1, source_target_pairs={{0,5},{1,6},{2,7},{3,0},{4,1},{5,2},{6,3},{7,4},{8,13},{9,14},{10,... | collective-permute-start | bytes 491528 | tf_op jit(solution)/shard_map/ppermute | solution.py:226
  110.2 25.2 %collective-permute-start.18 = (bf16[2,320,128]{2,1,0:T(8,128)(2,1)S(1)}, bf16[2,320,128]{2,1,0:T(8,128)(2,1)S(1)}, u32[]{:S(2)}, u32[]{:S(2)}) collective-permute-start(bf16[2,320,128]{2,1,0:T(8,128)(2,1)S(1)} %get-tuple-element.87), channel_id=1, source_target_pairs={{0,4},{1,5},{2,6},{3,7},{4,0},{5,1},{6,2},{7,3},{8,12},{9,13},{10,... | collective-permute-start | bytes 491528 | tf_op jit(solution)/shard_map/ppermute | solution.py:226
  117.1 18.3 %collective-permute-start.16 = (bf16[2,320,128]{2,1,0:T(8,128)(2,1)S(1)}, bf16[2,320,128]{2,1,0:T(8,128)(2,1)S(1)}, u32[]{:S(2)}, u32[]{:S(2)}) collective-permute-start(bf16[2,320,128]{2,1,0:T(8,128)(2,1)S(1)} %get-tuple-element.85), channel_id=1, source_target_pairs={{0,6},{1,7},{2,0},{3,1},{4,2},{5,3},{6,4},{7,5},{8,14},{9,15},{10,... | collective-permute-start | bytes 491528 | tf_op jit(solution)/shard_map/ppermute | solution.py:226
  117.2 18.2 %collective-permute-start.19 = (bf16[2,320,128]{2,1,0:T(8,128)(2,1)S(1)}, bf16[2,320,128]{2,1,0:T(8,128)(2,1)S(1)}, u32[]{:S(2)}, u32[]{:S(2)}) collective-permute-start(bf16[2,320,128]{2,1,0:T(8,128)(2,1)S(1)} %get-tuple-element.88), channel_id=1, source_target_pairs={{0,3},{1,4},{2,5},{3,6},{4,7},{5,0},{6,1},{7,2},{8,11},{9,12},{10,... | collective-permute-start | bytes 491528 | tf_op jit(solution)/shard_map/ppermute | solution.py:226
  125.2 28.2 %copy-start.3 = (bf16[1,320,3072]{2,1,0:T(8,128)(2,1)S(1)}, bf16[1,320,3072]{2,1,0:T(8,128)(2,1)}, u32[]{:S(2)}) copy-start(bf16[1,320,3072]{2,1,0:T(8,128)(2,1)} %refs_0_.11) | copy-start | bytes 5898244
  125.2 13.1 %collective-permute-start.15 = (bf16[2,320,128]{2,1,0:T(8,128)(2,1)S(1)}, bf16[2,320,128]{2,1,0:T(8,128)(2,1)S(1)}, u32[]{:S(2)}, u32[]{:S(2)}) collective-permute-start(bf16[2,320,128]{2,1,0:T(8,128)(2,1)S(1)} %get-tuple-element.84), channel_id=1, source_target_pairs={{0,7},{1,0},{2,1},{3,2},{4,3},{5,4},{6,5},{7,6},{8,15},{9,8},{10,9... | collective-permute-start | bytes 491528 | tf_op jit(solution)/shard_map/ppermute | solution.py:226
  135.4 9.2 %collective-permute-start.20 = (bf16[2,320,128]{2,1,0:T(8,128)(2,1)S(1)}, bf16[2,320,128]{2,1,0:T(8,128)(2,1)S(1)}, u32[]{:S(2)}, u32[]{:S(2)}) collective-permute-start(bf16[2,320,128]{2,1,0:T(8,128)(2,1)S(1)} %get-tuple-element.89), channel_id=1, source_target_pairs={{0,2},{1,3},{2,4},{3,5},{4,6},{5,7},{6,0},{7,1},{8,10},{9,11},{10,... | collective-permute-start | bytes 491528 | tf_op jit(solution)/shard_map/ppermute | solution.py:226
  135.4 11.1 %collective-permute-start.21 = (bf16[2,320,128]{2,1,0:T(8,128)(2,1)S(1)}, bf16[2,320,128]{2,1,0:T(8,128)(2,1)S(1)}, u32[]{:S(2)}, u32[]{:S(2)}) collective-permute-start(bf16[2,320,128]{2,1,0:T(8,128)(2,1)S(1)} %get-tuple-element.90), channel_id=1, source_target_pairs={{0,1},{1,2},{2,3},{3,4},{4,5},{5,6},{6,7},{7,0},{8,9},{9,10},{10,1... | collective-permute-start | bytes 491528 | tf_op jit(solution)/shard_map/ppermute | solution.py:226
  135.5 18.0 %collective-permute-start.22 = (bf16[4,320,128]{2,1,0:T(8,128)(2,1)S(1)}, bf16[4,320,128]{2,1,0:T(8,128)(2,1)S(1)}, u32[]{:S(2)}, u32[]{:S(2)}) collective-permute-start(bf16[4,320,128]{2,1,0:T(8,128)(2,1)S(1)} %join.3), channel_id=1, source_target_pairs={{0,128},{8,136},{16,144},{24,152},{32,160},{40,168},{48,176},{56,1... | collective-permute-start | bytes 983048 | tf_op jit(solution)/shard_map/ppermute | solution.py:233
  144.7 6.9 %collective-permute-start.23 = (bf16[2,320,128]{2,1,0:T(8,128)(2,1)S(1)}, bf16[2,320,128]{2,1,0:T(8,128)(2,1)S(1)}, u32[]{:S(2)}, u32[]{:S(2)}) collective-permute-start(bf16[2,320,128]{2,1,0:T(8,128)(2,1)S(1)} %join.4), channel_id=1, source_target_pairs={{0,128},{8,136},{16,144},{24,152},{32,160},{40,168},{48,176},{56,1... | collective-permute-start | bytes 491528 | tf_op jit(solution)/shard_map/ppermute | solution.py:233
  146.5 6.9 %collective-permute-start.24 = (bf16[2,320,128]{2,1,0:T(8,128)(2,1)S(1)}, bf16[2,320,128]{2,1,0:T(8,128)(2,1)S(1)}, u32[]{:S(2)}, u32[]{:S(2)}) collective-permute-start(bf16[2,320,128]{2,1,0:T(8,128)(2,1)S(1)} %join.5), channel_id=1, source_target_pairs={{0,128},{8,136},{16,144},{24,152},{32,160},{40,168},{48,176},{56,1... | collective-permute-start | bytes 491528 | tf_op jit(solution)/shard_map/ppermute | solution.py:233

commit v5 on v4

--- a/solution.py
+++ b/solution.py
@@ -292,7 +292,8 @@
     )(*ordered((assignment, timestep, plan), first_in[order[2]]))
 
     second_in = [None] * pieces
-    early, late = [*order[:-1], 0], order[-1:]
+    one, last, two, next_last, three, third_last, middle = order
+    early, late = [last, two, next_last, three, third_last, middle, 0], [one]
     for offset, value in zip(early, pack_second(early, sources)):
         second_in[offset] = forward(value, offset)
 
@@ -306,7 +307,7 @@
         compiler_params=SHARED,
         cost_estimate=cost(pieces),
         name="attend_first",
-    )(*ordered(first_in, second_in[order[0]]))
+    )(*ordered(first_in, second_in[last]))
 
     for offset, value in zip(late, pack_second(late, ordered(sources, first_result))):
         second_in[offset] = forward(value, offset)

time: 158 us -> 155 us (0.981)
  waiting for transfers between devices: 57.3 us -> 40.2 us
  starting transfers between devices: 55.5 us -> 71 us
    ppermute x21, waiting for transfers between devices: 45.6 us -> 24.7 us  [forward(): lax.ppermute(value, 'seq', [(s, (s + offset) % pieces) for s in range(pie...]
    ppermute x21, starting transfers between devices: 45.7 us -> 58.8 us  [forward(): lax.ppermute(value, 'seq', [(s, (s + offset) % pieces) for s in range(pie...]
    ppermute x4, waiting for transfers between devices: 11.7 us -> 15.5 us  [across(): return lax.ppermute(value, 'batch', [(s, s ^ mask) for s in range(slots)])]
    ppermute x4, starting transfers between devices: 9.83 us -> 12.2 us  [across(): return lax.ppermute(value, 'batch', [(s, s ^ mask) for s in range(slots)])]
  transfers between devices with their start and end apart: 25 -> 25, of which waited for: 10 -> 9; matrix products, arithmetic and copies ran while one was open for 0% -> 0% of each run, Pallas kernels for 21% -> 22%
where the time goes in v5:
time: 155 us; the launch traced here: 154 us
  starting transfers between devices  71 us (46%)
  Pallas kernels  41 us (26%)
  waiting for transfers between devices  40.2 us (26%)
  local copies, waits for them, and re-layouts  1.57 us (1%)
    ppermute x21, starting transfers between devices, forward(): lax.ppermute(value, 'seq', [(s, (s + offset) % pieces) for s in range(pie...  58.8 us
    ppermute x21, waiting for transfers between devices, forward(): lax.ppermute(value, 'seq', [(s, (s + offset) % pieces) for s in range(pie...  24.7 us
    ppermute x4, waiting for transfers between devices, across(): return lax.ppermute(value, 'batch', [(s, s ^ mask) for s in range(slots)])  15.5 us
    ppermute x4, starting transfers between devices, across(): return lax.ppermute(value, 'batch', [(s, s ^ mask) for s in range(slots)])  12.2 us
    pallas_call x1, Pallas kernels, body(): pl.pallas_call(functools.partial(first_kernel, pieces, rows), out_shape=s...  11.7 us
    pallas_call x4, Pallas kernels, body(): pl.pallas_call(functools.partial(second_kernel, pieces, rows, offsets), o...  11.1 us
    pallas_call x4, Pallas kernels, pack_first(): pl.pallas_call(functools.partial(pack_kernel, pieces, offsets), out_shape...  7.58 us
    pallas_call x2, Pallas kernels, pack_second(): pl.pallas_call(functools.partial(pack_second_kernel, pieces, offsets), ou...  4.15 us
  transfers between devices with their start and end apart: 25, of which 9 were waited for; matrix products, arithmetic and copies ran while one was open for 0% of the time, Pallas kernels for 22%

profile of v5, /device:TPU:34, one launch (start us, length us, event | category | flops | bytes accessed | tf_op | source)
XLA Modules:
  0.0 154.1 jit_solution(3573165092091076791)
XLA Ops:
  0.0 2.8 %pack_far.1 = bf16[3,320,1024]{2,1,0:T(8,128)(2,1)} custom-call(bf16[1,320,3072]{2,1,0:T(8,128)(2,1)} %refs_0_.10, bf16[1,320,3072]{2,1,0:T(8,128)(2,1)} %refs_1_.9, bf16[1,320,3072]{2,1,0:T(8,128)(2,1)} %refs_2_.9), custom_call_target="tpu_custom_call" | custom-call | tf_op jit(solution)/shard_map/pack_far/pallas_call | solution.py:246
  2.8 3.3 %collective-permute-start.1 = (bf16[3,320,1024]{2,1,0:T(8,128)(2,1)}, bf16[3,320,1024]{2,1,0:T(8,128)(2,1)}, u32[]{:S(2)}, u32[]{:S(2)}) collective-permute-start(bf16[3,320,1024]{2,1,0:T(8,128)(2,1)} %pack_far.1), channel_id=1, source_target_pairs={{0,128},{8,136},{16,144},{24,152},{32,160},{40,168},{48,176},{56,1... | collective-permute-start | bytes 5898248 | tf_op jit(solution)/shard_map/ppermute | solution.py:233
  6.1 2.5 %pack_first.4 = (bf16[3,320,128]{2,1,0:T(8,128)(2,1)}, bf16[3,320,128]{2,1,0:T(8,128)(2,1)}, bf16[3,320,128]{2,1,0:T(8,128)(2,1)}, bf16[3,320,128]{2,1,0:T(8,128)(2,1)}, bf16[3,320,128]{2,1,0:T(8,128)(2,1)}) custom-call(bf16[1,320,3072]{2,1,0:T(8,128)(2,1)} %refs_0_.10, bf16[1,320,3072]{2,1,0:T(8,128)(2,1)} %refs_1_.9, bf16[1,320,3072]{2,1,0:T(8,128)(2,1)} %refs_2_.9), custom_call_target="tpu_custom_call" | custom-call | tf_op jit(solution)/shard_map/pack_first/pallas_call | solution.py:260
  8.6 3.3 %collective-permute-start = (bf16[3,320,128]{2,1,0:T(8,128)(2,1)}, bf16[3,320,128]{2,1,0:T(8,128)(2,1)S(1)}, u32[]{:S(2)}, u32[]{:S(2)}) collective-permute-start(bf16[3,320,128]{2,1,0:T(8,128)(2,1)} %get-tuple-element.48), channel_id=1, source_target_pairs={{0,2},{1,3},{2,4},{3,5},{4,6},{5,7},{6,0},{7,1},{8,10},{9,11},{10,... | collective-permute-start | bytes 737288 | tf_op jit(solution)/shard_map/ppermute | solution.py:226
  12.0 3.1 %collective-permute-start.2 = (bf16[3,320,128]{2,1,0:T(8,128)(2,1)}, bf16[3,320,128]{2,1,0:T(8,128)(2,1)S(1)}, u32[]{:S(2)}, u32[]{:S(2)}) collective-permute-start(bf16[3,320,128]{2,1,0:T(8,128)(2,1)} %get-tuple-element.54), channel_id=1, source_target_pairs={{0,1},{1,2},{2,3},{3,4},{4,5},{5,6},{6,7},{7,0},{8,9},{9,10},{10,1... | collective-permute-start | bytes 737288 | tf_op jit(solution)/shard_map/ppermute | solution.py:226
  15.1 0.0 collective-permute-start.5
  15.1 1.1 collective-permute-start.7
  16.2 9.3 %collective-permute-done.refs_2_ = bf16[3,320,128]{2,1,0:T(8,128)(2,1)S(1)} collective-permute-done((bf16[3,320,128]{2,1,0:T(8,128)(2,1)}, bf16[3,320,128]{2,1,0:T(8,128)(2,1)S(1)}, u32[]{:S(2)}, u32[]{:S(2)}) %collective-permute-start) | collective-permute-done | bytes 245792 | tf_op jit(solution)/shard_map/ppermute | solution.py:226
  25.5 1.7 %pack_first.6 = bf16[3,320,128]{2,1,0:T(8,128)(2,1)} custom-call(bf16[1,320,3072]{2,1,0:T(8,128)(2,1)} %refs_0_.10, bf16[1,320,3072]{2,1,0:T(8,128)(2,1)} %refs_1_.9, bf16[1,320,3072]{2,1,0:T(8,128)(2,1)} %refs_2_.9), custom_call_target="tpu_custom_call" | custom-call | tf_op jit(solution)/shard_map/pack_first/pallas_call | solution.py:260
  27.2 5.3 %collective-permute-start.4 = (bf16[3,320,128]{2,1,0:T(8,128)(2,1)}, bf16[3,320,128]{2,1,0:T(8,128)(2,1)S(1)}, u32[]{:S(2)}, u32[]{:S(2)}) collective-permute-start(bf16[3,320,128]{2,1,0:T(8,128)(2,1)} %pack_first.6), channel_id=1, source_target_pairs={{0,4},{1,5},{2,6},{3,7},{4,0},{5,1},{6,2},{7,3},{8,12},{9,13},{10,... | collective-permute-start | bytes 737288 | tf_op jit(solution)/shard_map/ppermute | solution.py:226
  32.5 0.0 collective-permute-done.2.refs_1_
  32.5 1.7 %pack_first.5 = bf16[3,320,128]{2,1,0:T(8,128)(2,1)} custom-call(bf16[1,320,3072]{2,1,0:T(8,128)(2,1)} %refs_0_.10, bf16[1,320,3072]{2,1,0:T(8,128)(2,1)} %refs_1_.9, bf16[1,320,3072]{2,1,0:T(8,128)(2,1)} %refs_2_.9), custom_call_target="tpu_custom_call" | custom-call | tf_op jit(solution)/shard_map/pack_first/pallas_call | solution.py:260
  34.2 0.0 copy-start
  34.2 2.4 %collective-permute-start.3 = (bf16[3,320,128]{2,1,0:T(8,128)(2,1)}, bf16[3,320,128]{2,1,0:T(8,128)(2,1)S(1)}, u32[]{:S(2)}, u32[]{:S(2)}) collective-permute-start(bf16[3,320,128]{2,1,0:T(8,128)(2,1)} %pack_first.5), channel_id=1, source_target_pairs={{0,3},{1,4},{2,5},{3,6},{4,7},{5,0},{6,1},{7,2},{8,11},{9,12},{10,... | collective-permute-start | bytes 737288 | tf_op jit(solution)/shard_map/ppermute | solution.py:226
  36.6 0.0 collective-permute-done.5.refs_7_
  36.6 1.7 %pack_first.7 = bf16[3,320,128]{2,1,0:T(8,128)(2,1)} custom-call(bf16[1,320,3072]{2,1,0:T(8,128)(2,1)} %refs_0_.10, bf16[1,320,3072]{2,1,0:T(8,128)(2,1)} %refs_1_.9, bf16[1,320,3072]{2,1,0:T(8,128)(2,1)} %refs_2_.9), custom_call_target="tpu_custom_call" | custom-call | tf_op jit(solution)/shard_map/pack_first/pallas_call | solution.py:260
  38.3 2.8 %collective-permute-start.6 = (bf16[3,320,128]{2,1,0:T(8,128)(2,1)}, bf16[3,320,128]{2,1,0:T(8,128)(2,1)}, u32[]{:S(2)}, u32[]{:S(2)}) collective-permute-start(bf16[3,320,128]{2,1,0:T(8,128)(2,1)} %pack_first.7), channel_id=1, source_target_pairs={{0,5},{1,6},{2,7},{3,0},{4,1},{5,2},{6,3},{7,4},{8,13},{9,14},{10,... | collective-permute-start | bytes 737288 | tf_op jit(solution)/shard_map/ppermute | solution.py:226
  41.1 1.5 flag.1
  42.6 6.7 %collective-permute-done.1.refs_3_ = bf16[3,320,1024]{2,1,0:T(8,128)(2,1)} collective-permute-done((bf16[3,320,1024]{2,1,0:T(8,128)(2,1)}, bf16[3,320,1024]{2,1,0:T(8,128)(2,1)}, u32[]{:S(2)}, u32[]{:S(2)}) %collective-permute-start.1) | collective-permute-done | bytes 1966112 | tf_op jit(solution)/shard_map/ppermute | solution.py:233
  49.3 1.5 %copy-done.1 = bf16[1,320,3072]{2,1,0:T(8,128)(2,1)S(1)} copy-done((bf16[1,320,3072]{2,1,0:T(8,128)(2,1)S(1)}, bf16[1,320,3072]{2,1,0:T(8,128)(2,1)}, u32[]{:S(2)}) %copy-start.1) | copy-done | bytes 1966104
  50.8 2.5 %pack_second.2 = (bf16[3,320,128]{2,1,0:T(8,128)(2,1)S(1)}, bf16[3,320,128]{2,1,0:T(8,128)(2,1)S(1)}, bf16[3,320,128]{2,1,0:T(8,128)(2,1)S(1)}, bf16[3,320,128]{...) custom-call(s32[1]{0:T(128)} %flag.1, ...), custom_call_target="tpu_custom_call" | custom-call | tf_op jit(solution)/shard_map/pack_second/pallas_call | solution.py:270
  53.3 0.2 collective-permute-start.8
  53.5 0.0 collective-permute-done.7.refs_6_
  53.5 3.3 %collective-permute-start.10 = (bf16[3,320,128]{2,1,0:T(8,128)(2,1)S(1)}, bf16[3,320,128]{2,1,0:T(8,128)(2,1)S(1)}, u32[]{:S(2)}, u32[]{:S(2)}) collective-permute-start(bf16[3,320,128]{2,1,0:T(8,128)(2,1)S(1)} %get-tuple-element.78), channel_id=1, source_target_pairs={{0,2},{1,3},{2,4},{3,5},{4,6},{5,7},{6,0},{7,1},{8,10},{9,11},{10,... | collective-permute-start | bytes 737288 | tf_op jit(solution)/shard_map/ppermute | solution.py:226
  56.7 0.0 collective-permute-done.4.refs_4_
  56.7 4.9 %collective-permute-start.11 = (bf16[3,320,128]{2,1,0:T(8,128)(2,1)S(1)}, bf16[3,320,128]{2,1,0:T(8,128)(2,1)S(1)}, u32[]{:S(2)}, u32[]{:S(2)}) collective-permute-start(bf16[3,320,128]{2,1,0:T(8,128)(2,1)S(1)} %get-tuple-element.79), channel_id=1, source_target_pairs={{0,3},{1,4},{2,5},{3,6},{4,7},{5,0},{6,1},{7,2},{8,11},{9,12},{10,... | collective-permute-start | bytes 737288 | tf_op jit(solution)/shard_map/ppermute | solution.py:226
  61.7 0.0 collective-permute-done.3.refs_3_
  61.7 2.2 %collective-permute-start.12 = (bf16[3,320,128]{2,1,0:T(8,128)(2,1)S(1)}, bf16[3,320,128]{2,1,0:T(8,128)(2,1)S(1)}, u32[]{:S(2)}, u32[]{:S(2)}) collective-permute-start(bf16[3,320,128]{2,1,0:T(8,128)(2,1)S(1)} %get-tuple-element.80), channel_id=1, source_target_pairs={{0,4},{1,5},{2,6},{3,7},{4,0},{5,1},{6,2},{7,3},{8,12},{9,13},{10,... | collective-permute-start | bytes 737288 | tf_op jit(solution)/shard_map/ppermute | solution.py:226
  63.9 0.0 collective-permute-done.6.refs_5_
  63.9 3.3 %collective-permute-start.13 = (bf16[3,320,128]{2,1,0:T(8,128)(2,1)S(1)}, bf16[3,320,128]{2,1,0:T(8,128)(2,1)S(1)}, u32[]{:S(2)}, u32[]{:S(2)}) collective-permute-start(bf16[3,320,128]{2,1,0:T(8,128)(2,1)S(1)} %get-tuple-element.81), channel_id=1, source_target_pairs={{0,5},{1,6},{2,7},{3,0},{4,1},{5,2},{6,3},{7,4},{8,13},{9,14},{10,... | collective-permute-start | bytes 737288 | tf_op jit(solution)/shard_map/ppermute | solution.py:226
  67.2 0.0 collective-permute-done.8.refs_7_
  67.2 12.5 %collective-permute-start.14 = (bf16[3,320,128]{2,1,0:T(8,128)(2,1)S(1)}, bf16[3,320,128]{2,1,0:T(8,128)(2,1)S(1)}, u32[]{:S(2)}, u32[]{:S(2)}) collective-permute-start(bf16[3,320,128]{2,1,0:T(8,128)(2,1)S(1)} %get-tuple-element.82), channel_id=1, source_target_pairs={{0,6},{1,7},{2,0},{3,1},{4,2},{5,3},{6,4},{7,5},{8,14},{9,15},{10,... | collective-permute-start | bytes 737288 | tf_op jit(solution)/shard_map/ppermute | solution.py:226
  79.7 11.7 %attend_first.1.refs_8_ = bf16[2560,128]{1,0:T(8,128)(2,1)S(1)} custom-call(bf16[3,320,128]{2,1,0:T(8,128)(2,1)S(1)} %copy-done.4, bf16[3,320,128]{2,1,0:T(8,128)(2,1)S(1)} %collective-permute-done.2.refs_1_, bf16[3,320,128]{2,1,0:T(8,128)(2,1)S(1)} %collective-permute-done.refs_2_, bf16[3,320,128]{2,1,0:T(8,128)(2,1)S(1)} %collective-permute-done.3.refs_3_, ...), custom_call_target="tpu_custom_call" | custom-call | flops 3355443200 | bytes 2621440 | tf_op jit(solution)/shard_map/attend_first/pallas_call | solution.py:301
  91.4 1.7 %pack_second.3 = bf16[3,320,128]{2,1,0:T(8,128)(2,1)S(1)} custom-call(s32[1]{0:T(128)} %flag.1, bf16[1,320,3072]{2,1,0:T(8,128)(2,1)S(1)} %copy-done, bf16[1,320,3072]{2,1,0:T(8,128)(2,1)S(1)} %copy-done.1, bf16[1,320,3072]{2,1,0:T(8,128)(2,1)S(1)} %copy-done.2, bf16[3,320,1024]{2,1,0:T(8,128)(2,1)} %collective-permute-done.1.refs_3_), custom_call_target="tpu_custom_call" | custom-call | tf_op jit(solution)/shard_map/pack_second/pallas_call | solution.py:270
  93.1 0.0 collective-permute-done.10.refs_2_
  93.1 0.1 collective-permute-start.9
  93.2 0.5 collective-permute-done.11.refs_3_
  93.7 0.0 collective-permute-done.12.refs_4_
  93.7 5.1 %collective-permute-done.13.refs_5_ = bf16[3,320,128]{2,1,0:T(8,128)(2,1)S(1)} collective-permute-done((bf16[3,320,128]{2,1,0:T(8,128)(2,1)S(1)}, bf16[3,320,128]{2,1,0:T(8,128)(2,1)S(1)}, u32[]{:S(2)}, u32[]{:S(2)}) %collective-permute-start.13) | collective-permute-done | bytes 245792 | tf_op jit(solution)/shard_map/ppermute | solution.py:226
  98.8 0.0 collective-permute-done.14.refs_6_
  98.8 2.1 %collective-permute-done.9.refs_1_ = bf16[3,320,128]{2,1,0:T(8,128)(2,1)S(1)} collective-permute-done((bf16[3,320,128]{2,1,0:T(8,128)(2,1)S(1)}, bf16[3,320,128]{2,1,0:T(8,128)(2,1)S(1)}, u32[]{:S(2)}, u32[]{:S(2)}) %collective-permute-start.9) | collective-permute-done | bytes 245792 | tf_op jit(solution)/shard_map/ppermute | solution.py:226
  101.0 2.8 %attend_second.7 = (bf16[2,320,128]{2,1,0:T(8,128)(2,1)S(1)}, bf16[2,320,128]{2,1,0:T(8,128)(2,1)S(1)}) custom-call(bf16[3,320,128]{2,1,0:T(8,128)(2,1)S(1)} %get-tuple-element.52.refs_0_, bf16[3,320,128]{2,1,0:T(8,128)(2,1)S(1)} %collective-permute-done.9.refs_1_, bf16[3,320,128]{2,1,0:T(8,128)(2,1)S(1)} %collective-permute-done.10.refs_2_, ...), custom_call_target="tpu_custom_call" | custom-call | flops 838860800 | bytes 1638400 | tf_op jit(solution)/shard_map/attend_second/pallas_call | solution.py:320
  103.7 4.7 %collective-permute-start.17 = (bf16[2,320,128]{2,1,0:T(8,128)(2,1)S(1)}, bf16[2,320,128]{2,1,0:T(8,128)(2,1)S(1)}, u32[]{:S(2)}, u32[]{:S(2)}) collective-permute-start(bf16[2,320,128]{2,1,0:T(8,128)(2,1)S(1)} %get-tuple-element.86), channel_id=1, source_target_pairs={{0,5},{1,6},{2,7},{3,0},{4,1},{5,2},{6,3},{7,4},{8,13},{9,14},{10,... | collective-permute-start | bytes 491528 | tf_op jit(solution)/shard_map/ppermute | solution.py:226
  108.4 3.1 %collective-permute-start.18 = (bf16[2,320,128]{2,1,0:T(8,128)(2,1)S(1)}, bf16[2,320,128]{2,1,0:T(8,128)(2,1)S(1)}, u32[]{:S(2)}, u32[]{:S(2)}) collective-permute-start(bf16[2,320,128]{2,1,0:T(8,128)(2,1)S(1)} %get-tuple-element.87), channel_id=1, source_target_pairs={{0,4},{1,5},{2,6},{3,7},{4,0},{5,1},{6,2},{7,3},{8,12},{9,13},{10,... | collective-permute-start | bytes 491528 | tf_op jit(solution)/shard_map/ppermute | solution.py:226
  111.5 2.8 %attend_second.6 = (bf16[2,320,128]{2,1,0:T(8,128)(2,1)S(1)}, bf16[2,320,128]{2,1,0:T(8,128)(2,1)S(1)}) custom-call(bf16[3,320,128]{2,1,0:T(8,128)(2,1)S(1)} %get-tuple-element.52.refs_0_, bf16[3,320,128]{2,1,0:T(8,128)(2,1)S(1)} %collective-permute-done.9.refs_1_, bf16[3,320,128]{2,1,0:T(8,128)(2,1)S(1)} %collective-permute-done.10.refs_2_, ...), custom_call_target="tpu_custom_call" | custom-call | flops 838860800 | bytes 1638400 | tf_op jit(solution)/shard_map/attend_second/pallas_call | solution.py:320
  114.2 1.1 collective-permute-start.16
  115.3 1.7 %collective-permute-start.19 = (bf16[2,320,128]{2,1,0:T(8,128)(2,1)S(1)}, bf16[2,320,128]{2,1,0:T(8,128)(2,1)S(1)}, u32[]{:S(2)}, u32[]{:S(2)}) collective-permute-start(bf16[2,320,128]{2,1,0:T(8,128)(2,1)S(1)} %get-tuple-element.88), channel_id=1, source_target_pairs={{0,3},{1,4},{2,5},{3,6},{4,7},{5,0},{6,1},{7,2},{8,11},{9,12},{10,... | collective-permute-start | bytes 491528 | tf_op jit(solution)/shard_map/ppermute | solution.py:226
  117.0 2.8 %attend_second.5 = (bf16[2,320,128]{2,1,0:T(8,128)(2,1)S(1)}, bf16[2,320,128]{2,1,0:T(8,128)(2,1)S(1)}) custom-call(bf16[3,320,128]{2,1,0:T(8,128)(2,1)S(1)} %get-tuple-element.52.refs_0_, bf16[3,320,128]{2,1,0:T(8,128)(2,1)S(1)} %collective-permute-done.9.refs_1_, bf16[3,320,128]{2,1,0:T(8,128)(2,1)S(1)} %collective-permute-done.10.refs_2_, ...), custom_call_target="tpu_custom_call" | custom-call | flops 838860800 | bytes 1638400 | tf_op jit(solution)/shard_map/attend_second/pallas_call | solution.py:320
  119.8 0.0 copy-start.3
  119.8 1.8 %collective-permute-start.15 = (bf16[2,320,128]{2,1,0:T(8,128)(2,1)S(1)}, bf16[2,320,128]{2,1,0:T(8,128)(2,1)S(1)}, u32[]{:S(2)}, u32[]{:S(2)}) collective-permute-start(bf16[2,320,128]{2,1,0:T(8,128)(2,1)S(1)} %get-tuple-element.84), channel_id=1, source_target_pairs={{0,7},{1,0},{2,1},{3,2},{4,3},{5,4},{6,5},{7,6},{8,15},{9,8},{10,9... | collective-permute-start | bytes 491528 | tf_op jit(solution)/shard_map/ppermute | solution.py:226
  121.6 2.8 %attend_second.4 = (bf16[2,320,128]{2,1,0:T(8,128)(2,1)S(1)}, bf16[2,320,128]{2,1,0:T(8,128)(2,1)S(1)}) custom-call(bf16[3,320,128]{2,1,0:T(8,128)(2,1)S(1)} %get-tuple-element.52.refs_0_, bf16[3,320,128]{2,1,0:T(8,128)(2,1)S(1)} %collective-permute-done.9.refs_1_, bf16[3,320,128]{2,1,0:T(8,128)(2,1)S(1)} %collective-permute-done.10.refs_2_, ...), custom_call_target="tpu_custom_call" | custom-call | flops 838860800 | bytes 1638400 | tf_op jit(solution)/shard_map/attend_second/pallas_call | solution.py:320
  124.4 2.0 %collective-permute-start.20 = (bf16[2,320,128]{2,1,0:T(8,128)(2,1)S(1)}, bf16[2,320,128]{2,1,0:T(8,128)(2,1)S(1)}, u32[]{:S(2)}, u32[]{:S(2)}) collective-permute-start(bf16[2,320,128]{2,1,0:T(8,128)(2,1)S(1)} %get-tuple-element.89), channel_id=1, source_target_pairs={{0,2},{1,3},{2,4},{3,5},{4,6},{5,7},{6,0},{7,1},{8,10},{9,11},{10,... | collective-permute-start | bytes 491528 | tf_op jit(solution)/shard_map/ppermute | solution.py:226
  126.4 6.6 %collective-permute-done.18.refs_0_.refs_5_ = bf16[2,320,128]{2,1,0:T(8,128)(2,1)S(1)} collective-permute-done((bf16[2,320,128]{2,1,0:T(8,128)(2,1)S(1)}, bf16[2,320,128]{2,1,0:T(8,128)(2,1)S(1)}, u32[]{:S(2)}, u32[]{:S(2)}) %collective-permute-start.18) | collective-permute-done | bytes 163872 | tf_op jit(solution)/shard_map/ppermute | solution.py:226
  133.0 1.0 collective-permute-done.16.refs_3_
  134.0 3.7 %collective-permute-start.22 = (bf16[4,320,128]{2,1,0:T(8,128)(2,1)S(1)}, bf16[4,320,128]{2,1,0:T(8,128)(2,1)S(1)}, u32[]{:S(2)}, u32[]{:S(2)}) collective-permute-start(bf16[4,320,128]{2,1,0:T(8,128)(2,1)S(1)} %join.3), channel_id=1, source_target_pairs={{0,128},{8,136},{16,144},{24,152},{32,160},{40,168},{48,176},{56,1... | collective-permute-start | bytes 983048 | tf_op jit(solution)/shard_map/ppermute | solution.py:233
  137.7 0.0 collective-permute-done.15.refs_1_.refs_2_
  137.7 0.0 collective-permute-done.20.refs_0_.refs_7_
  137.7 2.2 %collective-permute-start.23 = (bf16[2,320,128]{2,1,0:T(8,128)(2,1)S(1)}, bf16[2,320,128]{2,1,0:T(8,128)(2,1)S(1)}, u32[]{:S(2)}, u32[]{:S(2)}) collective-permute-start(bf16[2,320,128]{2,1,0:T(8,128)(2,1)S(1)} %join.4), channel_id=1, source_target_pairs={{0,128},{8,136},{16,144},{24,152},{32,160},{40,168},{48,176},{56,1... | collective-permute-start | bytes 491528 | tf_op jit(solution)/shard_map/ppermute | solution.py:233
  139.8 0.0 collective-permute-done.21.refs_0_.refs_8_
  139.9 3.1 %collective-permute-start.24 = (bf16[2,320,128]{2,1,0:T(8,128)(2,1)S(1)}, bf16[2,320,128]{2,1,0:T(8,128)(2,1)S(1)}, u32[]{:S(2)}, u32[]{:S(2)}) collective-permute-start(bf16[2,320,128]{2,1,0:T(8,128)(2,1)S(1)} %join.5), channel_id=1, source_target_pairs={{0,128},{8,136},{16,144},{24,152},{32,160},{40,168},{48,176},{56,1... | collective-permute-start | bytes 491528 | tf_op jit(solution)/shard_map/ppermute | solution.py:233
  142.9 6.9 %collective-permute-done.23.refs_10_ = bf16[2,320,128]{2,1,0:T(8,128)(2,1)S(1)} collective-permute-done((bf16[2,320,128]{2,1,0:T(8,128)(2,1)S(1)}, bf16[2,320,128]{2,1,0:T(8,128)(2,1)S(1)}, u32[]{:S(2)}, u32[]{:S(2)}) %collective-permute-start.23) | collective-permute-done | bytes 163872 | tf_op jit(solution)/shard_map/ppermute | solution.py:233
  149.8 1.9 %collective-permute-done.24.refs_11_ = bf16[2,320,128]{2,1,0:T(8,128)(2,1)S(1)} collective-permute-done((bf16[2,320,128]{2,1,0:T(8,128)(2,1)S(1)}, bf16[2,320,128]{2,1,0:T(8,128)(2,1)S(1)}, u32[]{:S(2)}, u32[]{:S(2)}) %collective-permute-start.24) | collective-permute-done | bytes 163872 | tf_op jit(solution)/shard_map/ppermute | solution.py:233
  151.7 0.0 collective-permute-done.22.refs_9_
  151.7 2.2 %final.1 = bf16[1,320,3072]{2,1,0:T(8,128)(2,1)} custom-call(s32[1]{0:T(128)} %flag.1, bf16[1,320,3072]{2,1,0:T(8,128)(2,1)S(1)} %copy-done.3, bf16[2,320,128]{2,1,0:T(8,128)(2,1)S(1)} %get-tuple-element.83.refs_1_, bf16[2,320,128]{2,1,0:T(8,128)(2,1)S(1)} %collective-permute-done.15.refs_1_.refs_2_, ...), custom_call_target="tpu_custom_call" | custom-call | tf_op jit(solution)/shard_map/final/pallas_call | solution.py:352
  (13 shorter events, 0.1 us)
Async XLA Ops:
  2.8 46.5 %collective-permute-start.1 = (bf16[3,320,1024]{2,1,0:T(8,128)(2,1)}, bf16[3,320,1024]{2,1,0:T(8,128)(2,1)}, u32[]{:S(2)}, u32[]{:S(2)}) collective-permute-start(bf16[3,320,1024]{2,1,0:T(8,128)(2,1)} %pack_far.1), channel_id=1, source_target_pairs={{0,128},{8,136},{16,144},{24,152},{32,160},{40,168},{48,176},{56,1... | collective-permute-start | bytes 5898248 | tf_op jit(solution)/shard_map/ppermute | solution.py:233
  8.6 16.9 %collective-permute-start = (bf16[3,320,128]{2,1,0:T(8,128)(2,1)}, bf16[3,320,128]{2,1,0:T(8,128)(2,1)S(1)}, u32[]{:S(2)}, u32[]{:S(2)}) collective-permute-start(bf16[3,320,128]{2,1,0:T(8,128)(2,1)} %get-tuple-element.48), channel_id=1, source_target_pairs={{0,2},{1,3},{2,4},{3,5},{4,6},{5,7},{6,0},{7,1},{8,10},{9,11},{10,... | collective-permute-start | bytes 737288 | tf_op jit(solution)/shard_map/ppermute | solution.py:226
  12.0 20.6 %collective-permute-start.2 = (bf16[3,320,128]{2,1,0:T(8,128)(2,1)}, bf16[3,320,128]{2,1,0:T(8,128)(2,1)S(1)}, u32[]{:S(2)}, u32[]{:S(2)}) collective-permute-start(bf16[3,320,128]{2,1,0:T(8,128)(2,1)} %get-tuple-element.54), channel_id=1, source_target_pairs={{0,1},{1,2},{2,3},{3,4},{4,5},{5,6},{6,7},{7,0},{8,9},{9,10},{10,1... | collective-permute-start | bytes 737288 | tf_op jit(solution)/shard_map/ppermute | solution.py:226
  15.1 21.5 %collective-permute-start.5 = (bf16[3,320,128]{2,1,0:T(8,128)(2,1)}, bf16[3,320,128]{2,1,0:T(8,128)(2,1)S(1)}, u32[]{:S(2)}, u32[]{:S(2)}) collective-permute-start(bf16[3,320,128]{2,1,0:T(8,128)(2,1)} %get-tuple-element.61), channel_id=1, source_target_pairs={{0,7},{1,0},{2,1},{3,2},{4,3},{5,4},{6,5},{7,6},{8,15},{9,8},{10,9... | collective-permute-start | bytes 737288 | tf_op jit(solution)/shard_map/ppermute | solution.py:226
  15.1 38.4 %collective-permute-start.7 = (bf16[3,320,128]{2,1,0:T(8,128)(2,1)}, bf16[3,320,128]{2,1,0:T(8,128)(2,1)S(1)}, u32[]{:S(2)}, u32[]{:S(2)}) collective-permute-start(bf16[3,320,128]{2,1,0:T(8,128)(2,1)} %get-tuple-element.65), channel_id=1, source_target_pairs={{0,6},{1,7},{2,0},{3,1},{4,2},{5,3},{6,4},{7,5},{8,14},{9,15},{10,... | collective-permute-start | bytes 737288 | tf_op jit(solution)/shard_map/ppermute | solution.py:226
  27.2 29.5 %collective-permute-start.4 = (bf16[3,320,128]{2,1,0:T(8,128)(2,1)}, bf16[3,320,128]{2,1,0:T(8,128)(2,1)S(1)}, u32[]{:S(2)}, u32[]{:S(2)}) collective-permute-start(bf16[3,320,128]{2,1,0:T(8,128)(2,1)} %pack_first.6), channel_id=1, source_target_pairs={{0,4},{1,5},{2,6},{3,7},{4,0},{5,1},{6,2},{7,3},{8,12},{9,13},{10,... | collective-permute-start | bytes 737288 | tf_op jit(solution)/shard_map/ppermute | solution.py:226
  34.2 15.1 %copy-start = (bf16[1,320,3072]{2,1,0:T(8,128)(2,1)S(1)}, bf16[1,320,3072]{2,1,0:T(8,128)(2,1)}, u32[]{:S(2)}) copy-start(bf16[1,320,3072]{2,1,0:T(8,128)(2,1)} %refs_0_.10) | copy-start | bytes 5898244
  34.2 27.5 %collective-permute-start.3 = (bf16[3,320,128]{2,1,0:T(8,128)(2,1)}, bf16[3,320,128]{2,1,0:T(8,128)(2,1)S(1)}, u32[]{:S(2)}, u32[]{:S(2)}) collective-permute-start(bf16[3,320,128]{2,1,0:T(8,128)(2,1)} %pack_first.5), channel_id=1, source_target_pairs={{0,3},{1,4},{2,5},{3,6},{4,7},{5,0},{6,1},{7,2},{8,11},{9,12},{10,... | collective-permute-start | bytes 737288 | tf_op jit(solution)/shard_map/ppermute | solution.py:226
  38.3 25.6 %collective-permute-start.6 = (bf16[3,320,128]{2,1,0:T(8,128)(2,1)}, bf16[3,320,128]{2,1,0:T(8,128)(2,1)}, u32[]{:S(2)}, u32[]{:S(2)}) collective-permute-start(bf16[3,320,128]{2,1,0:T(8,128)(2,1)} %pack_first.7), channel_id=1, source_target_pairs={{0,5},{1,6},{2,7},{3,0},{4,1},{5,2},{6,3},{7,4},{8,13},{9,14},{10,... | collective-permute-start | bytes 737288 | tf_op jit(solution)/shard_map/ppermute | solution.py:226
  49.3 1.5 %copy-start.1 = (bf16[1,320,3072]{2,1,0:T(8,128)(2,1)S(1)}, bf16[1,320,3072]{2,1,0:T(8,128)(2,1)}, u32[]{:S(2)}) copy-start(bf16[1,320,3072]{2,1,0:T(8,128)(2,1)} %refs_1_.9) | copy-start | bytes 5898244
  50.8 28.9 %copy-start.4 = (bf16[3,320,128]{2,1,0:T(8,128)(2,1)S(1)}, bf16[3,320,128]{2,1,0:T(8,128)(2,1)}, u32[]{:S(2)}) copy-start(bf16[3,320,128]{2,1,0:T(8,128)(2,1)} %get-tuple-element.67.refs_0_) | copy-start | bytes 737284
  53.3 13.9 %collective-permute-start.8 = (bf16[3,320,128]{2,1,0:T(8,128)(2,1)S(1)}, bf16[3,320,128]{2,1,0:T(8,128)(2,1)S(1)}, u32[]{:S(2)}, u32[]{:S(2)}) collective-permute-start(bf16[3,320,128]{2,1,0:T(8,128)(2,1)S(1)} %get-tuple-element.66), channel_id=1, source_target_pairs={{0,7},{1,0},{2,1},{3,2},{4,3},{5,4},{6,5},{7,6},{8,15},{9,8},{10,9... | collective-permute-start | bytes 737288 | tf_op jit(solution)/shard_map/ppermute | solution.py:226
  53.5 39.7 %collective-permute-start.10 = (bf16[3,320,128]{2,1,0:T(8,128)(2,1)S(1)}, bf16[3,320,128]{2,1,0:T(8,128)(2,1)S(1)}, u32[]{:S(2)}, u32[]{:S(2)}) collective-permute-start(bf16[3,320,128]{2,1,0:T(8,128)(2,1)S(1)} %get-tuple-element.78), channel_id=1, source_target_pairs={{0,2},{1,3},{2,4},{3,5},{4,6},{5,7},{6,0},{7,1},{8,10},{9,11},{10,... | collective-permute-start | bytes 737288 | tf_op jit(solution)/shard_map/ppermute | solution.py:226
  56.7 36.9 %collective-permute-start.11 = (bf16[3,320,128]{2,1,0:T(8,128)(2,1)S(1)}, bf16[3,320,128]{2,1,0:T(8,128)(2,1)S(1)}, u32[]{:S(2)}, u32[]{:S(2)}) collective-permute-start(bf16[3,320,128]{2,1,0:T(8,128)(2,1)S(1)} %get-tuple-element.79), channel_id=1, source_target_pairs={{0,3},{1,4},{2,5},{3,6},{4,7},{5,0},{6,1},{7,2},{8,11},{9,12},{10,... | collective-permute-start | bytes 737288 | tf_op jit(solution)/shard_map/ppermute | solution.py:226
  61.7 32.0 %collective-permute-start.12 = (bf16[3,320,128]{2,1,0:T(8,128)(2,1)S(1)}, bf16[3,320,128]{2,1,0:T(8,128)(2,1)S(1)}, u32[]{:S(2)}, u32[]{:S(2)}) collective-permute-start(bf16[3,320,128]{2,1,0:T(8,128)(2,1)S(1)} %get-tuple-element.80), channel_id=1, source_target_pairs={{0,4},{1,5},{2,6},{3,7},{4,0},{5,1},{6,2},{7,3},{8,12},{9,13},{10,... | collective-permute-start | bytes 737288 | tf_op jit(solution)/shard_map/ppermute | solution.py:226
  63.9 34.9 %collective-permute-start.13 = (bf16[3,320,128]{2,1,0:T(8,128)(2,1)S(1)}, bf16[3,320,128]{2,1,0:T(8,128)(2,1)S(1)}, u32[]{:S(2)}, u32[]{:S(2)}) collective-permute-start(bf16[3,320,128]{2,1,0:T(8,128)(2,1)S(1)} %get-tuple-element.81), channel_id=1, source_target_pairs={{0,5},{1,6},{2,7},{3,0},{4,1},{5,2},{6,3},{7,4},{8,13},{9,14},{10,... | collective-permute-start | bytes 737288 | tf_op jit(solution)/shard_map/ppermute | solution.py:226
  67.2 31.6 %collective-permute-start.14 = (bf16[3,320,128]{2,1,0:T(8,128)(2,1)S(1)}, bf16[3,320,128]{2,1,0:T(8,128)(2,1)S(1)}, u32[]{:S(2)}, u32[]{:S(2)}) collective-permute-start(bf16[3,320,128]{2,1,0:T(8,128)(2,1)S(1)} %get-tuple-element.82), channel_id=1, source_target_pairs={{0,6},{1,7},{2,0},{3,1},{4,2},{5,3},{6,4},{7,5},{8,14},{9,15},{10,... | collective-permute-start | bytes 737288 | tf_op jit(solution)/shard_map/ppermute | solution.py:226
  79.7 11.7 %copy-start.2 = (bf16[1,320,3072]{2,1,0:T(8,128)(2,1)S(1)}, bf16[1,320,3072]{2,1,0:T(8,128)(2,1)}, u32[]{:S(2)}) copy-start(bf16[1,320,3072]{2,1,0:T(8,128)(2,1)} %refs_2_.9) | copy-start | bytes 5898244
  93.1 7.8 %collective-permute-start.9 = (bf16[3,320,128]{2,1,0:T(8,128)(2,1)S(1)}, bf16[3,320,128]{2,1,0:T(8,128)(2,1)S(1)}, u32[]{:S(2)}, u32[]{:S(2)}) collective-permute-start(bf16[3,320,128]{2,1,0:T(8,128)(2,1)S(1)} %pack_second.3), channel_id=1, source_target_pairs={{0,1},{1,2},{2,3},{3,4},{4,5},{5,6},{6,7},{7,0},{8,9},{9,10},{10,1... | collective-permute-start | bytes 737288 | tf_op jit(solution)/shard_map/ppermute | solution.py:226
  103.7 20.6 %collective-permute-start.17 = (bf16[2,320,128]{2,1,0:T(8,128)(2,1)S(1)}, bf16[2,320,128]{2,1,0:T(8,128)(2,1)S(1)}, u32[]{:S(2)}, u32[]{:S(2)}) collective-permute-start(bf16[2,320,128]{2,1,0:T(8,128)(2,1)S(1)} %get-tuple-element.86), channel_id=1, source_target_pairs={{0,5},{1,6},{2,7},{3,0},{4,1},{5,2},{6,3},{7,4},{8,13},{9,14},{10,... | collective-permute-start | bytes 491528 | tf_op jit(solution)/shard_map/ppermute | solution.py:226
  108.4 24.5 %collective-permute-start.18 = (bf16[2,320,128]{2,1,0:T(8,128)(2,1)S(1)}, bf16[2,320,128]{2,1,0:T(8,128)(2,1)S(1)}, u32[]{:S(2)}, u32[]{:S(2)}) collective-permute-start(bf16[2,320,128]{2,1,0:T(8,128)(2,1)S(1)} %get-tuple-element.87), channel_id=1, source_target_pairs={{0,4},{1,5},{2,6},{3,7},{4,0},{5,1},{6,2},{7,3},{8,12},{9,13},{10,... | collective-permute-start | bytes 491528 | tf_op jit(solution)/shard_map/ppermute | solution.py:226
  114.2 19.7 %collective-permute-start.16 = (bf16[2,320,128]{2,1,0:T(8,128)(2,1)S(1)}, bf16[2,320,128]{2,1,0:T(8,128)(2,1)S(1)}, u32[]{:S(2)}, u32[]{:S(2)}) collective-permute-start(bf16[2,320,128]{2,1,0:T(8,128)(2,1)S(1)} %get-tuple-element.85), channel_id=1, source_target_pairs={{0,6},{1,7},{2,0},{3,1},{4,2},{5,3},{6,4},{7,5},{8,14},{9,15},{10,... | collective-permute-start | bytes 491528 | tf_op jit(solution)/shard_map/ppermute | solution.py:226
  115.3 18.6 %collective-permute-start.19 = (bf16[2,320,128]{2,1,0:T(8,128)(2,1)S(1)}, bf16[2,320,128]{2,1,0:T(8,128)(2,1)S(1)}, u32[]{:S(2)}, u32[]{:S(2)}) collective-permute-start(bf16[2,320,128]{2,1,0:T(8,128)(2,1)S(1)} %get-tuple-element.88), channel_id=1, source_target_pairs={{0,3},{1,4},{2,5},{3,6},{4,7},{5,0},{6,1},{7,2},{8,11},{9,12},{10,... | collective-permute-start | bytes 491528 | tf_op jit(solution)/shard_map/ppermute | solution.py:226
  119.8 32.0 %copy-start.3 = (bf16[1,320,3072]{2,1,0:T(8,128)(2,1)S(1)}, bf16[1,320,3072]{2,1,0:T(8,128)(2,1)}, u32[]{:S(2)}) copy-start(bf16[1,320,3072]{2,1,0:T(8,128)(2,1)} %refs_0_.11) | copy-start | bytes 5898244
  119.8 17.8 %collective-permute-start.15 = (bf16[2,320,128]{2,1,0:T(8,128)(2,1)S(1)}, bf16[2,320,128]{2,1,0:T(8,128)(2,1)S(1)}, u32[]{:S(2)}, u32[]{:S(2)}) collective-permute-start(bf16[2,320,128]{2,1,0:T(8,128)(2,1)S(1)} %get-tuple-element.84), channel_id=1, source_target_pairs={{0,7},{1,0},{2,1},{3,2},{4,3},{5,4},{6,5},{7,6},{8,15},{9,8},{10,9... | collective-permute-start | bytes 491528 | tf_op jit(solution)/shard_map/ppermute | solution.py:226
  124.4 13.3 %collective-permute-start.20 = (bf16[2,320,128]{2,1,0:T(8,128)(2,1)S(1)}, bf16[2,320,128]{2,1,0:T(8,128)(2,1)S(1)}, u32[]{:S(2)}, u32[]{:S(2)}) collective-permute-start(bf16[2,320,128]{2,1,0:T(8,128)(2,1)S(1)} %get-tuple-element.89), channel_id=1, source_target_pairs={{0,2},{1,3},{2,4},{3,5},{4,6},{5,7},{6,0},{7,1},{8,10},{9,11},{10,... | collective-permute-start | bytes 491528 | tf_op jit(solution)/shard_map/ppermute | solution.py:226
  133.0 6.9 %collective-permute-start.21 = (bf16[2,320,128]{2,1,0:T(8,128)(2,1)S(1)}, bf16[2,320,128]{2,1,0:T(8,128)(2,1)S(1)}, u32[]{:S(2)}, u32[]{:S(2)}) collective-permute-start(bf16[2,320,128]{2,1,0:T(8,128)(2,1)S(1)} %get-tuple-element.90), channel_id=1, source_target_pairs={{0,1},{1,2},{2,3},{3,4},{4,5},{5,6},{6,7},{7,0},{8,9},{9,10},{10,1... | collective-permute-start | bytes 491528 | tf_op jit(solution)/shard_map/ppermute | solution.py:226
  134.0 17.7 %collective-permute-start.22 = (bf16[4,320,128]{2,1,0:T(8,128)(2,1)S(1)}, bf16[4,320,128]{2,1,0:T(8,128)(2,1)S(1)}, u32[]{:S(2)}, u32[]{:S(2)}) collective-permute-start(bf16[4,320,128]{2,1,0:T(8,128)(2,1)S(1)} %join.3), channel_id=1, source_target_pairs={{0,128},{8,136},{16,144},{24,152},{32,160},{40,168},{48,176},{56,1... | collective-permute-start | bytes 983048 | tf_op jit(solution)/shard_map/ppermute | solution.py:233
  137.7 12.1 %collective-permute-start.23 = (bf16[2,320,128]{2,1,0:T(8,128)(2,1)S(1)}, bf16[2,320,128]{2,1,0:T(8,128)(2,1)S(1)}, u32[]{:S(2)}, u32[]{:S(2)}) collective-permute-start(bf16[2,320,128]{2,1,0:T(8,128)(2,1)S(1)} %join.4), channel_id=1, source_target_pairs={{0,128},{8,136},{16,144},{24,152},{32,160},{40,168},{48,176},{56,1... | collective-permute-start | bytes 491528 | tf_op jit(solution)/shard_map/ppermute | solution.py:233
  139.9 11.9 %collective-permute-start.24 = (bf16[2,320,128]{2,1,0:T(8,128)(2,1)S(1)}, bf16[2,320,128]{2,1,0:T(8,128)(2,1)S(1)}, u32[]{:S(2)}, u32[]{:S(2)}) collective-permute-start(bf16[2,320,128]{2,1,0:T(8,128)(2,1)S(1)} %join.5), channel_id=1, source_target_pairs={{0,128},{8,136},{16,144},{24,152},{32,160},{40,168},{48,176},{56,1... | collective-permute-start | bytes 491528 | tf_op jit(solution)/shard_map/ppermute | solution.py:233

commit v6 on v5

--- a/solution.py
+++ b/solution.py
@@ -10,7 +10,7 @@
 
 HEAD_DIM = 128
 GROUPS = 3
-PACK = pltpu.CompilerParams(vmem_limit_bytes=48 << 20)
+PACK = pltpu.CompilerParams(vmem_limit_bytes=58 << 20)
 SHARED = pltpu.CompilerParams(vmem_limit_bytes=40 << 20)
 
 ANY = pl.BlockSpec(memory_space=pl.ANY)
@@ -294,8 +294,9 @@
     second_in = [None] * pieces
     one, last, two, next_last, three, third_last, middle = order
     early, late = [last, two, next_last, three, third_last, middle, 0], [one]
-    for offset, value in zip(early, pack_second(early, sources)):
-        second_in[offset] = forward(value, offset)
+    for offsets in (early[:2], early[2:]):
+        for offset, value in zip(offsets, pack_second(offsets, sources)):
+            second_in[offset] = forward(value, offset)
 
     score_buffers = [pltpu.VMEM((rows, pieces * rows), jnp.float32)] * 2
     first_result = pl.pallas_call(

time: 155 us -> 156 us (level)
  starting transfers between devices: 71 us -> 66.1 us
  waiting for transfers between devices: 40.2 us -> 45.1 us
  Pallas kernels: 41 us -> 43.9 us
    ppermute x21, waiting for transfers between devices: 24.7 us -> 30.3 us  [forward(): lax.ppermute(value, 'seq', [(s, (s + offset) % pieces) for s in range(pie...]
    pallas_call x2 -> x3, Pallas kernels: 4.15 us -> 8.2 us  [pack_second(): pl.pallas_call(functools.partial(pack_second_kernel, pieces, offsets), ou...]
    ppermute x21, starting transfers between devices: 58.8 us -> 55.9 us  [forward(): lax.ppermute(value, 'seq', [(s, (s + offset) % pieces) for s in range(pie...]
    ppermute x4, starting transfers between devices: 12.2 us -> 10.3 us  [across(): return lax.ppermute(value, 'batch', [(s, s ^ mask) for s in range(slots)])]
  transfers between devices with their start and end apart: 25 -> 25, of which waited for: 9 -> 10; matrix products, arithmetic and copies ran while one was open for 0% -> 0% of each run, Pallas kernels for 22% -> 23%
where the time goes in v6:
time: 156 us
  starting transfers between devices  66.1 us (42%)
  waiting for transfers between devices  45.1 us (29%)
  Pallas kernels  43.9 us (28%)
    ppermute x21, starting transfers between devices, forward(): lax.ppermute(value, 'seq', [(s, (s + offset) % pieces) for s in range(pie...  55.9 us
    ppermute x21, waiting for transfers between devices, forward(): lax.ppermute(value, 'seq', [(s, (s + offset) % pieces) for s in range(pie...  30.3 us
    ppermute x4, waiting for transfers between devices, across(): return lax.ppermute(value, 'batch', [(s, s ^ mask) for s in range(slots)])  14.8 us
    pallas_call x4, Pallas kernels, body(): pl.pallas_call(functools.partial(second_kernel, pieces, rows, offsets), o...  11.1 us
    pallas_call x1, Pallas kernels, body(): pl.pallas_call(functools.partial(first_kernel, pieces, rows), out_shape=s...  10.6 us
    ppermute x4, starting transfers between devices, across(): return lax.ppermute(value, 'batch', [(s, s ^ mask) for s in range(slots)])  10.3 us
    pallas_call x3, Pallas kernels, pack_second(): pl.pallas_call(functools.partial(pack_second_kernel, pieces, offsets), ou...  8.2 us
    pallas_call x4, Pallas kernels, pack_first(): pl.pallas_call(functools.partial(pack_kernel, pieces, offsets), out_shape...  7.6 us
  transfers between devices with their start and end apart: 25, of which 10 were waited for; matrix products, arithmetic and copies ran while one was open for 0% of the time, Pallas kernels for 23%

profile of v6, /device:TPU:34, one launch (start us, length us, event | category | flops | bytes accessed | tf_op | source)
XLA Modules:
  0.0 155.5 jit_solution(9295851491592633936)
XLA Ops:
  0.0 2.8 %pack_far.1 = bf16[3,320,1024]{2,1,0:T(8,128)(2,1)} custom-call(bf16[1,320,3072]{2,1,0:T(8,128)(2,1)} %refs_0_.12, bf16[1,320,3072]{2,1,0:T(8,128)(2,1)} %refs_1_.11, bf16[1,320,3072]{2,1,0:T(8,128)(2,1)} %refs_2_.11), custom_call_target="tpu_custom_call" | custom-call | tf_op jit(solution)/shard_map/pack_far/pallas_call | solution.py:246
  2.8 3.3 %collective-permute-start.1 = (bf16[3,320,1024]{2,1,0:T(8,128)(2,1)}, bf16[3,320,1024]{2,1,0:T(8,128)(2,1)}, u32[]{:S(2)}, u32[]{:S(2)}) collective-permute-start(bf16[3,320,1024]{2,1,0:T(8,128)(2,1)} %pack_far.1), channel_id=1, source_target_pairs={{0,128},{8,136},{16,144},{24,152},{32,160},{40,168},{48,176},{56,1... | collective-permute-start | bytes 5898248 | tf_op jit(solution)/shard_map/ppermute | solution.py:233
  6.1 2.5 %pack_first.4 = (bf16[3,320,128]{2,1,0:T(8,128)(2,1)}, bf16[3,320,128]{2,1,0:T(8,128)(2,1)}, bf16[3,320,128]{2,1,0:T(8,128)(2,1)}, bf16[3,320,128]{2,1,0:T(8,128)(2,1)}, bf16[3,320,128]{2,1,0:T(8,128)(2,1)}) custom-call(bf16[1,320,3072]{2,1,0:T(8,128)(2,1)} %refs_0_.12, bf16[1,320,3072]{2,1,0:T(8,128)(2,1)} %refs_1_.11, bf16[1,320,3072]{2,1,0:T(8,128)(2,1)} %refs_2_.11), custom_call_target="tpu_custom_call" | custom-call | tf_op jit(solution)/shard_map/pack_first/pallas_call | solution.py:260
  8.6 3.3 %collective-permute-start = (bf16[3,320,128]{2,1,0:T(8,128)(2,1)}, bf16[3,320,128]{2,1,0:T(8,128)(2,1)S(1)}, u32[]{:S(2)}, u32[]{:S(2)}) collective-permute-start(bf16[3,320,128]{2,1,0:T(8,128)(2,1)} %get-tuple-element.48), channel_id=1, source_target_pairs={{0,2},{1,3},{2,4},{3,5},{4,6},{5,7},{6,0},{7,1},{8,10},{9,11},{10,... | collective-permute-start | bytes 737288 | tf_op jit(solution)/shard_map/ppermute | solution.py:226
  12.0 3.1 %collective-permute-start.2 = (bf16[3,320,128]{2,1,0:T(8,128)(2,1)}, bf16[3,320,128]{2,1,0:T(8,128)(2,1)S(1)}, u32[]{:S(2)}, u32[]{:S(2)}) collective-permute-start(bf16[3,320,128]{2,1,0:T(8,128)(2,1)} %get-tuple-element.54), channel_id=1, source_target_pairs={{0,1},{1,2},{2,3},{3,4},{4,5},{5,6},{6,7},{7,0},{8,9},{9,10},{10,1... | collective-permute-start | bytes 737288 | tf_op jit(solution)/shard_map/ppermute | solution.py:226
  15.1 0.0 collective-permute-start.5
  15.1 1.1 collective-permute-start.7
  16.2 9.3 %collective-permute-done.refs_2_ = bf16[3,320,128]{2,1,0:T(8,128)(2,1)S(1)} collective-permute-done((bf16[3,320,128]{2,1,0:T(8,128)(2,1)}, bf16[3,320,128]{2,1,0:T(8,128)(2,1)S(1)}, u32[]{:S(2)}, u32[]{:S(2)}) %collective-permute-start) | collective-permute-done | bytes 245792 | tf_op jit(solution)/shard_map/ppermute | solution.py:226
  25.5 1.7 %pack_first.6 = bf16[3,320,128]{2,1,0:T(8,128)(2,1)} custom-call(bf16[1,320,3072]{2,1,0:T(8,128)(2,1)} %refs_0_.12, bf16[1,320,3072]{2,1,0:T(8,128)(2,1)} %refs_1_.11, bf16[1,320,3072]{2,1,0:T(8,128)(2,1)} %refs_2_.11), custom_call_target="tpu_custom_call" | custom-call | tf_op jit(solution)/shard_map/pack_first/pallas_call | solution.py:260
  27.2 5.3 %collective-permute-start.4 = (bf16[3,320,128]{2,1,0:T(8,128)(2,1)}, bf16[3,320,128]{2,1,0:T(8,128)(2,1)S(1)}, u32[]{:S(2)}, u32[]{:S(2)}) collective-permute-start(bf16[3,320,128]{2,1,0:T(8,128)(2,1)} %pack_first.6), channel_id=1, source_target_pairs={{0,4},{1,5},{2,6},{3,7},{4,0},{5,1},{6,2},{7,3},{8,12},{9,13},{10,... | collective-permute-start | bytes 737288 | tf_op jit(solution)/shard_map/ppermute | solution.py:226
  32.5 0.0 collective-permute-done.2.refs_1_
  32.5 1.7 %pack_first.5 = bf16[3,320,128]{2,1,0:T(8,128)(2,1)} custom-call(bf16[1,320,3072]{2,1,0:T(8,128)(2,1)} %refs_0_.12, bf16[1,320,3072]{2,1,0:T(8,128)(2,1)} %refs_1_.11, bf16[1,320,3072]{2,1,0:T(8,128)(2,1)} %refs_2_.11), custom_call_target="tpu_custom_call" | custom-call | tf_op jit(solution)/shard_map/pack_first/pallas_call | solution.py:260
  34.2 2.4 %collective-permute-start.3 = (bf16[3,320,128]{2,1,0:T(8,128)(2,1)}, bf16[3,320,128]{2,1,0:T(8,128)(2,1)S(1)}, u32[]{:S(2)}, u32[]{:S(2)}) collective-permute-start(bf16[3,320,128]{2,1,0:T(8,128)(2,1)} %pack_first.5), channel_id=1, source_target_pairs={{0,3},{1,4},{2,5},{3,6},{4,7},{5,0},{6,1},{7,2},{8,11},{9,12},{10,... | collective-permute-start | bytes 737288 | tf_op jit(solution)/shard_map/ppermute | solution.py:226
  36.6 0.0 collective-permute-done.5.refs_7_
  36.6 1.7 %pack_first.7 = bf16[3,320,128]{2,1,0:T(8,128)(2,1)} custom-call(bf16[1,320,3072]{2,1,0:T(8,128)(2,1)} %refs_0_.12, bf16[1,320,3072]{2,1,0:T(8,128)(2,1)} %refs_1_.11, bf16[1,320,3072]{2,1,0:T(8,128)(2,1)} %refs_2_.11), custom_call_target="tpu_custom_call" | custom-call | tf_op jit(solution)/shard_map/pack_first/pallas_call | solution.py:260
  38.3 2.8 %collective-permute-start.6 = (bf16[3,320,128]{2,1,0:T(8,128)(2,1)}, bf16[3,320,128]{2,1,0:T(8,128)(2,1)S(1)}, u32[]{:S(2)}, u32[]{:S(2)}) collective-permute-start(bf16[3,320,128]{2,1,0:T(8,128)(2,1)} %pack_first.7), channel_id=1, source_target_pairs={{0,5},{1,6},{2,7},{3,0},{4,1},{5,2},{6,3},{7,4},{8,13},{9,14},{10,... | collective-permute-start | bytes 737288 | tf_op jit(solution)/shard_map/ppermute | solution.py:226
  41.1 1.5 flag.1
  42.6 6.7 %collective-permute-done.1.refs_3_ = bf16[3,320,1024]{2,1,0:T(8,128)(2,1)} collective-permute-done((bf16[3,320,1024]{2,1,0:T(8,128)(2,1)}, bf16[3,320,1024]{2,1,0:T(8,128)(2,1)}, u32[]{:S(2)}, u32[]{:S(2)}) %collective-permute-start.1) | collective-permute-done | bytes 1966112 | tf_op jit(solution)/shard_map/ppermute | solution.py:233
  49.3 2.6 %pack_second.4 = (bf16[3,320,128]{2,1,0:T(8,128)(2,1)}, bf16[3,320,128]{2,1,0:T(8,128)(2,1)}) custom-call(s32[1]{0:T(128)} %flag.1, bf16[1,320,3072]{2,1,0:T(8,128)(2,1)} %refs_0_.12, bf16[1,320,3072]{2,1,0:T(8,128)(2,1)} %refs_1_.11, bf16[1,320,3072]{2,1,0:T(8,128)(2,1)} %refs_2_.11, bf16[3,320,1024]{2,1,0:T(8,128)(2,1)} %collective-permute-done.1.refs_3_), custom_call_target="tpu_custom_call" | custom-call | tf_op jit(solution)/shard_map/pack_second/pallas_call | solution.py:270
  51.9 0.2 collective-permute-start.8
  52.1 3.2 %pack_second.3 = (bf16[3,320,128]{2,1,0:T(8,128)(2,1)}, bf16[3,320,128]{2,1,0:T(8,128)(2,1)}, bf16[3,320,128]{2,1,0:T(8,128)(2,1)}, bf16[3,320,128]{2,1,0:T(8,128)(2,1)}, bf16[3,320,128]{2,1,0:T(8,128)(2,1)}) custom-call(s32[1]{0:T(128)} %flag.1, bf16[1,320,3072]{2,1,0:T(8,128)(2,1)} %refs_0_.12, bf16[1,320,3072]{2,1,0:T(8,128)(2,1)} %refs_1_.11, ...), custom_call_target="tpu_custom_call" | custom-call | tf_op jit(solution)/shard_map/pack_second/pallas_call | solution.py:270
  55.3 0.0 collective-permute-done.7.refs_6_
  55.3 5.9 %collective-permute-start.11 = (bf16[3,320,128]{2,1,0:T(8,128)(2,1)}, bf16[3,320,128]{2,1,0:T(8,128)(2,1)S(1)}, u32[]{:S(2)}, u32[]{:S(2)}) collective-permute-start(bf16[3,320,128]{2,1,0:T(8,128)(2,1)} %get-tuple-element.79), channel_id=1, source_target_pairs={{0,3},{1,4},{2,5},{3,6},{4,7},{5,0},{6,1},{7,2},{8,11},{9,12},{10,... | collective-permute-start | bytes 737288 | tf_op jit(solution)/shard_map/ppermute | solution.py:226
  61.2 0.0 collective-permute-done.4.refs_4_
  61.2 4.5 %collective-permute-start.12 = (bf16[3,320,128]{2,1,0:T(8,128)(2,1)}, bf16[3,320,128]{2,1,0:T(8,128)(2,1)S(1)}, u32[]{:S(2)}, u32[]{:S(2)}) collective-permute-start(bf16[3,320,128]{2,1,0:T(8,128)(2,1)} %get-tuple-element.80), channel_id=1, source_target_pairs={{0,4},{1,5},{2,6},{3,7},{4,0},{5,1},{6,2},{7,3},{8,12},{9,13},{10,... | collective-permute-start | bytes 737288 | tf_op jit(solution)/shard_map/ppermute | solution.py:226
  65.7 0.0 collective-permute-done.3.refs_3_
  65.7 1.9 %collective-permute-start.13 = (bf16[3,320,128]{2,1,0:T(8,128)(2,1)}, bf16[3,320,128]{2,1,0:T(8,128)(2,1)S(1)}, u32[]{:S(2)}, u32[]{:S(2)}) collective-permute-start(bf16[3,320,128]{2,1,0:T(8,128)(2,1)} %get-tuple-element.81), channel_id=1, source_target_pairs={{0,5},{1,6},{2,7},{3,0},{4,1},{5,2},{6,3},{7,4},{8,13},{9,14},{10,... | collective-permute-start | bytes 737288 | tf_op jit(solution)/shard_map/ppermute | solution.py:226
  67.6 0.0 collective-permute-done.6.refs_5_
  67.6 0.0 collective-permute-start.14
  67.6 0.0 collective-permute-done.8.refs_7_
  67.6 6.2 %collective-permute-start.10 = (bf16[3,320,128]{2,1,0:T(8,128)(2,1)S(1)}, bf16[3,320,128]{2,1,0:T(8,128)(2,1)S(1)}, u32[]{:S(2)}, u32[]{:S(2)}) collective-permute-start(bf16[3,320,128]{2,1,0:T(8,128)(2,1)S(1)} %copy-done.3), channel_id=1, source_target_pairs={{0,2},{1,3},{2,4},{3,5},{4,6},{5,7},{6,0},{7,1},{8,10},{9,11},{10,... | collective-permute-start | bytes 737288 | tf_op jit(solution)/shard_map/ppermute | solution.py:226
  73.8 10.6 %attend_first.1.refs_8_ = bf16[2560,128]{1,0:T(8,128)(2,1)S(1)} custom-call(bf16[3,320,128]{2,1,0:T(8,128)(2,1)S(1)} %copy-done.2, bf16[3,320,128]{2,1,0:T(8,128)(2,1)S(1)} %collective-permute-done.2.refs_1_, bf16[3,320,128]{2,1,0:T(8,128)(2,1)S(1)} %collective-permute-done.refs_2_, bf16[3,320,128]{2,1,0:T(8,128)(2,1)S(1)} %collective-permute-done.3.refs_3_, ...), custom_call_target="tpu_custom_call" | custom-call | flops 3355443200 | bytes 2621440 | tf_op jit(solution)/shard_map/attend_first/pallas_call | solution.py:302
  84.4 2.4 %pack_second.5 = bf16[3,320,128]{2,1,0:T(8,128)(2,1)} custom-call(s32[1]{0:T(128)} %flag.1, bf16[1,320,3072]{2,1,0:T(8,128)(2,1)} %refs_0_.12, bf16[1,320,3072]{2,1,0:T(8,128)(2,1)} %refs_1_.11, bf16[1,320,3072]{2,1,0:T(8,128)(2,1)} %refs_2_.11, bf16[3,320,1024]{2,1,0:T(8,128)(2,1)} %collective-permute-done.1.refs_3_), custom_call_target="tpu_custom_call" | custom-call | tf_op jit(solution)/shard_map/pack_second/pallas_call | solution.py:270
  86.8 0.0 collective-permute-done.11.refs_3_
  86.8 0.1 collective-permute-start.9
  86.9 0.0 collective-permute-done.12.refs_4_
  86.9 9.0 %collective-permute-done.13.refs_5_ = bf16[3,320,128]{2,1,0:T(8,128)(2,1)S(1)} collective-permute-done((bf16[3,320,128]{2,1,0:T(8,128)(2,1)}, bf16[3,320,128]{2,1,0:T(8,128)(2,1)S(1)}, u32[]{:S(2)}, u32[]{:S(2)}) %collective-permute-start.13) | collective-permute-done | bytes 245792 | tf_op jit(solution)/shard_map/ppermute | solution.py:226
  95.9 1.6 %collective-permute-done.14.refs_6_ = bf16[3,320,128]{2,1,0:T(8,128)(2,1)S(1)} collective-permute-done((bf16[3,320,128]{2,1,0:T(8,128)(2,1)}, bf16[3,320,128]{2,1,0:T(8,128)(2,1)S(1)}, u32[]{:S(2)}, u32[]{:S(2)}) %collective-permute-start.14) | collective-permute-done | bytes 245792 | tf_op jit(solution)/shard_map/ppermute | solution.py:226
  97.5 1.3 collective-permute-done.10.refs_2_
  98.9 4.3 %collective-permute-done.9.refs_1_ = bf16[3,320,128]{2,1,0:T(8,128)(2,1)S(1)} collective-permute-done((bf16[3,320,128]{2,1,0:T(8,128)(2,1)}, bf16[3,320,128]{2,1,0:T(8,128)(2,1)S(1)}, u32[]{:S(2)}, u32[]{:S(2)}) %collective-permute-start.9) | collective-permute-done | bytes 245792 | tf_op jit(solution)/shard_map/ppermute | solution.py:226
  103.1 2.8 %attend_second.7 = (bf16[2,320,128]{2,1,0:T(8,128)(2,1)S(1)}, bf16[2,320,128]{2,1,0:T(8,128)(2,1)S(1)}) custom-call(bf16[3,320,128]{2,1,0:T(8,128)(2,1)S(1)} %copy-done.1, bf16[3,320,128]{2,1,0:T(8,128)(2,1)S(1)} %collective-permute-done.9.refs_1_, bf16[3,320,128]{2,1,0:T(8,128)(2,1)S(1)} %collective-permute-done.10.refs_2_, ...), custom_call_target="tpu_custom_call" | custom-call | flops 838860800 | bytes 1638400 | tf_op jit(solution)/shard_map/attend_second/pallas_call | solution.py:321
  105.9 4.2 %collective-permute-start.17 = (bf16[2,320,128]{2,1,0:T(8,128)(2,1)S(1)}, bf16[2,320,128]{2,1,0:T(8,128)(2,1)S(1)}, u32[]{:S(2)}, u32[]{:S(2)}) collective-permute-start(bf16[2,320,128]{2,1,0:T(8,128)(2,1)S(1)} %get-tuple-element.86), channel_id=1, source_target_pairs={{0,5},{1,6},{2,7},{3,0},{4,1},{5,2},{6,3},{7,4},{8,13},{9,14},{10,... | collective-permute-start | bytes 491528 | tf_op jit(solution)/shard_map/ppermute | solution.py:226
  110.0 1.9 %collective-permute-start.18 = (bf16[2,320,128]{2,1,0:T(8,128)(2,1)S(1)}, bf16[2,320,128]{2,1,0:T(8,128)(2,1)S(1)}, u32[]{:S(2)}, u32[]{:S(2)}) collective-permute-start(bf16[2,320,128]{2,1,0:T(8,128)(2,1)S(1)} %get-tuple-element.87), channel_id=1, source_target_pairs={{0,4},{1,5},{2,6},{3,7},{4,0},{5,1},{6,2},{7,3},{8,12},{9,13},{10,... | collective-permute-start | bytes 491528 | tf_op jit(solution)/shard_map/ppermute | solution.py:226
  112.0 2.8 %attend_second.6 = (bf16[2,320,128]{2,1,0:T(8,128)(2,1)S(1)}, bf16[2,320,128]{2,1,0:T(8,128)(2,1)S(1)}) custom-call(bf16[3,320,128]{2,1,0:T(8,128)(2,1)S(1)} %copy-done.1, bf16[3,320,128]{2,1,0:T(8,128)(2,1)S(1)} %collective-permute-done.9.refs_1_, bf16[3,320,128]{2,1,0:T(8,128)(2,1)S(1)} %collective-permute-done.10.refs_2_, ...), custom_call_target="tpu_custom_call" | custom-call | flops 838860800 | bytes 1638400 | tf_op jit(solution)/shard_map/attend_second/pallas_call | solution.py:321
  114.7 1.0 collective-permute-start.16
  115.8 4.2 %collective-permute-start.19 = (bf16[2,320,128]{2,1,0:T(8,128)(2,1)S(1)}, bf16[2,320,128]{2,1,0:T(8,128)(2,1)S(1)}, u32[]{:S(2)}, u32[]{:S(2)}) collective-permute-start(bf16[2,320,128]{2,1,0:T(8,128)(2,1)S(1)} %get-tuple-element.88), channel_id=1, source_target_pairs={{0,3},{1,4},{2,5},{3,6},{4,7},{5,0},{6,1},{7,2},{8,11},{9,12},{10,... | collective-permute-start | bytes 491528 | tf_op jit(solution)/shard_map/ppermute | solution.py:226
  120.0 2.8 %attend_second.4 = (bf16[2,320,128]{2,1,0:T(8,128)(2,1)S(1)}, bf16[2,320,128]{2,1,0:T(8,128)(2,1)S(1)}) custom-call(bf16[3,320,128]{2,1,0:T(8,128)(2,1)S(1)} %copy-done.1, bf16[3,320,128]{2,1,0:T(8,128)(2,1)S(1)} %collective-permute-done.9.refs_1_, bf16[3,320,128]{2,1,0:T(8,128)(2,1)S(1)} %collective-permute-done.10.refs_2_, ...), custom_call_target="tpu_custom_call" | custom-call | flops 838860800 | bytes 1638400 | tf_op jit(solution)/shard_map/attend_second/pallas_call | solution.py:321
  122.7 0.0 copy-start
  122.8 1.6 %collective-permute-start.21 = (bf16[2,320,128]{2,1,0:T(8,128)(2,1)S(1)}, bf16[2,320,128]{2,1,0:T(8,128)(2,1)S(1)}, u32[]{:S(2)}, u32[]{:S(2)}) collective-permute-start(bf16[2,320,128]{2,1,0:T(8,128)(2,1)S(1)} %get-tuple-element.90), channel_id=1, source_target_pairs={{0,1},{1,2},{2,3},{3,4},{4,5},{5,6},{6,7},{7,0},{8,9},{9,10},{10,1... | collective-permute-start | bytes 491528 | tf_op jit(solution)/shard_map/ppermute | solution.py:226
  124.4 2.8 %attend_second.5 = (bf16[2,320,128]{2,1,0:T(8,128)(2,1)S(1)}, bf16[2,320,128]{2,1,0:T(8,128)(2,1)S(1)}) custom-call(bf16[3,320,128]{2,1,0:T(8,128)(2,1)S(1)} %copy-done.1, bf16[3,320,128]{2,1,0:T(8,128)(2,1)S(1)} %collective-permute-done.9.refs_1_, bf16[3,320,128]{2,1,0:T(8,128)(2,1)S(1)} %collective-permute-done.10.refs_2_, ...), custom_call_target="tpu_custom_call" | custom-call | flops 838860800 | bytes 1638400 | tf_op jit(solution)/shard_map/attend_second/pallas_call | solution.py:321
  127.1 0.0 collective-permute-done.17.refs_1_.refs_4_
  127.1 0.6 collective-permute-start.15
  127.7 3.2 %collective-permute-done.18.refs_0_.refs_5_ = bf16[2,320,128]{2,1,0:T(8,128)(2,1)S(1)} collective-permute-done((bf16[2,320,128]{2,1,0:T(8,128)(2,1)S(1)}, bf16[2,320,128]{2,1,0:T(8,128)(2,1)S(1)}, u32[]{:S(2)}, u32[]{:S(2)}) %collective-permute-start.18) | collective-permute-done | bytes 163872 | tf_op jit(solution)/shard_map/ppermute | solution.py:226
  130.9 5.5 %collective-permute-start.20 = (bf16[2,320,128]{2,1,0:T(8,128)(2,1)S(1)}, bf16[2,320,128]{2,1,0:T(8,128)(2,1)S(1)}, u32[]{:S(2)}, u32[]{:S(2)}) collective-permute-start(bf16[2,320,128]{2,1,0:T(8,128)(2,1)S(1)} %get-tuple-element.89), channel_id=1, source_target_pairs={{0,2},{1,3},{2,4},{3,5},{4,6},{5,7},{6,0},{7,1},{8,10},{9,11},{10,... | collective-permute-start | bytes 491528 | tf_op jit(solution)/shard_map/ppermute | solution.py:226
  136.5 2.6 %collective-permute-start.22 = (bf16[4,320,128]{2,1,0:T(8,128)(2,1)S(1)}, bf16[4,320,128]{2,1,0:T(8,128)(2,1)S(1)}, u32[]{:S(2)}, u32[]{:S(2)}) collective-permute-start(bf16[4,320,128]{2,1,0:T(8,128)(2,1)S(1)} %join.3), channel_id=1, source_target_pairs={{0,128},{8,136},{16,144},{24,152},{32,160},{40,168},{48,176},{56,1... | collective-permute-start | bytes 983048 | tf_op jit(solution)/shard_map/ppermute | solution.py:233
  139.1 0.0 collective-permute-done.21.refs_0_.refs_8_
  139.1 1.1 collective-permute-start.24
  140.2 0.0 collective-permute-done.15.refs_1_.refs_2_
  140.2 1.6 %collective-permute-done.20.refs_0_.refs_7_ = bf16[2,320,128]{2,1,0:T(8,128)(2,1)S(1)} collective-permute-done((bf16[2,320,128]{2,1,0:T(8,128)(2,1)S(1)}, bf16[2,320,128]{2,1,0:T(8,128)(2,1)S(1)}, u32[]{:S(2)}, u32[]{:S(2)}) %collective-permute-start.20) | collective-permute-done | bytes 163872 | tf_op jit(solution)/shard_map/ppermute | solution.py:226
  141.8 3.3 %collective-permute-start.23 = (bf16[2,320,128]{2,1,0:T(8,128)(2,1)S(1)}, bf16[2,320,128]{2,1,0:T(8,128)(2,1)S(1)}, u32[]{:S(2)}, u32[]{:S(2)}) collective-permute-start(bf16[2,320,128]{2,1,0:T(8,128)(2,1)S(1)} %join.4), channel_id=1, source_target_pairs={{0,128},{8,136},{16,144},{24,152},{32,160},{40,168},{48,176},{56,1... | collective-permute-start | bytes 491528 | tf_op jit(solution)/shard_map/ppermute | solution.py:233
  145.1 6.4 %collective-permute-done.24.refs_11_ = bf16[2,320,128]{2,1,0:T(8,128)(2,1)S(1)} collective-permute-done((bf16[2,320,128]{2,1,0:T(8,128)(2,1)S(1)}, bf16[2,320,128]{2,1,0:T(8,128)(2,1)S(1)}, u32[]{:S(2)}, u32[]{:S(2)}) %collective-permute-start.24) | collective-permute-done | bytes 163872 | tf_op jit(solution)/shard_map/ppermute | solution.py:233
  151.5 1.8 %collective-permute-done.23.refs_10_ = bf16[2,320,128]{2,1,0:T(8,128)(2,1)S(1)} collective-permute-done((bf16[2,320,128]{2,1,0:T(8,128)(2,1)S(1)}, bf16[2,320,128]{2,1,0:T(8,128)(2,1)S(1)}, u32[]{:S(2)}, u32[]{:S(2)}) %collective-permute-start.23) | collective-permute-done | bytes 163872 | tf_op jit(solution)/shard_map/ppermute | solution.py:233
  153.2 0.0 collective-permute-done.22.refs_9_
  153.2 2.1 %final.1 = bf16[1,320,3072]{2,1,0:T(8,128)(2,1)} custom-call(s32[1]{0:T(128)} %flag.1, bf16[1,320,3072]{2,1,0:T(8,128)(2,1)S(1)} %copy-done, bf16[2,320,128]{2,1,0:T(8,128)(2,1)S(1)} %get-tuple-element.83.refs_1_, bf16[2,320,128]{2,1,0:T(8,128)(2,1)S(1)} %collective-permute-done.15.refs_1_.refs_2_, bf16[2,320,128]{2,1,0:T(8,128)(2,1)S(1)} %collective-permute-done.16.refs_3_, ...), custom_call_target="tpu_custom_call" | custom-call | tf_op jit(solution)/shard_map/final/pallas_call | solution.py:353
  (12 shorter events, 0.1 us)
Async XLA Ops:
  2.8 46.5 %collective-permute-start.1 = (bf16[3,320,1024]{2,1,0:T(8,128)(2,1)}, bf16[3,320,1024]{2,1,0:T(8,128)(2,1)}, u32[]{:S(2)}, u32[]{:S(2)}) collective-permute-start(bf16[3,320,1024]{2,1,0:T(8,128)(2,1)} %pack_far.1), channel_id=1, source_target_pairs={{0,128},{8,136},{16,144},{24,152},{32,160},{40,168},{48,176},{56,1... | collective-permute-start | bytes 5898248 | tf_op jit(solution)/shard_map/ppermute | solution.py:233
  8.6 16.9 %collective-permute-start = (bf16[3,320,128]{2,1,0:T(8,128)(2,1)}, bf16[3,320,128]{2,1,0:T(8,128)(2,1)S(1)}, u32[]{:S(2)}, u32[]{:S(2)}) collective-permute-start(bf16[3,320,128]{2,1,0:T(8,128)(2,1)} %get-tuple-element.48), channel_id=1, source_target_pairs={{0,2},{1,3},{2,4},{3,5},{4,6},{5,7},{6,0},{7,1},{8,10},{9,11},{10,... | collective-permute-start | bytes 737288 | tf_op jit(solution)/shard_map/ppermute | solution.py:226
  12.0 20.6 %collective-permute-start.2 = (bf16[3,320,128]{2,1,0:T(8,128)(2,1)}, bf16[3,320,128]{2,1,0:T(8,128)(2,1)S(1)}, u32[]{:S(2)}, u32[]{:S(2)}) collective-permute-start(bf16[3,320,128]{2,1,0:T(8,128)(2,1)} %get-tuple-element.54), channel_id=1, source_target_pairs={{0,1},{1,2},{2,3},{3,4},{4,5},{5,6},{6,7},{7,0},{8,9},{9,10},{10,1... | collective-permute-start | bytes 737288 | tf_op jit(solution)/shard_map/ppermute | solution.py:226
  15.1 21.5 %collective-permute-start.5 = (bf16[3,320,128]{2,1,0:T(8,128)(2,1)}, bf16[3,320,128]{2,1,0:T(8,128)(2,1)S(1)}, u32[]{:S(2)}, u32[]{:S(2)}) collective-permute-start(bf16[3,320,128]{2,1,0:T(8,128)(2,1)} %get-tuple-element.61), channel_id=1, source_target_pairs={{0,7},{1,0},{2,1},{3,2},{4,3},{5,4},{6,5},{7,6},{8,15},{9,8},{10,9... | collective-permute-start | bytes 737288 | tf_op jit(solution)/shard_map/ppermute | solution.py:226
  15.1 40.2 %collective-permute-start.7 = (bf16[3,320,128]{2,1,0:T(8,128)(2,1)}, bf16[3,320,128]{2,1,0:T(8,128)(2,1)S(1)}, u32[]{:S(2)}, u32[]{:S(2)}) collective-permute-start(bf16[3,320,128]{2,1,0:T(8,128)(2,1)} %get-tuple-element.65), channel_id=1, source_target_pairs={{0,6},{1,7},{2,0},{3,1},{4,2},{5,3},{6,4},{7,5},{8,14},{9,15},{10,... | collective-permute-start | bytes 737288 | tf_op jit(solution)/shard_map/ppermute | solution.py:226
  27.2 34.0 %collective-permute-start.4 = (bf16[3,320,128]{2,1,0:T(8,128)(2,1)}, bf16[3,320,128]{2,1,0:T(8,128)(2,1)S(1)}, u32[]{:S(2)}, u32[]{:S(2)}) collective-permute-start(bf16[3,320,128]{2,1,0:T(8,128)(2,1)} %pack_first.6), channel_id=1, source_target_pairs={{0,4},{1,5},{2,6},{3,7},{4,0},{5,1},{6,2},{7,3},{8,12},{9,13},{10,... | collective-permute-start | bytes 737288 | tf_op jit(solution)/shard_map/ppermute | solution.py:226
  34.2 31.5 %collective-permute-start.3 = (bf16[3,320,128]{2,1,0:T(8,128)(2,1)}, bf16[3,320,128]{2,1,0:T(8,128)(2,1)S(1)}, u32[]{:S(2)}, u32[]{:S(2)}) collective-permute-start(bf16[3,320,128]{2,1,0:T(8,128)(2,1)} %pack_first.5), channel_id=1, source_target_pairs={{0,3},{1,4},{2,5},{3,6},{4,7},{5,0},{6,1},{7,2},{8,11},{9,12},{10,... | collective-permute-start | bytes 737288 | tf_op jit(solution)/shard_map/ppermute | solution.py:226
  38.3 29.3 %collective-permute-start.6 = (bf16[3,320,128]{2,1,0:T(8,128)(2,1)}, bf16[3,320,128]{2,1,0:T(8,128)(2,1)S(1)}, u32[]{:S(2)}, u32[]{:S(2)}) collective-permute-start(bf16[3,320,128]{2,1,0:T(8,128)(2,1)} %pack_first.7), channel_id=1, source_target_pairs={{0,5},{1,6},{2,7},{3,0},{4,1},{5,2},{6,3},{7,4},{8,13},{9,14},{10,... | collective-permute-start | bytes 737288 | tf_op jit(solution)/shard_map/ppermute | solution.py:226
  51.9 15.7 %copy-start.3 = (bf16[3,320,128]{2,1,0:T(8,128)(2,1)S(1)}, bf16[3,320,128]{2,1,0:T(8,128)(2,1)}, u32[]{:S(2)}) copy-start(bf16[3,320,128]{2,1,0:T(8,128)(2,1)} %get-tuple-element.78) | copy-start | bytes 737284
  51.9 21.9 %copy-start.2 = (bf16[3,320,128]{2,1,0:T(8,128)(2,1)S(1)}, bf16[3,320,128]{2,1,0:T(8,128)(2,1)}, u32[]{:S(2)}) copy-start(bf16[3,320,128]{2,1,0:T(8,128)(2,1)} %get-tuple-element.67.refs_0_) | copy-start | bytes 737284
  51.9 15.7 %collective-permute-start.8 = (bf16[3,320,128]{2,1,0:T(8,128)(2,1)}, bf16[3,320,128]{2,1,0:T(8,128)(2,1)S(1)}, u32[]{:S(2)}, u32[]{:S(2)}) collective-permute-start(bf16[3,320,128]{2,1,0:T(8,128)(2,1)} %get-tuple-element.66), channel_id=1, source_target_pairs={{0,7},{1,0},{2,1},{3,2},{4,3},{5,4},{6,5},{7,6},{8,15},{9,8},{10,9... | collective-permute-start | bytes 737288 | tf_op jit(solution)/shard_map/ppermute | solution.py:226
  55.3 31.5 %collective-permute-start.11 = (bf16[3,320,128]{2,1,0:T(8,128)(2,1)}, bf16[3,320,128]{2,1,0:T(8,128)(2,1)S(1)}, u32[]{:S(2)}, u32[]{:S(2)}) collective-permute-start(bf16[3,320,128]{2,1,0:T(8,128)(2,1)} %get-tuple-element.79), channel_id=1, source_target_pairs={{0,3},{1,4},{2,5},{3,6},{4,7},{5,0},{6,1},{7,2},{8,11},{9,12},{10,... | collective-permute-start | bytes 737288 | tf_op jit(solution)/shard_map/ppermute | solution.py:226
  61.2 25.7 %collective-permute-start.12 = (bf16[3,320,128]{2,1,0:T(8,128)(2,1)}, bf16[3,320,128]{2,1,0:T(8,128)(2,1)S(1)}, u32[]{:S(2)}, u32[]{:S(2)}) collective-permute-start(bf16[3,320,128]{2,1,0:T(8,128)(2,1)} %get-tuple-element.80), channel_id=1, source_target_pairs={{0,4},{1,5},{2,6},{3,7},{4,0},{5,1},{6,2},{7,3},{8,12},{9,13},{10,... | collective-permute-start | bytes 737288 | tf_op jit(solution)/shard_map/ppermute | solution.py:226
  65.7 30.2 %collective-permute-start.13 = (bf16[3,320,128]{2,1,0:T(8,128)(2,1)}, bf16[3,320,128]{2,1,0:T(8,128)(2,1)S(1)}, u32[]{:S(2)}, u32[]{:S(2)}) collective-permute-start(bf16[3,320,128]{2,1,0:T(8,128)(2,1)} %get-tuple-element.81), channel_id=1, source_target_pairs={{0,5},{1,6},{2,7},{3,0},{4,1},{5,2},{6,3},{7,4},{8,13},{9,14},{10,... | collective-permute-start | bytes 737288 | tf_op jit(solution)/shard_map/ppermute | solution.py:226
  67.6 29.9 %collective-permute-start.14 = (bf16[3,320,128]{2,1,0:T(8,128)(2,1)}, bf16[3,320,128]{2,1,0:T(8,128)(2,1)S(1)}, u32[]{:S(2)}, u32[]{:S(2)}) collective-permute-start(bf16[3,320,128]{2,1,0:T(8,128)(2,1)} %get-tuple-element.82), channel_id=1, source_target_pairs={{0,6},{1,7},{2,0},{3,1},{4,2},{5,3},{6,4},{7,5},{8,14},{9,15},{10,... | collective-permute-start | bytes 737288 | tf_op jit(solution)/shard_map/ppermute | solution.py:226
  67.6 31.2 %collective-permute-start.10 = (bf16[3,320,128]{2,1,0:T(8,128)(2,1)S(1)}, bf16[3,320,128]{2,1,0:T(8,128)(2,1)S(1)}, u32[]{:S(2)}, u32[]{:S(2)}) collective-permute-start(bf16[3,320,128]{2,1,0:T(8,128)(2,1)S(1)} %copy-done.3), channel_id=1, source_target_pairs={{0,2},{1,3},{2,4},{3,5},{4,6},{5,7},{6,0},{7,1},{8,10},{9,11},{10,... | collective-permute-start | bytes 737288 | tf_op jit(solution)/shard_map/ppermute | solution.py:226
  84.4 18.7 %copy-start.1 = (bf16[3,320,128]{2,1,0:T(8,128)(2,1)S(1)}, bf16[3,320,128]{2,1,0:T(8,128)(2,1)}, u32[]{:S(2)}) copy-start(bf16[3,320,128]{2,1,0:T(8,128)(2,1)} %get-tuple-element.52.refs_0_) | copy-start | bytes 737284
  86.8 16.3 %collective-permute-start.9 = (bf16[3,320,128]{2,1,0:T(8,128)(2,1)}, bf16[3,320,128]{2,1,0:T(8,128)(2,1)S(1)}, u32[]{:S(2)}, u32[]{:S(2)}) collective-permute-start(bf16[3,320,128]{2,1,0:T(8,128)(2,1)} %pack_second.5), channel_id=1, source_target_pairs={{0,1},{1,2},{2,3},{3,4},{4,5},{5,6},{6,7},{7,0},{8,9},{9,10},{10,1... | collective-permute-start | bytes 737288 | tf_op jit(solution)/shard_map/ppermute | solution.py:226
  105.9 21.2 %collective-permute-start.17 = (bf16[2,320,128]{2,1,0:T(8,128)(2,1)S(1)}, bf16[2,320,128]{2,1,0:T(8,128)(2,1)S(1)}, u32[]{:S(2)}, u32[]{:S(2)}) collective-permute-start(bf16[2,320,128]{2,1,0:T(8,128)(2,1)S(1)} %get-tuple-element.86), channel_id=1, source_target_pairs={{0,5},{1,6},{2,7},{3,0},{4,1},{5,2},{6,3},{7,4},{8,13},{9,14},{10,... | collective-permute-start | bytes 491528 | tf_op jit(solution)/shard_map/ppermute | solution.py:226
  110.0 20.9 %collective-permute-start.18 = (bf16[2,320,128]{2,1,0:T(8,128)(2,1)S(1)}, bf16[2,320,128]{2,1,0:T(8,128)(2,1)S(1)}, u32[]{:S(2)}, u32[]{:S(2)}) collective-permute-start(bf16[2,320,128]{2,1,0:T(8,128)(2,1)S(1)} %get-tuple-element.87), channel_id=1, source_target_pairs={{0,4},{1,5},{2,6},{3,7},{4,0},{5,1},{6,2},{7,3},{8,12},{9,13},{10,... | collective-permute-start | bytes 491528 | tf_op jit(solution)/shard_map/ppermute | solution.py:226
  114.7 21.7 %collective-permute-start.16 = (bf16[2,320,128]{2,1,0:T(8,128)(2,1)S(1)}, bf16[2,320,128]{2,1,0:T(8,128)(2,1)S(1)}, u32[]{:S(2)}, u32[]{:S(2)}) collective-permute-start(bf16[2,320,128]{2,1,0:T(8,128)(2,1)S(1)} %get-tuple-element.85), channel_id=1, source_target_pairs={{0,6},{1,7},{2,0},{3,1},{4,2},{5,3},{6,4},{7,5},{8,14},{9,15},{10,... | collective-permute-start | bytes 491528 | tf_op jit(solution)/shard_map/ppermute | solution.py:226
  115.8 20.7 %collective-permute-start.19 = (bf16[2,320,128]{2,1,0:T(8,128)(2,1)S(1)}, bf16[2,320,128]{2,1,0:T(8,128)(2,1)S(1)}, u32[]{:S(2)}, u32[]{:S(2)}) collective-permute-start(bf16[2,320,128]{2,1,0:T(8,128)(2,1)S(1)} %get-tuple-element.88), channel_id=1, source_target_pairs={{0,3},{1,4},{2,5},{3,6},{4,7},{5,0},{6,1},{7,2},{8,11},{9,12},{10,... | collective-permute-start | bytes 491528 | tf_op jit(solution)/shard_map/ppermute | solution.py:226
  122.7 30.5 %copy-start = (bf16[1,320,3072]{2,1,0:T(8,128)(2,1)S(1)}, bf16[1,320,3072]{2,1,0:T(8,128)(2,1)}, u32[]{:S(2)}) copy-start(bf16[1,320,3072]{2,1,0:T(8,128)(2,1)} %refs_0_.13) | copy-start | bytes 5898244
  122.8 16.4 %collective-permute-start.21 = (bf16[2,320,128]{2,1,0:T(8,128)(2,1)S(1)}, bf16[2,320,128]{2,1,0:T(8,128)(2,1)S(1)}, u32[]{:S(2)}, u32[]{:S(2)}) collective-permute-start(bf16[2,320,128]{2,1,0:T(8,128)(2,1)S(1)} %get-tuple-element.90), channel_id=1, source_target_pairs={{0,1},{1,2},{2,3},{3,4},{4,5},{5,6},{6,7},{7,0},{8,9},{9,10},{10,1... | collective-permute-start | bytes 491528 | tf_op jit(solution)/shard_map/ppermute | solution.py:226
  127.1 13.1 %collective-permute-start.15 = (bf16[2,320,128]{2,1,0:T(8,128)(2,1)S(1)}, bf16[2,320,128]{2,1,0:T(8,128)(2,1)S(1)}, u32[]{:S(2)}, u32[]{:S(2)}) collective-permute-start(bf16[2,320,128]{2,1,0:T(8,128)(2,1)S(1)} %get-tuple-element.84), channel_id=1, source_target_pairs={{0,7},{1,0},{2,1},{3,2},{4,3},{5,4},{6,5},{7,6},{8,15},{9,8},{10,9... | collective-permute-start | bytes 491528 | tf_op jit(solution)/shard_map/ppermute | solution.py:226
  130.9 10.9 %collective-permute-start.20 = (bf16[2,320,128]{2,1,0:T(8,128)(2,1)S(1)}, bf16[2,320,128]{2,1,0:T(8,128)(2,1)S(1)}, u32[]{:S(2)}, u32[]{:S(2)}) collective-permute-start(bf16[2,320,128]{2,1,0:T(8,128)(2,1)S(1)} %get-tuple-element.89), channel_id=1, source_target_pairs={{0,2},{1,3},{2,4},{3,5},{4,6},{5,7},{6,0},{7,1},{8,10},{9,11},{10,... | collective-permute-start | bytes 491528 | tf_op jit(solution)/shard_map/ppermute | solution.py:226
  136.5 16.8 %collective-permute-start.22 = (bf16[4,320,128]{2,1,0:T(8,128)(2,1)S(1)}, bf16[4,320,128]{2,1,0:T(8,128)(2,1)S(1)}, u32[]{:S(2)}, u32[]{:S(2)}) collective-permute-start(bf16[4,320,128]{2,1,0:T(8,128)(2,1)S(1)} %join.3), channel_id=1, source_target_pairs={{0,128},{8,136},{16,144},{24,152},{32,160},{40,168},{48,176},{56,1... | collective-permute-start | bytes 983048 | tf_op jit(solution)/shard_map/ppermute | solution.py:233
  139.1 12.3 %collective-permute-start.24 = (bf16[2,320,128]{2,1,0:T(8,128)(2,1)S(1)}, bf16[2,320,128]{2,1,0:T(8,128)(2,1)S(1)}, u32[]{:S(2)}, u32[]{:S(2)}) collective-permute-start(bf16[2,320,128]{2,1,0:T(8,128)(2,1)S(1)} %join.5), channel_id=1, source_target_pairs={{0,128},{8,136},{16,144},{24,152},{32,160},{40,168},{48,176},{56,1... | collective-permute-start | bytes 491528 | tf_op jit(solution)/shard_map/ppermute | solution.py:233
  141.8 11.4 %collective-permute-start.23 = (bf16[2,320,128]{2,1,0:T(8,128)(2,1)S(1)}, bf16[2,320,128]{2,1,0:T(8,128)(2,1)S(1)}, u32[]{:S(2)}, u32[]{:S(2)}) collective-permute-start(bf16[2,320,128]{2,1,0:T(8,128)(2,1)S(1)} %join.4), channel_id=1, source_target_pairs={{0,128},{8,136},{16,144},{24,152},{32,160},{40,168},{48,176},{56,1... | collective-permute-start | bytes 491528 | tf_op jit(solution)/shard_map/ppermute | solution.py:233
